TPU v7x, 256 devices: a whole 4x4x8 slice. The times are simulated.
256 devices in a mesh: gx: 8 (over z), gy: 32 (over x, y, core).
Axes of the slice: x: 4, y: 4, z: 8, core: 2. Of those that a mesh axis runs over, the one named last changes fastest.
Arguments:
- right_side: float32 [256, 1024, 128], P('gx', 'gy'), may hold values from -6 to 6
- permittivity: float32 [256, 1024, 128], P('gx', 'gy'), may hold values from 0.175 to 5.6
Outputs:
- potential: float32 [256, 1024, 128], P('gx', 'gy')
All inputs are finite; a program needn't handle non-finite values.
Results may differ from a plain program's by a relative error of at most 0.00002.
Values sent between devices are 32-bit elements; how exact they have to be, the bound alone decides.
No kernel may reach another device: no remote copies, remote signals or barrier semaphores. Data moves between devices by JAX's collectives and lax.ppermute only.
A program may use at most 192 MiB of HBM per device.

v0:
```python
import jax
import jax.numpy as jnp
from jax import lax
from jax.sharding import PartitionSpec as P

LEVELS = 5
SMOOTH = 2
COARSE_SWEEPS = 12


def padded(cells, sides, width):
    for axis, dim in sides:
        count = lax.axis_size(axis)
        ends = count - 1
        head = lax.slice_in_dim(cells, 0, width, axis=dim)
        tail = lax.slice_in_dim(cells, cells.shape[dim] - width, cells.shape[dim], axis=dim)
        cells = jnp.concatenate(
            [
                lax.ppermute(tail, axis, [(i, (i + 1) % count) for i in range(ends)]),
                cells,
                lax.ppermute(head, axis, [((i + 1) % count, i) for i in range(ends)]),
            ],
            axis=dim,
        )
    return cells


def restrict(values):
    rows_x, rows_y, rows_z = values.shape
    return (
        values.reshape(rows_x // 2, 2, rows_y // 2, 2, rows_z // 2, 2).sum(axis=(1, 3, 5)) * 0.125
    )


def inject(values):
    rows_x, rows_y, rows_z = values.shape
    spread_out = jnp.broadcast_to(
        values[:, None, :, None, :, None], (rows_x, 2, rows_y, 2, rows_z, 2)
    )
    return spread_out.reshape(2 * rows_x, 2 * rows_y, 2 * rows_z)


def side_values(extended):
    return (
        extended[2:, 1:-1, 1:-1],
        extended[:-2, 1:-1, 1:-1],
        extended[1:-1, 2:, 1:-1],
        extended[1:-1, :-2, 1:-1],
        extended[1:-1, 1:-1, 2:],
        extended[1:-1, 1:-1, :-2],
    )


def face_weights(permit, extended, level_scale):
    return tuple(
        (
            level_scale * 2.0 * permit * neighbour / (permit + neighbour)
            for neighbour in side_values(extended)
        )
    )


def beside_sum(weights, extended):
    values = side_values(extended)
    running = weights[0] * values[0]
    for k in range(1, 6):
        running = running + weights[k] * values[k]
    return running


def weight_total(weights):
    running = weights[0]
    for k in range(1, 6):
        running = running + weights[k]
    return running


def colours(rows_x, rows_y, rows_z, offset_x, offset_y):
    index_x = offset_x + jnp.arange(rows_x, dtype=jnp.int32)
    index_y = offset_y + jnp.arange(rows_y, dtype=jnp.int32)
    index_z = jnp.arange(rows_z, dtype=jnp.int32)
    return (index_x[:, None, None] + index_y[None, :, None] + index_z[None, None, :]) % 2


def extend(values):
    return padded(values, (("gx", 0), ("gy", 1)), 1)


def pad_potential(values):
    return jnp.pad(extend(values), ((0, 0), (0, 0), (1, 1)))


def smooth(potential, source, weights, weight_sum, parity, sweeps, from_zero):

    def half_sweep(values, colour, extended):
        updated = (source + beside_sum(weights, extended)) / weight_sum
        return jnp.where(parity == colour, updated, values)

    def full_sweep(step_index, values):
        values = half_sweep(values, 0, pad_potential(values))
        return half_sweep(values, 1, pad_potential(values))

    remaining = sweeps
    if from_zero:
        rows_x, rows_y, rows_z = source.shape
        empty_rim = jnp.zeros((rows_x + 2, rows_y + 2, rows_z + 2), jnp.float32)
        potential = half_sweep(potential, 0, empty_rim)
        potential = half_sweep(potential, 1, pad_potential(potential))
        remaining = sweeps - 1
    return lax.fori_loop(0, remaining, full_sweep, potential)


def cycle(level_index, source, permit, spread, gather_level):
    rows_x, rows_y, rows_z = source.shape
    index_x = lax.axis_index("gx")
    index_y = lax.axis_index("gy")
    total_x = lax.axis_size("gx") * rows_x
    total_y = lax.axis_size("gy") * rows_y
    offset_x = index_x * rows_x
    offset_y = index_y * rows_y
    parity = colours(rows_x, rows_y, rows_z, offset_x, offset_y)
    edge_flags = (
        offset_x == 0,
        offset_x + rows_x == total_x,
        offset_y == 0,
        offset_y + rows_y == total_y,
    )
    extended = extend(permit)
    extended = extended.at[0, 1:-1].set(jnp.where(edge_flags[0], permit[0], extended[0, 1:-1]))
    extended = extended.at[-1, 1:-1].set(jnp.where(edge_flags[1], permit[-1], extended[-1, 1:-1]))
    extended = extended.at[1:-1, 0].set(jnp.where(edge_flags[2], permit[:, 0], extended[1:-1, 0]))
    extended = extended.at[1:-1, -1].set(
        jnp.where(edge_flags[3], permit[:, -1], extended[1:-1, -1])
    )
    extended = jnp.pad(extended, ((0, 0), (0, 0), (1, 1)))
    level_scale = 0.25**level_index
    weights = face_weights(permit, extended, level_scale)
    weight_sum = weight_total(weights)
    zeros_start = jnp.zeros(source.shape, jnp.float32)
    if level_index == LEVELS - 1:
        return smooth(zeros_start, source, weights, weight_sum, parity, COARSE_SWEEPS, True)
    potential = smooth(zeros_start, source, weights, weight_sum, parity, SMOOTH, True)
    residual_field = source - (
        weight_sum * potential - beside_sum(weights, pad_potential(potential))
    )
    correction = cycle(
        level_index + 1, restrict(residual_field), restrict(permit), spread, gather_level
    )
    potential = potential + inject(correction)
    return smooth(potential, source, weights, weight_sum, parity, SMOOTH, False)


def per_device(right_side, permittivity):
    gather_level = LEVELS
    return cycle(0, right_side, permittivity, True, gather_level)


def solution(mesh):
    placed = (P("gx", "gy", None), P("gx", "gy", None))
    return jax.shard_map(
        per_device, mesh=mesh, in_specs=placed, out_specs=P("gx", "gy", None), check_vma=False
    )
```

profile of v0, /device:TPU:134, one launch (start us, length us, event | category | flops | bytes accessed | tf_op | source)
XLA Modules:
  0.0 1461.0 jit_solution(13883266161227190000)
XLA Ops:
  3.6 35.6 %reshape.897 = f32[16,2,16,2,64,2]{5,4,3,2,1,0:T(8,128)} reshape(f32[32,32,128]{2,1,0:T(8,128)} %param.53) | data formatting | bytes 1048576 | tf_op jit(solution)/shard_map/reshape | solution.py:31
  39.2 12.2 reduce_sum.73
  54.4 5.7 mul.1106
  78.7 5.2 collective-permute-done.42
  140.1 5.8 collective-permute-start.63
  168.1 5.4 collective-permute-done.55
  203.6 35.6 %reshape.896 = f32[16,2,16,2,64,2]{5,4,3,2,1,0:T(8,128)} reshape(f32[32,32,128]{2,1,0:T(8,128)} %fusion.149) | data formatting | bytes 1048576 | tf_op jit(solution)/shard_map/reshape | solution.py:31
  239.2 12.2 reduce_sum.72
  294.5 5.8 collective-permute-start.83
  316.1 5.2 collective-permute-start.74
  357.1 6.5 reshape.898
  405.4 5.3 collective-permute-start.103
  426.0 5.2 collective-permute-start.94
  505.6 5.8 collective-permute-start.123
  525.9 5.2 collective-permute-start.114
  589.1 459.1 %while.101 = (s32[]{:T(128)}, f32[2,2,8]{2,1,0:T(2,128)S(1)}, f32[2,2,8]{2,1,0:T(2,128)}, f32[2,2,8]{2,1,0:T(2,128)}, f32[2,2,8]{2,1,0:T(2,128)}, /*index=5*/f32...) while((s32[]{:T(128)}, f32[2,2,8]{2,1,0:T(2,128)S(1)}, ...), condition=%wide.region_9.10_spmd.clone, body=%wide.region_8.9_spmd.clone.sunk | while | flops 5442 | bytes 20329 | solution.py:110
  608.9 5.4 collective-permute-start.4
  632.8 5.1 collective-permute-start.1
  650.7 5.4 collective-permute-start.4
  692.4 5.4 collective-permute-start.4
  716.3 5.1 collective-permute-start.1
  734.1 5.4 collective-permute-start.4
  758.0 5.1 collective-permute-start.1
  775.9 5.4 collective-permute-start.4
  799.7 5.1 collective-permute-start.1
  817.6 5.4 collective-permute-start.4
  841.5 5.1 collective-permute-start.1
  859.3 5.4 collective-permute-start.4
  901.1 5.4 collective-permute-start.4
  924.9 5.1 collective-permute-start.1
  942.8 5.4 collective-permute-start.4
  984.5 5.4 collective-permute-start.4
  1026.3 5.4 collective-permute-start.4
  1051.1 84.9 %while.102 = (s32[]{:T(128)}, f32[4,4,16]{2,1,0:T(4,128)}, f32[4,4,16]{2,1,0:T(4,128)}, f32[4,4,16]{2,1,0:T(4,128)}, f32[4,4,16]{2,1,0:T(4,128)}, /*index=5*/f32...) while((s32[]{:T(128)}, f32[4,4,16]{2,1,0:T(4,128)}, ...), condition=%wide.region_11.12_spmd.clone, body=%wide.region_10.11_spmd.clone.sunk | while | flops 30242 | bytes 70773 | solution.py:110
  1070.2 5.4 collective-permute-start.12
  1112.6 5.4 collective-permute-start.12
  1140.3 87.2 %while.103 = (s32[]{:T(128)}, f32[8,8,32]{2,1,0:T(8,128)}, f32[8,8,32]{2,1,0:T(8,128)S(1)}, f32[8,8,32]{2,1,0:T(8,128)S(1)}, f32[8,8,32]{2,1,0:T(8,128)}, /*inde...) while((s32[]{:T(128)}, f32[8,8,32]{2,1,0:T(8,128)}, ...), condition=%wide.region_13.14_spmd.clone, body=%wide.region_12.13_spmd.clone.sunk | while | flops 204450 | bytes 395309 | solution.py:110
  1159.5 5.4 collective-permute-start.20
  1203.1 5.4 collective-permute-start.20
  1230.8 5.5 reshape.903
  1237.9 89.2 %while.104 = (s32[]{:T(128)}, f32[16,16,64]{2,1,0:T(8,128)}, f32[16,16,64]{2,1,0:T(8,128)S(1)}, f32[16,16,64]{2,1,0:T(8,128)S(1)}, f32[16,16,64]{2,1,0:T(8,128)S...) while((s32[]{:T(128)}, f32[16,16,64]{2,1,0:T(8,128)}, ...), condition=%wide.region_15.16_spmd.clone, body=%wide.region_14.15_spmd.clone.sunk | while | flops 1513634 | bytes 2552365 | solution.py:110
  1257.6 5.4 collective-permute-start.28
  1302.2 5.4 collective-permute-start.28
  1327.1 12.1 broadcast_in_dim.11
  1339.2 24.5 %reshape.904 = f32[32,32,128]{2,1,0:T(8,128)} reshape(f32[16,2,16,2,64,2]{5,4,3,2,1,0:T(8,128)} %broadcast_in_dim.11) | data formatting | bytes 1048576 | tf_op jit(solution)/shard_map/reshape | solution.py:40
  1365.6 94.9 %while.105 = (s32[]{:T(128)}, f32[32,32,128]{2,1,0:T(8,128)}, f32[32,32,128]{2,1,0:T(8,128)S(1)}, f32[32,32,128]{2,1,0:T(8,128)S(1)}, f32[32,32,128]{2,1,0:T(8,1...) while((s32[]{:T(128)}, f32[32,32,128]{2,1,0:T(8,128)}, ...), condition=%wide.region_17.18_spmd.clone, body=%wide.region_16.17_spmd.clone.sunk | while | flops 11673762 | bytes 18117108 | solution.py:110
  1387.9 5.4 collective-permute-start.36
  1435.3 5.4 collective-permute-start.36
  (981 shorter events, 1123.8 us)
Async XLA Ops:
  0.7 67.4 %collective-permute-start.40 = (f32[1,32,128]{2,1,0:T(8,128)S(1)}, f32[1,32,128]{2,1,0:T(8,128)S(1)}, u32[]{:S(2)}, u32[]{:S(2)}) collective-permute-start(f32[1,32,128]{2,1,0:T(8,128)S(1)} %slice.2219), channel_id=1, source_target_pairs={{0,32},{32,64},{64,96},{96,128},{128,160},{160,192},{192,224},{1,3... | collective-permute-start | bytes 49160 | tf_op jit(solution)/shard_map/ppermute | solution.py:19
  51.5 77.8 %collective-permute-start.60 = (f32[1,16,64]{2,1,0:T(8,128)S(1)}, f32[1,16,64]{2,1,0:T(8,128)S(1)}, u32[]{:S(2)}, u32[]{:S(2)}) collective-permute-start(f32[1,16,64]{2,1,0:T(8,128)S(1)} %slice.2633), channel_id=1, source_target_pairs={{0,32},{32,64},{64,96},{96,128},{128,160},{160,192},{192,224},{1,3... | collective-permute-start | bytes 12296 | tf_op jit(solution)/shard_map/ppermute | solution.py:19
  63.3 217.9 %collective-permute-start.80 = (f32[1,8,32]{2,1,0:T(8,128)}, f32[1,8,32]{2,1,0:T(8,128)}, u32[]{:S(2)}, u32[]{:S(2)}) collective-permute-start(f32[1,8,32]{2,1,0:T(8,128)} %slice.2660), channel_id=1, source_target_pairs={{0,32},{32,64},{64,96},{96,128},{128,160},{160,192},{192,224},{1,3... | collective-permute-start | bytes 3080 | tf_op jit(solution)/shard_map/ppermute | solution.py:19
  99.1 7.9 collective-permute-start.44
  116.6 279.2 %collective-permute-start.100 = (f32[1,4,16]{2,1,0:T(4,128)}, f32[1,4,16]{2,1,0:T(4,128)}, u32[]{:S(2)}, u32[]{:S(2)}) collective-permute-start(f32[1,4,16]{2,1,0:T(4,128)} %slice.2687), channel_id=1, source_target_pairs={{0,32},{32,64},{64,96},{96,128},{128,160},{160,192},{192,224},{1,3... | collective-permute-start | bytes 776 | tf_op jit(solution)/shard_map/ppermute | solution.py:19
  123.4 10.6 collective-permute-start.48
  129.3 10.8 collective-permute-start.61
  134.0 11.9 collective-permute-start.50
  138.2 9.7 collective-permute-start.51
  140.1 13.8 collective-permute-start.63
  145.9 11.7 collective-permute-start.62
  151.7 8.0 collective-permute-start.52
  165.9 7.5 collective-permute-start.55
  191.8 7.5 collective-permute-start.59
  263.2 9.1 collective-permute-start.66
  269.4 216.5 %collective-permute-start.120 = (f32[1,2,8]{2,1,0:T(2,128)}, f32[1,2,8]{2,1,0:T(2,128)}, u32[]{:S(2)}, u32[]{:S(2)}) collective-permute-start(f32[1,2,8]{2,1,0:T(2,128)} %slice.2714), channel_id=1, source_target_pairs={{0,32},{32,64},{64,96},{96,128},{128,160},{160,192},{192,224},{1,3... | collective-permute-start | bytes 200 | tf_op jit(solution)/shard_map/ppermute | solution.py:19
  275.2 12.5 collective-permute-start.68
  279.3 8.4 collective-permute-start.69
  282.5 11.3 collective-permute-start.81
  287.7 12.6 collective-permute-start.70
  291.8 10.4 collective-permute-start.71
  294.5 12.5 collective-permute-start.83
  300.3 10.4 collective-permute-start.82
  304.8 9.8 collective-permute-start.72
  307.0 7.5 collective-permute-start.73
  316.1 9.8 collective-permute-start.74
  332.5 8.6 collective-permute-start.76
  389.9 10.3 collective-permute-start.88
  391.9 8.4 collective-permute-start.89
  397.1 7.5 collective-permute-start.101
  400.2 12.4 collective-permute-start.90
  402.2 10.4 collective-permute-start.91
  405.4 15.3 %collective-permute-start.103 = (f32[6,1,16]{2,1,0:T(1,128)S(1)}, f32[6,1,16]{2,1,0:T(1,128)S(1)}, u32[]{:S(2)}, u32[]{:S(2)}) collective-permute-start(f32[6,1,16]{2,1,0:T(1,128)S(1)} %get-tuple-element.1454), channel_id=1, source_target_pairs={{1,0},{2,1},{3,2},{4,3},{5,4},{6,5},{7,6},{8,7},{9,8},{10,9},{11,1... | collective-permute-start | bytes 1160 | tf_op jit(solution)/shard_map/ppermute | solution.py:21
  410.7 10.1 collective-permute-start.102
  414.9 9.7 collective-permute-start.92
  416.8 7.8 collective-permute-start.93
  426.0 9.7 collective-permute-start.94
  441.8 8.5 collective-permute-start.96
  481.6 7.8 collective-permute-start.106
  487.2 10.8 collective-permute-start.121
  500.8 12.6 collective-permute-start.110
  503.7 9.6 collective-permute-start.111
  505.6 15.1 %collective-permute-start.123 = (f32[4,1,8]{2,1,0:T(1,128)S(1)}, f32[4,1,8]{2,1,0:T(1,128)S(1)}, u32[]{:S(2)}, u32[]{:S(2)}) collective-permute-start(f32[4,1,8]{2,1,0:T(1,128)S(1)} %get-tuple-element.1469), channel_id=1, source_target_pairs={{1,0},{2,1},{3,2},{4,3},{5,4},{6,5},{7,6},{8,7},{9,8},{10,9},{11,1... | collective-permute-start | bytes 392 | tf_op jit(solution)/shard_map/ppermute | solution.py:21
  511.4 9.4 collective-permute-start.122
  514.9 9.6 collective-permute-start.112
  516.9 7.6 collective-permute-start.113
  525.9 9.7 collective-permute-start.114
  540.8 8.4 collective-permute-start.116
  (266 other events, 1822.3 us)
where the time goes:
time: 1480 us; the launch traced here: 1460 us
  starting transfers between devices  693 us (47%)
  waiting for transfers between devices  365 us (25%)
  other arithmetic  199 us (13%)
  local copies, waits for them, and re-layouts  198 us (13%)
    ppermute x120, starting transfers between devices, padded(): lax.ppermute(head, axis, [((i + 1) % count, i) for i in range(ends)])  417 us
    ppermute x120, waiting for transfers between devices, padded(): lax.ppermute(tail, axis, [(i, (i + 1) % count) for i in range(ends)])  347 us
    ppermute x120, starting transfers between devices, padded(): lax.ppermute(tail, axis, [(i, (i + 1) % count) for i in range(ends)])  276 us
    reshape x5, local copies, waits for them, and re-layouts, restrict(): values.reshape(rows_x // 2, 2, rows_y // 2, 2, rows_z // 2, 2)  80.9 us
    select_n x56, other arithmetic, half_sweep(): return jnp.where(parity == colour, updated, values)  78.9 us
    concatenate x97, other arithmetic, padded(): jnp.concatenate([lax.ppermute(tail, axis, [(i, (i + 1) % count) for i in...  51 us
    reshape x4, local copies, waits for them, and re-layouts, inject(): return spread_out.reshape(2 * rows_x, 2 * rows_y, 2 * rows_z)  32.2 us
    reduce_sum x8, other arithmetic, restrict(): values.reshape(rows_x // 2, 2, rows_y // 2, 2, rows_z // 2, 2)  31.9 us
  transfers between devices with their start and end apart: 240, of which 102 were waited for; matrix products, arithmetic and copies ran while one was open for 17% of the time, Pallas kernels for 0%

commit v1 on v0

v1 whole, which is shorter than its diff:
```python
import jax
import jax.numpy as jnp
from jax import lax
from jax.experimental import pallas as pl
from jax.experimental.pallas import tpu as pltpu
from jax.sharding import PartitionSpec as P

F32 = jnp.float32
LANES = 128
COARSE_SWEEPS = 12
OWN = (32, 16, 8)
HALO = (8, 16, 12)
EXT = (48, 48, 32)
GX = 8
GY = 32
CHUNK = 8


def iota(shape, dim):
    return lax.broadcasted_iota(jnp.int32, shape, dim)


def lane_roll(v, shift):
    return pltpu.roll(v, shift % LANES, v.ndim - 1)


def flip(v, bit):
    lane = iota(v.shape, v.ndim - 1)
    return jnp.where((lane & bit) == 0, lane_roll(v, -bit), lane_roll(v, bit))


def pair_is_even(level, rows):
    shape = (rows, LANES)
    return ((iota(shape, 0) ^ (iota(shape, 1) >> level)) & 1) == 0


def bounds(level, index, count):
    own, halo, ext = OWN[level], HALO[level], EXT[level]
    low = halo - index * own
    high = halo + (count - index) * own
    return low, high


def clamp_edges(level, e, gx, gy):
    own, halo, ext = OWN[level], HALO[level], EXT[level]
    for back in range(-(-halo // own)):
        low = halo - back * own
        high = halo + own + back * own
        if low >= 1:

            @pl.when(gx == back)
            def _():
                e[low - 1] = e[low]

            @pl.when(gy == back)
            def _():
                e[:, 8 + low - 1 : 8 + low, :] = e[:, 8 + low : 8 + low + 1, :]

        if high < ext:

            @pl.when(gx == GX - 1 - back)
            def _():
                e[high] = e[high - 1]

            @pl.when(gy == GY - 1 - back)
            def _():
                e[:, 8 + high : 8 + high + 1, :] = e[:, 8 + high - 1 : 8 + high, :]


def prepare(level, e, f, state, total, v, gx, gy):
    ext = EXT[level]
    step = 1 << level
    scale = 2.0 * 0.25**level
    rows = 16

    def face(a, b):
        return scale * a * b / (a + b)

    xlow, xhigh = bounds(level, gx, GX)
    ylow, yhigh = bounds(level, gy, GY)
    shape = (rows, LANES)
    lane = iota(shape, 1)
    z_last = (lane >> level) == (LANES >> level) - 1
    even = pair_is_even(level, rows)
    x_odd = jnp.where(even, 0, 1)

    def body(p, carry):
        for c in range(ext // rows):
            r = c * rows
            mid = slice(8 + r, 8 + r + rows)
            up = slice(9 + r, 9 + r + rows)
            down = slice(7 + r, 7 + r + rows)
            e0 = e[2 * p, mid, :]
            e1 = e[2 * p + 1, mid, :]
            before = e[jnp.maximum(2 * p - 1, 0), mid, :]
            after = e[2 * p + 2, mid, :]
            inner = face(e0, e1)
            outer0 = face(e0, before)
            outer1 = face(e1, after)
            yp0 = face(e0, e[2 * p, up, :])
            yp1 = face(e1, e[2 * p + 1, up, :])
            ym0 = face(e0, e[2 * p, down, :])
            ym1 = face(e1, e[2 * p + 1, down, :])
            zp0 = jnp.where(z_last, 0.0, face(e0, lane_roll(e0, -step)))
            zp1 = jnp.where(z_last, 0.0, face(e1, lane_roll(e1, -step)))
            zm0 = lane_roll(zp0, step)
            zm1 = lane_roll(zp1, step)
            f0 = f[2 * p, r : r + rows, :]
            f1 = f[2 * p + 1, r : r + rows, :]
            row = r + iota(shape, 0)
            y_ok = (row >= ylow) & (row < yhigh)
            for k in range(2):
                pick = even if k == 0 else jnp.logical_not(even)
                outer = jnp.where(pick, outer0, outer1)
                yp = jnp.where(pick, yp0, yp1)
                ym = jnp.where(pick, ym0, ym1)
                zp = jnp.where(pick, zp0, zp1)
                zm = jnp.where(pick, zm0, zm1)
                weight_sum = inner + outer + yp + ym + zp + zm
                x_at = 2 * p + (x_odd if k == 0 else 1 - x_odd)
                ok = y_ok & (x_at >= xlow) & (x_at < xhigh)
                inverse = jnp.where(ok, 1.0 / weight_sum, 0.0)
                source = jnp.where(pick, f0, f1) * inverse
                parts = (source, inner * inverse, outer * inverse, yp * inverse, ym * inverse,
                         zp * inverse, zm * inverse)
                for i in range(7):
                    state[k, i, p, r : r + rows, :] = parts[i]
                if k == 0:
                    total[p, r : r + rows, :] = weight_sum
                    v[0, p, mid, :] = source
        return carry

    lax.fori_loop(0, ext // 2, body, 0)


def clear(v, ext):
    def body(p, carry):
        for k in range(2):
            v[k, p] = jnp.zeros((ext + 16, LANES), F32)
        return carry

    lax.fori_loop(0, ext // 2, body, 0)


def updated(level, k, p, v, state):
    ext = EXT[level]
    step = 1 << level
    even = pair_is_even(level, ext)
    mid = slice(8, 8 + ext)
    other = 1 - k
    here = v[other, p, mid, :]
    before = v[other, p - 1, mid, :]
    after = v[other, p + 1, mid, :]
    outer = jnp.where(even, before, after) if k == 0 else jnp.where(even, after, before)
    sides = (here, outer, v[other, p, 9 : 9 + ext, :], v[other, p, 7 : 7 + ext, :],
             lane_roll(here, -step), lane_roll(here, step))
    value = state[k, 0, p]
    for i in range(6):
        value = value + state[k, 1 + i, p] * sides[i]
    return value


def half_sweep(level, k, reach, v, state):
    own, halo, ext = OWN[level], HALO[level], EXT[level]
    first = (halo - reach) // 2
    last = (halo + own + reach + 1) // 2

    def body(p, carry):
        v[k, p, 8 : 8 + ext, :] = updated(level, k, p, v, state)
        return carry

    lax.fori_loop(first, last, body, 0)


def restricted(level, first, row, count, v, state, total, e, tmp, store):
    ext = EXT[level]
    step = 1 << level

    def body(q, carry):
        p = first + q
        mid = slice(8, 8 + ext)
        tmp[0, q, 0:ext, :] = (updated(level, 0, p, v, state) - v[0, p, mid, :]) * total[p]
        tmp[1, q, 0:ext, :] = e[2 * p, mid, :] + e[2 * p + 1, mid, :]
        coarse = []
        for i in range(2):
            a = tmp[i, q, pl.ds(row, count, stride=2), :] + tmp[i, q, pl.ds(row + 1, count, stride=2), :]
            coarse.append((a + flip(a, step)) * 0.125)
        store(q, coarse[0], coarse[1])
        return carry

    return body


def interleave(f, e):
    return jnp.where((iota(f.shape, f.ndim - 1) & 1) == 0, f, e)


def split(both):
    low = (iota(both.shape, both.ndim - 1) & 1) == 0
    return jnp.where(low, both, lane_roll(both, 1)), jnp.where(low, lane_roll(both, -1), both)


def fill_rim(e, ext):
    one = jnp.ones((ext + 16, LANES), F32)
    e[ext] = one
    e[ext + 1] = one

    def body(x, carry):
        e[x, 0:8, :] = one[0:8]
        e[x, 8 + ext :, :] = one[0:8]
        return carry

    lax.fori_loop(0, ext, body, 0)


def down0(f_in, e_in, xl, xr, yl, yr, out, state, v, e, f, total, tmp):
    level = 0
    gx, gy = lax.axis_index("gx"), lax.axis_index("gy")
    fill_rim(e, 48)
    for i, (target, own, off) in enumerate(((f, f_in, 0), (e, e_in, 8))):
        target[0:8, off + 8 : off + 40, :] = xl[i]
        target[8:40, off + 8 : off + 40, :] = own[...]
        target[40:48, off + 8 : off + 40, :] = xr[i]
        target[0:48, off : off + 8, :] = yl[i]
        target[0:48, off + 40 : off + 48, :] = yr[i]
    clamp_edges(level, e, gx, gy)
    clear(v, 48)
    prepare(level, e, f, state, total, v, gx, gy)
    half_sweep(level, 1, 6, v, state)
    half_sweep(level, 0, 5, v, state)
    half_sweep(level, 1, 4, v, state)

    def store(q, fc, ec):
        out[q] = interleave(fc, ec)

    lax.fori_loop(0, 16, restricted(level, 4, 8, 16, v, state, total, e, tmp, store), 0)


def down1(own, xl, xr, yl, yr, out, state, v, e, f, total, tmp):
    level = 1
    gx, gy = lax.axis_index("gx"), lax.axis_index("gy")
    fill_rim(e, 48)

    def put(source, count, x, y):
        def body(i, carry):
            fi, ei = split(source[i])
            f[x + i, y : y + 16, :] = fi
            e[x + i, 8 + y : 8 + y + 16, :] = ei
            return carry

        lax.fori_loop(0, count, body, 0)

    put(xl, 16, 0, 16)
    put(own, 16, 16, 16)
    put(xr, 16, 32, 16)
    put(yl, 48, 0, 0)
    put(yr, 48, 0, 32)
    clamp_edges(level, e, gx, gy)
    clear(v, 48)
    prepare(level, e, f, state, total, v, gx, gy)
    half_sweep(level, 1, 11, v, state)
    half_sweep(level, 0, 10, v, state)
    half_sweep(level, 1, 9, v, state)

    def store(q, fc, ec):
        out[q] = interleave(fc, ec)

    lax.fori_loop(0, 16, restricted(level, 4, 8, 16, v, state, total, e, tmp, store), 0)


def down2(own, xl, xr, yl, yr, out, state, v, e, f, total, tmp, coarse):
    level = 2
    gx, gy = lax.axis_index("gx"), lax.axis_index("gy")
    fill_rim(e, 32)

    def put(source, count, x, y, height):
        def body(i, carry):
            fi, ei = split(source[i])
            f[x + i, y : y + height, :] = fi
            e[x + i, 8 + y : 8 + y + height, :] = ei
            return carry

        lax.fori_loop(0, count, body, 0)

    put(xl, 8, 0, 8, 16)
    put(own, 16, 8, 8, 16)
    put(xr, 8, 24, 8, 16)
    put(yl, 32, 0, 0, 8)
    put(yr, 32, 0, 24, 8)
    clamp_edges(level, e, gx, gy)
    clear(v, 32)
    prepare(level, e, f, state, total, v, gx, gy)
    half_sweep(level, 1, 9, v, state)
    half_sweep(level, 0, 8, v, state)
    half_sweep(level, 1, 7, v, state)

    def store(q, fc, ec):
        coarse[0, q, 0:4, :] = fc
        coarse[1, q, 0:4, :] = ec

    lax.fori_loop(0, 4, restricted(level, 6, 12, 4, v, state, total, e, tmp, store), 0)
    slot = iota((1, LANES), 1) & 7
    for i in range(2):
        for r in range(2):
            row = jnp.zeros((1, LANES), F32)
            for x1 in range(2):
                for y in range(4):
                    row = jnp.where(slot == 4 * x1 + y, coarse[i, 2 * x1 + r, y : y + 1, :], row)
            out[:, 2 * i + r : 2 * i + r + 1, :] = jnp.broadcast_to(row[None], (GX, 1, LANES))


BLOCK = (CHUNK, GX, LANES)


def pair_before(v, fill):
    lane, sub = iota(BLOCK, 2), iota(BLOCK, 1)
    low = (lane & 4) == 0
    moved = jnp.where(low, pltpu.roll(lane_roll(v, -4), 1, 1), lane_roll(v, 4))
    return jnp.where(low & (sub == 0), fill, moved)


def pair_after(v, fill):
    lane, sub = iota(BLOCK, 2), iota(BLOCK, 1)
    high = (lane & 4) != 0
    moved = jnp.where(high, pltpu.roll(lane_roll(v, 4), GX - 1, 1), lane_roll(v, -4))
    return jnp.where(high & (sub == GX - 1), fill, moved)


def y_after(level, v, following):
    lane = iota(BLOCK, 2)
    if level == 3:
        return jnp.where((lane & 3) == 3, lane_roll(following, 3), lane_roll(v, -1))
    return jnp.where((lane & 2) == 2, lane_roll(following, 2), lane_roll(v, -2))


def y_before(level, v, preceding):
    lane = iota(BLOCK, 2)
    if level == 3:
        return jnp.where((lane & 3) == 0, lane_roll(preceding, -3), lane_roll(v, 1))
    return jnp.where((lane & 2) == 0, lane_roll(preceding, -2), lane_roll(v, 2))


def coarse_levels(gathered, e3, s3, w3, v3, e4, f4, s4, v4):
    lane = iota(BLOCK, 2)
    even3 = ((lane ^ (lane >> 3)) & 1) == 0
    even4 = (((lane >> 1) ^ (lane >> 2) ^ (lane >> 4)) & 1) == 0
    z_last3 = (lane >> 3) == 15
    z_last4 = (lane >> 4) == 7
    chunks = range(0, GY, CHUNK)

    def face(scale, a, b):
        return (2.0 * scale) * a * b / (a + b)

    for g in range(GY):
        for r in range(2):
            e3[r, 1 + g] = gathered[g, pl.ds(2 + r, GX, stride=4), :]
    zero = jnp.zeros((GX, LANES), F32)
    for k in range(2):
        e3[k, 0] = lane_roll(e3[k, 1], 3)
        e3[k, 1 + GY] = lane_roll(e3[k, GY], -3)
        v3[k, 0] = zero
        v3[k, 1 + GY] = zero
    v4[0] = zero
    v4[1 + GY] = zero
    scale = 0.25**3
    for g in chunks:
        here = pl.ds(1 + g, CHUNK)
        both = (e3[0, here], e3[1, here])
        inner = face(scale, both[0], both[1])
        outer = (face(scale, both[0], pair_before(both[1], both[0])),
                 face(scale, both[1], pair_after(both[0], both[1])))
        yp, ym, zp, zm, f = [], [], [], [], []
        for r in range(2):
            own = both[r]
            yp.append(face(scale, own, y_after(3, own, e3[r, pl.ds(2 + g, CHUNK)])))
            ym.append(face(scale, own, y_before(3, own, e3[r, pl.ds(g, CHUNK)])))
            z = jnp.where(z_last3, 0.0, face(scale, own, lane_roll(own, -8)))
            zp.append(z)
            zm.append(lane_roll(z, 8))
            f.append(jnp.stack([gathered[g + i, pl.ds(r, GX, stride=4), :] for i in range(CHUNK)]))
        for k in range(2):
            a, b = k, 1 - k
            parts = [jnp.where(even3, t[a], t[b]) for t in (outer, yp, ym, zp, zm)]
            weight_sum = inner
            for t in parts:
                weight_sum = weight_sum + t
            inverse = 1.0 / weight_sum
            source = jnp.where(even3, f[a], f[b]) * inverse
            s3[k, 0, pl.ds(g, CHUNK)] = source
            s3[k, 1, pl.ds(g, CHUNK)] = inner * inverse
            for i in range(5):
                s3[k, 2 + i, pl.ds(g, CHUNK)] = parts[i] * inverse
            if k == 0:
                w3[pl.ds(g, CHUNK)] = weight_sum
                v3[0, here] = source
        t = both[0] + both[1]
        t = t + flip(t, 1)
        e4[here] = (t + flip(t, 8)) * 0.125

    def update3(k, g):
        o = 1 - k
        own = v3[o, pl.ds(1 + g, CHUNK)]
        before, after = pair_before(own, 0.0), pair_after(own, 0.0)
        outer = jnp.where(even3, before, after) if k == 0 else jnp.where(even3, after, before)
        sides = (own, outer, y_after(3, own, v3[o, pl.ds(2 + g, CHUNK)]),
                 y_before(3, own, v3[o, pl.ds(g, CHUNK)]), lane_roll(own, -8), lane_roll(own, 8))
        value = s3[k, 0, pl.ds(g, CHUNK)]
        for i in range(6):
            value = value + s3[k, 1 + i, pl.ds(g, CHUNK)] * sides[i]
        return value

    def sweep3(k):
        for g in chunks:
            v3[k, pl.ds(1 + g, CHUNK)] = update3(k, g)

    sweep3(1)
    sweep3(0)
    sweep3(1)
    for g in chunks:
        t = (update3(0, g) - v3[0, pl.ds(1 + g, CHUNK)]) * w3[pl.ds(g, CHUNK)]
        t = t + flip(t, 1)
        f4[pl.ds(g, CHUNK)] = (t + flip(t, 8)) * 0.125

    e4[0] = lane_roll(e4[1], 2)
    e4[1 + GY] = lane_roll(e4[GY], -2)
    scale = 0.25**4
    for g in chunks:
        own = e4[pl.ds(1 + g, CHUNK)]
        parts = [face(scale, own, pair_before(own, own)), face(scale, own, pair_after(own, own)),
                 face(scale, own, y_after(4, own, e4[pl.ds(2 + g, CHUNK)])),
                 face(scale, own, y_before(4, own, e4[pl.ds(g, CHUNK)]))]
        z = jnp.where(z_last4, 0.0, face(scale, own, lane_roll(own, -16)))
        parts += [z, lane_roll(z, 16)]
        weight_sum = parts[0]
        for t in parts[1:]:
            weight_sum = weight_sum + t
        inverse = 1.0 / weight_sum
        source = f4[pl.ds(g, CHUNK)] * inverse
        s4[0, pl.ds(g, CHUNK)] = source
        for i in range(6):
            s4[1 + i, pl.ds(g, CHUNK)] = parts[i] * inverse
        v4[pl.ds(1 + g, CHUNK)] = jnp.where(even4, source, 0.0)

    def sweep4(k):
        for g in chunks:
            own = v4[pl.ds(1 + g, CHUNK)]
            sides = (pair_before(own, 0.0), pair_after(own, 0.0),
                     y_after(4, own, v4[pl.ds(2 + g, CHUNK)]), y_before(4, own, v4[pl.ds(g, CHUNK)]),
                     lane_roll(own, -16), lane_roll(own, 16))
            value = s4[0, pl.ds(g, CHUNK)]
            for i in range(6):
                value = value + s4[1 + i, pl.ds(g, CHUNK)] * sides[i]
            mine = even4 if k == 0 else jnp.logical_not(even4)
            v4[pl.ds(1 + g, CHUNK)] = jnp.where(mine, value, own)

    sweep4(1)

    def full(i, carry):
        sweep4(0)
        sweep4(1)
        return carry

    lax.fori_loop(0, COARSE_SWEEPS - 1, full, 0)
    for g in chunks:
        here = pl.ds(1 + g, CHUNK)
        u = v4[here]
        v3[0, here] = v3[0, here] + u
        v3[1, here] = v3[1, here] + u
    sweep3(0)
    sweep3(1)
    sweep3(0)
    sweep3(1)


def around_from_level3(v3, up, gx, gy):
    shape = (GX, LANES)
    lane, sub = iota(shape, 1), iota(shape, 0)
    even3 = ((lane ^ (lane >> 3)) & 1) == 0
    head = (lane & 7) == 0
    outside = ((sub == 0) & (gx == 0)) | ((sub == 2) & (gx == GX - 1))
    up[...] = jnp.zeros(up.shape, F32)
    for dy in range(3):
        red = v3[0, gy + dy]
        black = v3[1, gy + dy]
        for r in range(2):
            t = jnp.where(even3, red, black) if r == 0 else jnp.where(even3, black, red)
            t = jnp.where(outside, 0.0, pltpu.roll(t, lax.rem(GX + 1 - gx, GX), 0))
            for s in range(8):
                w = jnp.where(head, lane_roll(t, -s), 0.0)
                w = w + lane_roll(w, 1)
                w = w + lane_roll(w, 2)
                w = w + lane_roll(w, 4)
                for dx in range(3):
                    x = 4 * dx + 2 * (s // 4) + r
                    y = 4 + 2 * (4 * dy + s % 4)
                    up[x, y : y + 2, :] = jnp.broadcast_to(w[dx : dx + 1], (2, LANES))


def spread(level, p, v, up):
    rows = 24
    even = pair_is_even(level, rows)
    start = 8 + (12 if level == 1 else 4)
    red = v[0, p, start : start + rows, :]
    black = v[1, p, start : start + rows, :]
    for s in range(2):
        u = jnp.where(even, red, black) if s == 0 else jnp.where(even, black, red)
        for twice in range(2):
            up[s, pl.ds(twice, rows, stride=2), :] = u


def climb(gathered, s0, in0, s1, in1, s2, in2, out, e3, s3, w3, v3, e4, f4, s4, v4, v2, v1, v0, up3, up):
    gx, gy = lax.axis_index("gx"), lax.axis_index("gy")
    coarse_levels(gathered, e3, s3, w3, v3, e4, f4, s4, v4)
    around_from_level3(v3, up3, gx, gy)

    clear(v2, 32)

    def add2(p, carry):
        for k in range(2):
            v2[k, p, 8:40, :] = in2[k, p, 8:40, :] + up3[p - 2]
        return carry

    lax.fori_loop(2, 14, add2, 0)
    half_sweep(2, 0, 6, v2, s2)
    half_sweep(2, 1, 5, v2, s2)
    half_sweep(2, 0, 4, v2, s2)
    half_sweep(2, 1, 3, v2, s2)

    clear(v1, 48)

    def add1(c, carry):
        slot = up.at[c]
        spread(2, c, v2, slot)
        for s in range(2):
            for k in range(2):
                p = 2 * c - 4 + s
                v1[k, p, 8:56, :] = in1[k, p, 8:56, :] + slot[s]
        return carry

    lax.fori_loop(4, 12, add1, 0)
    half_sweep(1, 0, 5, v1, s1)
    half_sweep(1, 1, 4, v1, s1)
    half_sweep(1, 0, 3, v1, s1)
    half_sweep(1, 1, 2, v1, s1)

    clear(v0, 48)

    def add0(c, carry):
        slot = up.at[c]
        spread(1, c, v1, slot)
        for s in range(2):
            for k in range(2):
                p = 2 * c - 12 + s
                v0[k, p, 8:56, :] = in0[k, p, 8:56, :] + slot[s]
        return carry

    lax.fori_loop(7, 17, add0, 0)
    half_sweep(0, 0, 3, v0, s0)
    half_sweep(0, 1, 2, v0, s0)
    half_sweep(0, 0, 1, v0, s0)
    half_sweep(0, 1, 0, v0, s0)
    even = pair_is_even(0, 32)

    def finish(q, carry):
        red = v0[0, 4 + q, 16:48, :]
        black = v0[1, 4 + q, 16:48, :]
        out[2 * q] = jnp.where(even, red, black)
        out[2 * q + 1] = jnp.where(even, black, red)
        return carry

    lax.fori_loop(0, 16, finish, 0)


def shaped(*dims):
    return jax.ShapeDtypeStruct(dims, F32)


def state_shapes(level):
    ext = EXT[level]
    return shaped(2, 7, ext // 2, ext, LANES), shaped(2, ext // 2, ext + 16, LANES)


def kernel_call(body, out_shape, scratch, *operands):
    return pl.pallas_call(
        body,
        out_shape=out_shape,
        scratch_shapes=[pltpu.VMEM(s, F32) for s in scratch],
        compiler_params=pltpu.CompilerParams(vmem_limit_bytes=58 << 20),
        name=body.__name__,
    )(*operands)


def down_scratch(level):
    ext = EXT[level]
    return [(ext + 2, ext + 16, LANES), (ext, ext, LANES), (ext // 2, ext, LANES), (2, 16, ext, LANES)]


def exchange(axis, to_next, to_previous):
    count = lax.axis_size(axis)
    onward = [(i, (i + 1) % count) for i in range(count)]
    backward = [((i + 1) % count, i) for i in range(count)]
    return lax.ppermute(to_next, axis, onward), lax.ppermute(to_previous, axis, backward)


def per_device(right_side, permittivity):
    both = (right_side, permittivity)
    xl, xr = exchange("gx", jnp.stack([b[24:] for b in both]), jnp.stack([b[:8] for b in both]))

    def y_slab(rows):
        middle = jnp.stack([b[:, rows] for b in both])
        return jnp.concatenate([xl[:, :, rows], middle, xr[:, :, rows]], axis=1)

    yl, yr = exchange("gy", y_slab(slice(24, 32)), y_slab(slice(0, 8)))
    p1, s0, v0 = kernel_call(
        down0, (shaped(16, 16, LANES),) + state_shapes(0), down_scratch(0),
        right_side, permittivity, xl, xr, yl, yr)

    xl, xr = exchange("gx", p1, p1)
    wide = jnp.concatenate([xl, p1, xr], axis=0)
    yl, yr = exchange("gy", wide, wide)
    p2, s1, v1 = kernel_call(
        down1, (shaped(16, 16, LANES),) + state_shapes(1), down_scratch(1), p1, xl, xr, yl, yr)

    xl, xr = exchange("gx", p2[:8], p2[8:])
    wide = jnp.concatenate([xl, p2, xr], axis=0)
    yl, yr = exchange("gy", wide[:, :8], wide[:, 8:])
    p3, s2, v2 = kernel_call(
        down2, (shaped(GX, 4, LANES),) + state_shapes(2), down_scratch(2) + [(2, 4, 8, LANES)],
        p2, xl, xr, yl, yr)

    column = lax.all_to_all(p3, "gx", 0, 0, tiled=True).reshape(4 * GX, LANES)
    gathered = lax.all_to_all(
        jnp.broadcast_to(column[None], (GY, 4 * GX, LANES)), "gy", 0, 0, tiled=True)

    rows = GY + 2
    scratch = [
        (2, rows, GX, LANES), (2, 7, GY, GX, LANES), (GY, GX, LANES), (2, rows, GX, LANES),
        (rows, GX, LANES), (GY, GX, LANES), (7, GY, GX, LANES), (rows, GX, LANES),
        (2, 16, 48, LANES), (2, 24, 64, LANES), (2, 24, 64, LANES), (12, 32, LANES), (17, 2, 48, LANES),
    ]
    return kernel_call(climb, shaped(32, 32, LANES), scratch, gathered, s0, v0, s1, v1, s2, v2)


def solution(mesh):
    placed = (P("gx", "gy", None), P("gx", "gy", None))
    return jax.shard_map(
        per_device, mesh=mesh, in_specs=placed, out_specs=P("gx", "gy", None), check_vma=False
    )
```

time: 1480 us -> 195 us (0.13)
  the two profiles are of different devices: /device:TPU:134 before, /device:TPU:1 now
where the time goes in v1:
time: 195 us
  Pallas kernels  101 us (52%)
  blocking collectives  34.2 us (18%)
  starting transfers between devices  28.2 us (14%)
  waiting for transfers between devices  23.1 us (12%)
  local copies, waits for them, and re-layouts  7.93 us (4%)
    pallas_call x4, Pallas kernels, kernel_call(): pl.pallas_call(body, out_shape=out_shape, scratch_shapes=[pltpu.VMEM(s, F...  101 us
    all_to_all x1, blocking collectives, per_device(): lax.all_to_all(jnp.broadcast_to(column[None], (GY, 4 * GX, LANES)), 'gy',...  22.4 us
    ppermute x6, starting transfers between devices, exchange(): lax.ppermute(to_previous, axis, backward)  21.7 us
    ppermute x6, waiting for transfers between devices, exchange(): lax.ppermute(to_next, axis, onward)  14.7 us
    all_to_all x1, blocking collectives, per_device(): column = lax.all_to_all(p3, 'gx', 0, 0, tiled=True).reshape(4 * GX, LANES)  11.9 us
    ppermute x6, waiting for transfers between devices, exchange(): lax.ppermute(to_previous, axis, backward)  8.4 us
    ppermute x6, starting transfers between devices, exchange(): lax.ppermute(to_next, axis, onward)  6.45 us
    unnamed x28, local copies, waits for them, and re-layouts  4.68 us
  transfers between devices with their start and end apart: 12, of which 9 were waited for; matrix products, arithmetic and copies ran while one was open for 2% of the time, Pallas kernels for 0%

profile of v1, /device:TPU:1, one launch (start us, length us, event | category | flops | bytes accessed | tf_op | source)
XLA Modules:
  0.0 194.9 jit_solution(1380687588508634677)
XLA Ops:
  0.0 1.1 slice_bitcast_fusion.4
  1.2 2.5 %collective-permute-start = (f32[2,8,32,128]{3,2,1,0:T(8,128)S(1)}, f32[2,8,32,128]{3,2,1,0:T(8,128)S(1)}, u32[]{:S(2)}, u32[]{:S(2)}) collective-permute-start(f32[2,8,32,128]{3,2,1,0:T(8,128)S(1)} %pad_maximum_fusion.2), channel_id=1, source_target_pairs={{0,32},{32,64},{64,96},{96,128},{128,160},{160,192},{192,224},{224... | collective-permute-start | bytes 786440 | tf_op jit(solution)/shard_map/ppermute | solution.py:602
  3.7 4.0 %collective-permute-start.1 = (f32[2,8,32,128]{3,2,1,0:T(8,128)S(1)}, f32[2,8,32,128]{3,2,1,0:T(8,128)S(1)}, u32[]{:S(2)}, u32[]{:S(2)}) collective-permute-start(f32[2,8,32,128]{3,2,1,0:T(8,128)S(1)} %pad_maximum_fusion.3), channel_id=1, source_target_pairs={{32,0},{64,32},{96,64},{128,96},{160,128},{192,160},{224,192},{0,2... | collective-permute-start | bytes 786440 | tf_op jit(solution)/shard_map/ppermute | solution.py:602
  7.8 1.1 slice_bitcast_fusion
  8.9 4.8 %collective-permute-done.xl = f32[2,8,32,128]{3,2,1,0:T(8,128)S(1)} collective-permute-done((f32[2,8,32,128]{3,2,1,0:T(8,128)S(1)}, f32[2,8,32,128]{3,2,1,0:T(8,128)S(1)}, u32[]{:S(2)}, u32[]{:S(2)}) %collective-permute-start) | collective-permute-done | bytes 262176 | tf_op jit(solution)/shard_map/ppermute | solution.py:602
  13.7 0.0 collective-permute-done.1.xr
  13.7 0.0 copy-start.1
  13.8 2.5 %collective-permute-start.2 = (f32[2,48,8,128]{3,2,1,0:T(8,128)S(1)}, f32[2,48,8,128]{3,2,1,0:T(8,128)S(1)}, u32[]{:S(2)}, u32[]{:S(2)}) collective-permute-start(f32[2,48,8,128]{3,2,1,0:T(8,128)S(1)} %pad_maximum_fusion), channel_id=1, source_target_pairs={{0,1},{1,2},{2,3},{3,4},{4,5},{5,6},{6,7},{7,8},{8,9},{9,10},{10,1... | collective-permute-start | bytes 1179656 | tf_op jit(solution)/shard_map/ppermute | solution.py:602
  16.3 0.1 collective-permute-start.3
  16.4 4.6 %collective-permute-done.2.yl = f32[2,48,8,128]{3,2,1,0:T(8,128)S(1)} collective-permute-done((f32[2,48,8,128]{3,2,1,0:T(8,128)S(1)}, f32[2,48,8,128]{3,2,1,0:T(8,128)S(1)}, u32[]{:S(2)}, u32[]{:S(2)}) %collective-permute-start.2) | collective-permute-done | bytes 393248 | tf_op jit(solution)/shard_map/ppermute | solution.py:602
  21.0 2.9 %collective-permute-done.3.yr = f32[2,48,8,128]{3,2,1,0:T(8,128)S(1)} collective-permute-done((f32[2,48,8,128]{3,2,1,0:T(8,128)S(1)}, f32[2,48,8,128]{3,2,1,0:T(8,128)S(1)}, u32[]{:S(2)}, u32[]{:S(2)}) %collective-permute-start.3) | collective-permute-done | bytes 393248 | tf_op jit(solution)/shard_map/ppermute | solution.py:602
  23.9 0.0 copy-done
  23.9 0.0 copy-done.1
  23.9 0.0 copy-done.4
  23.9 0.0 copy-start.5
  23.9 0.8 copy-done.5
  24.6 18.9 %down0.1 = (f32[16,16,128]{2,1,0:T(8,128)}, f32[2,7,24,48,128]{4,3,2,1,0:T(8,128)}, f32[2,24,64,128]{3,2,1,0:T(8,128)}) custom-call(f32[32,32,128]{2,1,0:T(8,128)} %f_in.1, f32[32,32,128]{2,1,0:T(8,128)} %e_in.1, f32[2,8,32,128]{3,2,1,0:T(8,128)} %copy-done, f32[2,8,32,128]{3,2,1,0:T(8,128)} %copy-done.1, f32[2,48,8,128]{3,2,1,0:T(8,128)} %copy-done.4, ...), custom_call_target="tpu_custom_call" | custom-call | tf_op jit(solution)/shard_map/down0/pallas_call | solution.py:584
  43.5 0.0 collective-permute-start.4
  43.5 2.7 %collective-permute-start.5 = (f32[16,16,128]{2,1,0:T(8,128)}, f32[16,16,128]{2,1,0:T(8,128)S(1)}, u32[]{:S(2)}, u32[]{:S(2)}) collective-permute-start(f32[16,16,128]{2,1,0:T(8,128)} %get-tuple-element.14.own), channel_id=1, source_target_pairs={{32,0},{64,32},{96,64},{128,96},{160,128},{192,160},{224,192},{0,2... | collective-permute-start | bytes 393224 | tf_op jit(solution)/shard_map/ppermute | solution.py:602
  46.3 2.6 %collective-permute-done.4.xl = f32[16,16,128]{2,1,0:T(8,128)S(1)} collective-permute-done((f32[16,16,128]{2,1,0:T(8,128)}, f32[16,16,128]{2,1,0:T(8,128)S(1)}, u32[]{:S(2)}, u32[]{:S(2)}) %collective-permute-start.4) | collective-permute-done | bytes 131104 | tf_op jit(solution)/shard_map/ppermute | solution.py:602
  48.9 1.0 constant_dynamic-update-slice_fusion.1
  49.8 0.0 collective-permute-done.5.xr
  49.8 0.0 copy-start.3
  49.9 3.7 %collective-permute-start.7 = (f32[48,16,128]{2,1,0:T(8,128)S(1)}, f32[48,16,128]{2,1,0:T(8,128)S(1)}, u32[]{:S(2)}, u32[]{:S(2)}) collective-permute-start(f32[48,16,128]{2,1,0:T(8,128)S(1)} %constant_dynamic-update-slice_fusion), channel_id=1, source_target_pairs={{1,0},{2,1},{3,2},{4,3},{5,4},{6,5},{7,6},{8,7},{9,8},{10,9},{11,1... | collective-permute-start | bytes 1179656 | tf_op jit(solution)/shard_map/ppermute | solution.py:602
  53.5 0.0 collective-permute-start.6
  53.5 4.5 %collective-permute-done.7.yr = f32[48,16,128]{2,1,0:T(8,128)S(1)} collective-permute-done((f32[48,16,128]{2,1,0:T(8,128)S(1)}, f32[48,16,128]{2,1,0:T(8,128)S(1)}, u32[]{:S(2)}, u32[]{:S(2)}) %collective-permute-start.7) | collective-permute-done | bytes 393248 | tf_op jit(solution)/shard_map/ppermute | solution.py:602
  58.1 0.2 collective-permute-done.6.yl
  58.2 0.0 copy-done.2
  58.2 0.0 copy-done.3
  58.2 0.6 copy-done.6
  58.8 0.7 copy-done.7
  59.6 27.7 %down1.1 = (f32[16,16,128]{2,1,0:T(8,128)}, f32[2,7,24,48,128]{4,3,2,1,0:T(8,128)}, f32[2,24,64,128]{3,2,1,0:T(8,128)}) custom-call(f32[16,16,128]{2,1,0:T(8,128)} %get-tuple-element.14.own, f32[16,16,128]{2,1,0:T(8,128)} %copy-done.2, f32[16,16,128]{2,1,0:T(8,128)} %copy-done.3, f32[48,16,128]{2,1,0:T(8,128)} %copy-done.7, f32[48,16,128]{2,1,0:T(8,128)} %copy-done.6), custom_call_target="tpu_custom_call" | custom-call | tf_op jit(solution)/shard_map/down1/pallas_call | solution.py:584
  87.3 0.9 fusion.3
  88.2 1.4 collective-permute-start.8
  89.6 1.3 collective-permute-start.9
  90.9 1.6 collective-permute-done.8.xl
  92.6 0.9 constant_dynamic-update-slice_fusion.4
  93.5 0.0 collective-permute-done.9.xr
  93.6 9.9 %collective-permute-start.11 = (f32[32,8,128]{2,1,0:T(8,128)S(1)}, f32[32,8,128]{2,1,0:T(8,128)S(1)}, u32[]{:S(2)}, u32[]{:S(2)}) collective-permute-start(f32[32,8,128]{2,1,0:T(8,128)S(1)} %get-tuple-element.31), channel_id=1, source_target_pairs={{1,0},{2,1},{3,2},{4,3},{5,4},{6,5},{7,6},{8,7},{9,8},{10,9},{11,1... | collective-permute-start | bytes 393224 | tf_op jit(solution)/shard_map/ppermute | solution.py:602
  103.4 0.0 collective-permute-start.10
  103.4 1.0 collective-permute-done.11.yr
  104.4 1.0 collective-permute-done.10.yl
  105.4 0.0 copy-done.8
  105.4 0.6 copy-done.11
  106.1 16.8 %down2.1 = (f32[8,4,128]{2,1,0:T(4,128)}, f32[2,7,16,32,128]{4,3,2,1,0:T(8,128)}, f32[2,16,48,128]{3,2,1,0:T(8,128)}) custom-call(f32[16,16,128]{2,1,0:T(8,128)} %get-tuple-element.15.own, f32[8,16,128]{2,1,0:T(8,128)} %copy-done.8, f32[8,16,128]{2,1,0:T(8,128)} %copy-done.9, f32[32,8,128]{2,1,0:T(8,128)} %copy-done.11, f32[32,8,128]{2,1,0:T(8,128)} %copy-done.10), custom_call_target="tpu_custom_call" | custom-call | tf_op jit(solution)/shard_map/down2/pallas_call | solution.py:584
  122.8 11.9 %all_to_all.10 = f32[8,4,128]{2,1,0:T(4,128)S(1)} all-to-all(f32[8,4,128]{2,1,0:T(4,128)} %get-tuple-element.16), channel_id=1, replica_groups=mesh['gx'=8,'gy'=32] {'gx'}, dimensions={0} | all-to-all | bytes 32768 | tf_op jit(solution)/shard_map/all_to_all | solution.py:631
  134.8 22.4 %all_to_all.11.gathered = f32[32,32,128]{2,1,0:T(8,128)} all-to-all(f32[32,32,128]{2,1,0:T(8,128)S(1)} %broadcast_in_dim.8), channel_id=1, replica_groups=mesh['gx'=8,'gy'=32] {'gy'}, dimensions={0} | all-to-all | bytes 1048576 | tf_op jit(solution)/shard_map/all_to_all | solution.py:632
  157.1 37.8 %climb.1 = f32[32,32,128]{2,1,0:T(8,128)} custom-call(f32[32,32,128]{2,1,0:T(8,128)} %all_to_all.11.gathered, f32[2,7,24,48,128]{4,3,2,1,0:T(8,128)} %get-tuple-element.17.s0, f32[2,24,64,128]{3,2,1,0:T(8,128)} %get-tuple-element.18.in0, f32[2,7,24,48,128]{4,3,2,1,0:T(8,128)} %get-tuple-element.19.s1, f32[2,24,64,128]{3,2,1,0:T(8,128)} %get-tuple-element.20.in1, ...), custom_call_target="tpu_custom_call" | custom-call | tf_op jit(solution)/shard_map/climb/pallas_call | solution.py:584
  (23 shorter events, 0.2 us)
Async XLA Ops:
  1.2 12.5 %collective-permute-start = (f32[2,8,32,128]{3,2,1,0:T(8,128)S(1)}, f32[2,8,32,128]{3,2,1,0:T(8,128)S(1)}, u32[]{:S(2)}, u32[]{:S(2)}) collective-permute-start(f32[2,8,32,128]{3,2,1,0:T(8,128)S(1)} %pad_maximum_fusion.2), channel_id=1, source_target_pairs={{0,32},{32,64},{64,96},{96,128},{128,160},{160,192},{192,224},{224... | collective-permute-start | bytes 786440 | tf_op jit(solution)/shard_map/ppermute | solution.py:602
  3.7 10.0 %collective-permute-start.1 = (f32[2,8,32,128]{3,2,1,0:T(8,128)S(1)}, f32[2,8,32,128]{3,2,1,0:T(8,128)S(1)}, u32[]{:S(2)}, u32[]{:S(2)}) collective-permute-start(f32[2,8,32,128]{3,2,1,0:T(8,128)S(1)} %pad_maximum_fusion.3), channel_id=1, source_target_pairs={{32,0},{64,32},{96,64},{128,96},{160,128},{192,160},{224,192},{0,2... | collective-permute-start | bytes 786440 | tf_op jit(solution)/shard_map/ppermute | solution.py:602
  13.7 10.2 %copy-start = (f32[2,8,32,128]{3,2,1,0:T(8,128)}, f32[2,8,32,128]{3,2,1,0:T(8,128)S(1)}, u32[]{:S(2)}) copy-start(f32[2,8,32,128]{3,2,1,0:T(8,128)S(1)} %collective-permute-done.xl) | copy-start | bytes 786436
  13.7 10.2 %copy-start.1 = (f32[2,8,32,128]{3,2,1,0:T(8,128)}, f32[2,8,32,128]{3,2,1,0:T(8,128)S(1)}, u32[]{:S(2)}) copy-start(f32[2,8,32,128]{3,2,1,0:T(8,128)S(1)} %collective-permute-done.1.xr) | copy-start | bytes 786436
  13.8 7.2 %collective-permute-start.2 = (f32[2,48,8,128]{3,2,1,0:T(8,128)S(1)}, f32[2,48,8,128]{3,2,1,0:T(8,128)S(1)}, u32[]{:S(2)}, u32[]{:S(2)}) collective-permute-start(f32[2,48,8,128]{3,2,1,0:T(8,128)S(1)} %pad_maximum_fusion), channel_id=1, source_target_pairs={{0,1},{1,2},{2,3},{3,4},{4,5},{5,6},{6,7},{7,8},{8,9},{9,10},{10,1... | collective-permute-start | bytes 1179656 | tf_op jit(solution)/shard_map/ppermute | solution.py:602
  16.3 7.6 %collective-permute-start.3 = (f32[2,48,8,128]{3,2,1,0:T(8,128)S(1)}, f32[2,48,8,128]{3,2,1,0:T(8,128)S(1)}, u32[]{:S(2)}, u32[]{:S(2)}) collective-permute-start(f32[2,48,8,128]{3,2,1,0:T(8,128)S(1)} %pad_maximum_fusion.1), channel_id=1, source_target_pairs={{1,0},{2,1},{3,2},{4,3},{5,4},{6,5},{7,6},{8,7},{9,8},{10,9},{11,1... | collective-permute-start | bytes 1179656 | tf_op jit(solution)/shard_map/ppermute | solution.py:602
  21.0 2.9 %copy-start.4 = (f32[2,48,8,128]{3,2,1,0:T(8,128)}, f32[2,48,8,128]{3,2,1,0:T(8,128)S(1)}, u32[]{:S(2)}) copy-start(f32[2,48,8,128]{3,2,1,0:T(8,128)S(1)} %collective-permute-done.2.yl) | copy-start | bytes 1179652
  23.9 0.8 copy-start.5
  43.5 5.3 %collective-permute-start.4 = (f32[16,16,128]{2,1,0:T(8,128)}, f32[16,16,128]{2,1,0:T(8,128)S(1)}, u32[]{:S(2)}, u32[]{:S(2)}) collective-permute-start(f32[16,16,128]{2,1,0:T(8,128)} %get-tuple-element.14.own), channel_id=1, source_target_pairs={{0,32},{32,64},{64,96},{96,128},{128,160},{160,192},{192,224},{224... | collective-permute-start | bytes 393224 | tf_op jit(solution)/shard_map/ppermute | solution.py:602
  43.5 6.3 %collective-permute-start.5 = (f32[16,16,128]{2,1,0:T(8,128)}, f32[16,16,128]{2,1,0:T(8,128)S(1)}, u32[]{:S(2)}, u32[]{:S(2)}) collective-permute-start(f32[16,16,128]{2,1,0:T(8,128)} %get-tuple-element.14.own), channel_id=1, source_target_pairs={{32,0},{64,32},{96,64},{128,96},{160,128},{192,160},{224,192},{0,2... | collective-permute-start | bytes 393224 | tf_op jit(solution)/shard_map/ppermute | solution.py:602
  48.8 9.4 %copy-start.2 = (f32[16,16,128]{2,1,0:T(8,128)}, f32[16,16,128]{2,1,0:T(8,128)S(1)}, u32[]{:S(2)}) copy-start(f32[16,16,128]{2,1,0:T(8,128)S(1)} %collective-permute-done.4.xl) | copy-start | bytes 393220
  49.8 8.4 %copy-start.3 = (f32[16,16,128]{2,1,0:T(8,128)}, f32[16,16,128]{2,1,0:T(8,128)S(1)}, u32[]{:S(2)}) copy-start(f32[16,16,128]{2,1,0:T(8,128)S(1)} %collective-permute-done.5.xr) | copy-start | bytes 393220
  49.9 8.2 %collective-permute-start.7 = (f32[48,16,128]{2,1,0:T(8,128)S(1)}, f32[48,16,128]{2,1,0:T(8,128)S(1)}, u32[]{:S(2)}, u32[]{:S(2)}) collective-permute-start(f32[48,16,128]{2,1,0:T(8,128)S(1)} %constant_dynamic-update-slice_fusion), channel_id=1, source_target_pairs={{1,0},{2,1},{3,2},{4,3},{5,4},{6,5},{7,6},{8,7},{9,8},{10,9},{11,1... | collective-permute-start | bytes 1179656 | tf_op jit(solution)/shard_map/ppermute | solution.py:602
  53.5 4.7 %collective-permute-start.6 = (f32[48,16,128]{2,1,0:T(8,128)S(1)}, f32[48,16,128]{2,1,0:T(8,128)S(1)}, u32[]{:S(2)}, u32[]{:S(2)}) collective-permute-start(f32[48,16,128]{2,1,0:T(8,128)S(1)} %constant_dynamic-update-slice_fusion), channel_id=1, source_target_pairs={{0,1},{1,2},{2,3},{3,4},{4,5},{5,6},{6,7},{7,8},{8,9},{9,10},{10,1... | collective-permute-start | bytes 1179656 | tf_op jit(solution)/shard_map/ppermute | solution.py:602
  58.0 0.8 copy-start.6
  58.8 0.7 copy-start.7
  88.2 4.4 %collective-permute-start.8 = (f32[8,16,128]{2,1,0:T(8,128)S(1)}, f32[8,16,128]{2,1,0:T(8,128)S(1)}, u32[]{:S(2)}, u32[]{:S(2)}) collective-permute-start(f32[8,16,128]{2,1,0:T(8,128)S(1)} %get-tuple-element.38), channel_id=1, source_target_pairs={{0,32},{32,64},{64,96},{96,128},{128,160},{160,192},{192,224},{224... | collective-permute-start | bytes 196616 | tf_op jit(solution)/shard_map/ppermute | solution.py:602
  89.6 4.0 %collective-permute-start.9 = (f32[8,16,128]{2,1,0:T(8,128)S(1)}, f32[8,16,128]{2,1,0:T(8,128)S(1)}, u32[]{:S(2)}, u32[]{:S(2)}) collective-permute-start(f32[8,16,128]{2,1,0:T(8,128)S(1)} %get-tuple-element.37), channel_id=1, source_target_pairs={{32,0},{64,32},{96,64},{128,96},{160,128},{192,160},{224,192},{0,2... | collective-permute-start | bytes 196616 | tf_op jit(solution)/shard_map/ppermute | solution.py:602
  92.6 12.8 %copy-start.8 = (f32[8,16,128]{2,1,0:T(8,128)}, f32[8,16,128]{2,1,0:T(8,128)S(1)}, u32[]{:S(2)}) copy-start(f32[8,16,128]{2,1,0:T(8,128)S(1)} %collective-permute-done.8.xl) | copy-start | bytes 196612
  93.5 11.9 %copy-start.9 = (f32[8,16,128]{2,1,0:T(8,128)}, f32[8,16,128]{2,1,0:T(8,128)S(1)}, u32[]{:S(2)}) copy-start(f32[8,16,128]{2,1,0:T(8,128)S(1)} %collective-permute-done.9.xr) | copy-start | bytes 196612
  93.6 10.8 %collective-permute-start.11 = (f32[32,8,128]{2,1,0:T(8,128)S(1)}, f32[32,8,128]{2,1,0:T(8,128)S(1)}, u32[]{:S(2)}, u32[]{:S(2)}) collective-permute-start(f32[32,8,128]{2,1,0:T(8,128)S(1)} %get-tuple-element.31), channel_id=1, source_target_pairs={{1,0},{2,1},{3,2},{4,3},{5,4},{6,5},{7,6},{8,7},{9,8},{10,9},{11,1... | collective-permute-start | bytes 393224 | tf_op jit(solution)/shard_map/ppermute | solution.py:602
  103.4 2.0 %collective-permute-start.10 = (f32[32,8,128]{2,1,0:T(8,128)S(1)}, f32[32,8,128]{2,1,0:T(8,128)S(1)}, u32[]{:S(2)}, u32[]{:S(2)}) collective-permute-start(f32[32,8,128]{2,1,0:T(8,128)S(1)} %get-tuple-element.32), channel_id=1, source_target_pairs={{0,1},{1,2},{2,3},{3,4},{4,5},{5,6},{6,7},{7,8},{8,9},{9,10},{10,1... | collective-permute-start | bytes 393224 | tf_op jit(solution)/shard_map/ppermute | solution.py:602
  104.4 1.0 copy-start.10
  105.4 0.7 copy-start.11

commit v2 on v1

v2 whole, which is shorter than its diff:
```python
import jax
import jax.numpy as jnp
from jax import lax
from jax.experimental import pallas as pl
from jax.experimental.pallas import tpu as pltpu
from jax.sharding import PartitionSpec as P

F32 = jnp.float32
LANES = 128
COARSE_SWEEPS = 12
OWN = (32, 16, 8)
HALO = (8, 16, 12)
EXT = (48, 48, 32)
GX = 8
GY = 32
CHUNK = 8


UNROLL = {"sweep": 6, "restrict": 4, "put": 16, "add": 4}
STOP = 99


def loop(first, last, body, step):
    def several(base, count):
        for store in [body(base + j) for j in range(count)]:
            store()

    whole = (last - first) // step
    if whole > 1:
        def one(i, carry):
            several(first + i * step, step)
            return carry

        lax.fori_loop(0, whole, one, 0)
    elif whole == 1:
        several(first, step)
    if (last - first) % step:
        several(first + whole * step, (last - first) % step)


def iota(shape, dim):
    return lax.broadcasted_iota(jnp.int32, shape, dim)


def lane_roll(v, shift):
    return pltpu.roll(v, shift % LANES, v.ndim - 1)


def flip(v, bit):
    lane = iota(v.shape, v.ndim - 1)
    return jnp.where((lane & bit) == 0, lane_roll(v, -bit), lane_roll(v, bit))


def pair_is_even(level, rows):
    shape = (rows, LANES)
    return ((iota(shape, 0) ^ (iota(shape, 1) >> level)) & 1) == 0


def bounds(level, index, count):
    own, halo, ext = OWN[level], HALO[level], EXT[level]
    low = halo - index * own
    high = halo + (count - index) * own
    return low, high


def clamp_edges(level, e, gx, gy):
    own, halo, ext = OWN[level], HALO[level], EXT[level]
    for back in range(-(-halo // own)):
        low = halo - back * own
        high = halo + own + back * own
        if low >= 1:

            @pl.when(gx == back)
            def _():
                e[low - 1] = e[low]

            @pl.when(gy == back)
            def _():
                e[:, 8 + low - 1 : 8 + low, :] = e[:, 8 + low : 8 + low + 1, :]

        if high < ext:

            @pl.when(gx == GX - 1 - back)
            def _():
                e[high] = e[high - 1]

            @pl.when(gy == GY - 1 - back)
            def _():
                e[:, 8 + high : 8 + high + 1, :] = e[:, 8 + high - 1 : 8 + high, :]


def prepare(level, first, last, e, f, state, total, v, gx, gy, after_pair=None):
    ext = EXT[level]
    step = 1 << level
    scale = 2.0 * 0.25**level

    def face(a, b):
        return scale * a * b / (a + b)

    xlow, xhigh = bounds(level, gx, GX)
    ylow, yhigh = bounds(level, gy, GY)
    shape = (8, LANES)
    lane = iota(shape, 1)
    z_last = (lane >> level) == (LANES >> level) - 1
    even = pair_is_even(level, 8)
    x_odd = jnp.where(even, 0, 1)

    def tile(p, r, before, below):
        mid = slice(8 + r, 16 + r)
        up = slice(9 + r, 17 + r)
        e0 = e[2 * p, mid, :]
        e1 = e[2 * p + 1, mid, :]
        after = e[2 * p + 2, mid, :]
        inner = face(e0, e1)
        outer0 = before
        outer1 = face(e1, after)
        yp0 = face(e0, e[2 * p, up, :])
        yp1 = face(e1, e[2 * p + 1, up, :])
        turned = pltpu.roll(yp0, 1, 0), pltpu.roll(yp1, 1, 0)
        if below is None:
            below = turned
        ym0, ym1 = (jnp.where(top, below[i], turned[i]) for i in range(2))
        zp0 = jnp.where(z_last, 0.0, face(e0, lane_roll(e0, -step)))
        zp1 = jnp.where(z_last, 0.0, face(e1, lane_roll(e1, -step)))
        zm0 = lane_roll(zp0, step)
        zm1 = lane_roll(zp1, step)
        f0 = f[2 * p, r : r + 8, :]
        f1 = f[2 * p + 1, r : r + 8, :]
        row = r + iota(shape, 0)
        y_ok = (row >= ylow) & (row < yhigh)
        for k in range(2):
            pick = even if k == 0 else jnp.logical_not(even)
            outer = jnp.where(pick, outer0, outer1)
            yp = jnp.where(pick, yp0, yp1)
            ym = jnp.where(pick, ym0, ym1)
            zp = jnp.where(pick, zp0, zp1)
            zm = jnp.where(pick, zm0, zm1)
            weight_sum = (inner + outer) + (yp + ym) + (zp + zm)
            x_at = 2 * p + (x_odd if k == 0 else 1 - x_odd)
            ok = y_ok & (x_at >= xlow) & (x_at < xhigh)
            inverse = jnp.where(ok, 1.0 / weight_sum, 0.0)
            source = jnp.where(pick, f0, f1) * inverse
            parts = (source, inner * inverse, outer * inverse, yp * inverse, ym * inverse,
                     zp * inverse, zm * inverse)
            for i in range(7):
                state[p, k, i, r : r + 8, :] = parts[i]
            if k == 0:
                total[p, r : r + 8, :] = weight_sum
                v[0, p, mid, :] = source
        return outer1, turned

    top = iota(shape, 0) == 0

    def body(p, carry):
        new, turned = [], None
        for c in range(ext // 8):
            outer, turned = tile(p, 8 * c, carry[c], turned)
            new.append(outer)
        if after_pair is not None:
            after_pair(p)
        return tuple(new)

    start = max(2 * first - 1, 0)
    init = tuple(face(e[start, 8 + 8 * c : 16 + 8 * c, :], e[2 * first, 8 + 8 * c : 16 + 8 * c, :])
                 for c in range(ext // 8))
    lax.fori_loop(first, last, body, init)


def clear(v, ext):
    def body(p, carry):
        for j in range(4):
            for k in range(2):
                v[k, 4 * p + j] = jnp.zeros((ext + 16, LANES), F32)
        return carry

    lax.fori_loop(0, ext // 8, body, 0)


def updated(level, k, p, v, state, low, high):
    step = 1 << level
    even = pair_is_even(level, high - low)
    mid = slice(8 + low, 8 + high)
    other = 1 - k
    here = v[other, p, mid, :]
    before = v[other, p - 1, mid, :]
    after = v[other, p + 1, mid, :]
    outer = jnp.where(even, before, after) if k == 0 else jnp.where(even, after, before)
    part = [state[p, k, 1 + i, low:high, :] for i in range(6)]
    x = part[0] * here + part[1] * outer
    y = part[2] * v[other, p, 9 + low : 9 + high, :] + part[3] * v[other, p, 7 + low : 7 + high, :]
    z = part[4] * lane_roll(here, -step) + part[5] * lane_roll(here, step)
    return (state[p, k, 0, low:high, :] + x) + (y + z)


def half_sweep(level, k, reach, v, state):
    own, halo, ext = OWN[level], HALO[level], EXT[level]
    first = (halo - reach) // 2
    last = (halo + own + reach + 1) // 2
    low = (halo - reach) // 8 * 8
    high = -(-(halo + own + reach) // 8) * 8

    def body(p):
        value = updated(level, k, p, v, state, low, high)

        def store():
            v[k, p, 8 + low : 8 + high, :] = value

        return store

    loop(first, last, body, UNROLL["sweep"])


def restrict(level, first, pairs, row, count, v, state, total, e, tmp, put):
    step = 1 << level
    low = row // 8 * 8
    high = -(-(row + 2 * count) // 8) * 8
    mid = slice(8 + low, 8 + high)

    def fine(q):
        p = first + q
        residual = (updated(level, 0, p, v, state, low, high) - v[0, p, mid, :]) * total[p, low:high, :]
        both = e[2 * p, mid, :] + e[2 * p + 1, mid, :]

        def store():
            tmp[0, q, low:high, :] = residual
            tmp[1, q, low:high, :] = both

        return store

    def coarse(q):
        out = []
        for i in range(2):
            a = tmp[i, q, pl.ds(row, count, stride=2), :] + tmp[i, q, pl.ds(row + 1, count, stride=2), :]
            out.append((a + flip(a, step)) * 0.125)
        return lambda: put(q, out[0], out[1])

    loop(0, pairs, fine, UNROLL["restrict"])
    loop(0, pairs, coarse, 2 * UNROLL["restrict"])


def interleave(f, e):
    return jnp.where((iota(f.shape, f.ndim - 1) & 1) == 0, f, e)


def split(both):
    low = (iota(both.shape, both.ndim - 1) & 1) == 0
    return jnp.where(low, both, lane_roll(both, 1)), jnp.where(low, lane_roll(both, -1), both)


def fill_rim(e, ext):
    e[ext : ext + 2] = jnp.ones((2, ext + 16, LANES), F32)
    e[0:ext, 0:8, :] = jnp.ones((ext, 8, LANES), F32)
    e[0:ext, 8 + ext :, :] = jnp.ones((ext, 8, LANES), F32)


def start_all(copies):
    for copy in copies:
        copy.start()


def wait_all(copies):
    for copy in copies:
        copy.wait()


KEPT = ((2, 22, 0, 48), (5, 19, 8, 40), (3, 13, 0, 32))
KEPT_V = ((1, 23), (4, 20), (2, 14))
GROUPS = 4


def state_copies(level, kept, vmem, sems):
    first, last, low, high = KEPT[level]
    copies = []
    for g in range(GROUPS):
        a = first + (last - first) * g // GROUPS
        b = first + (last - first) * (g + 1) // GROUPS
        copies.append((vmem.at[pl.ds(a, b - a), :, :, pl.ds(low, high - low), :],
                       kept.at[pl.ds(a - first, b - a)], sems.at[g], b - 1))
    return copies


def v_copy(level, kept_v, v, sem):
    first, last = KEPT_V[level]
    return v.at[:, pl.ds(first, last - first)], kept_v, sem


def sweep_down(level, pairs, reaches, inner, e, f, kept, kept_v, state, v, total, tmp, sems, gx, gy, put):
    clamp_edges(level, e, gx, gy)
    clear(v, EXT[level])
    outgoing = state_copies(level, kept, state, sems)

    def after_pair(p):
        for source, target, sem, last in outgoing:

            @pl.when(p == last)
            def _():
                pltpu.make_async_copy(source, target, sem).start()

    prepare(level, pairs[0], pairs[1], e, f, state, total, v, gx, gy, after_pair)
    if STOP >= 2:
        half_sweep(level, 1, reaches[0], v, state)
        half_sweep(level, 0, reaches[1], v, state)
        half_sweep(level, 1, reaches[2], v, state)
    source, target, sem = v_copy(level, kept_v, v, sems.at[GROUPS])
    v_out = pltpu.make_async_copy(source, target, sem)
    v_out.start()
    if STOP >= 3:
        restrict(level, *inner, v, state, total, e, tmp, put)
    for source, target, sem, last in outgoing:
        pltpu.make_async_copy(source, target, sem).wait()
    v_out.wait()


def down0(f_in, e_in, xl, xr, yl, yr, out, kept, kept_v, state, v, e, f, total, tmp, sems, in_sems):
    gx, gy = lax.axis_index("gx"), lax.axis_index("gy")
    copies = []
    for i, (target, own, off) in enumerate(((f, f_in, 0), (e, e_in, 8))):
        parts = (
            (xl.at[i], target.at[pl.ds(0, 8), pl.ds(off + 8, 32)]),
            (own, target.at[pl.ds(8, 32), pl.ds(off + 8, 32)]),
            (xr.at[i], target.at[pl.ds(40, 8), pl.ds(off + 8, 32)]),
            (yl.at[i], target.at[pl.ds(0, 48), pl.ds(off, 8)]),
            (yr.at[i], target.at[pl.ds(0, 48), pl.ds(off + 40, 8)]),
        )
        for j, (source, to) in enumerate(parts):
            copies.append(pltpu.make_async_copy(source, to, in_sems.at[5 * i + j]))
    start_all(copies)
    fill_rim(e, 48)
    wait_all(copies)

    def put(q, fc, ec):
        out[q] = interleave(fc, ec)

    if STOP >= 1:
        sweep_down(0, (0, 24), (6, 5, 4), (4, 16, 8, 16), e, f, kept, kept_v, state, v, total, tmp, sems, gx, gy, put)


def put_split(source, count, x, y, e, f):
    height = source.shape[1]

    def body(i):
        fi, ei = split(source[i])

        def store():
            f[x + i, y : y + height, :] = fi
            e[x + i, 8 + y : 8 + y + height, :] = ei

        return store

    loop(0, count, body, UNROLL["put"])


def down1(own, xl, xr, yl, yr, out, kept, kept_v, state, v, e, f, total, tmp, sems):
    gx, gy = lax.axis_index("gx"), lax.axis_index("gy")
    fill_rim(e, 48)
    put_split(xl, 16, 0, 16, e, f)
    put_split(own, 16, 16, 16, e, f)
    put_split(xr, 16, 32, 16, e, f)
    put_split(yl, 48, 0, 0, e, f)
    put_split(yr, 48, 0, 32, e, f)

    def put(q, fc, ec):
        out[q] = interleave(fc, ec)

    if STOP >= 1:
        sweep_down(1, (2, 22), (11, 10, 9), (4, 16, 8, 16), e, f, kept, kept_v, state, v, total, tmp, sems, gx, gy, put)


def down2(own, xl, xr, yl, yr, out, kept, kept_v, state, v, e, f, total, tmp, sems, coarse):
    gx, gy = lax.axis_index("gx"), lax.axis_index("gy")
    fill_rim(e, 32)
    put_split(xl, 8, 0, 8, e, f)
    put_split(own, 16, 8, 8, e, f)
    put_split(xr, 8, 24, 8, e, f)
    put_split(yl, 32, 0, 0, e, f)
    put_split(yr, 32, 0, 24, e, f)

    def put(q, fc, ec):
        coarse[0, q, 0:4, :] = fc
        coarse[1, q, 0:4, :] = ec

    if STOP >= 1:
        sweep_down(2, (1, 15), (9, 8, 7), (6, 4, 12, 4), e, f, kept, kept_v, state, v, total, tmp, sems, gx, gy, put)
    slot = iota((1, LANES), 1) & 7
    for i in range(2):
        for r in range(2):
            row = jnp.zeros((1, LANES), F32)
            for x1 in range(2):
                for y in range(4):
                    row = jnp.where(slot == 4 * x1 + y, coarse[i, 2 * x1 + r, y : y + 1, :], row)
            out[:, 2 * i + r : 2 * i + r + 1, :] = jnp.broadcast_to(row[None], (GX, 1, LANES))


BLOCK = (CHUNK, GX, LANES)


def pair_before(v, fill):
    axis = v.ndim - 2
    low = (iota(v.shape, v.ndim - 1) & 4) == 0
    moved = jnp.where(low, pltpu.roll(lane_roll(v, -4), 1, axis), lane_roll(v, 4))
    return jnp.where(low & (iota(v.shape, axis) == 0), fill, moved)


def pair_after(v, fill):
    axis = v.ndim - 2
    high = (iota(v.shape, v.ndim - 1) & 4) != 0
    moved = jnp.where(high, pltpu.roll(lane_roll(v, 4), GX - 1, axis), lane_roll(v, -4))
    return jnp.where(high & (iota(v.shape, axis) == GX - 1), fill, moved)


def y_after(level, v, following):
    lane = iota(v.shape, v.ndim - 1)
    if level == 3:
        return jnp.where((lane & 3) == 3, lane_roll(following, 3), lane_roll(v, -1))
    return jnp.where((lane & 2) == 2, lane_roll(following, 2), lane_roll(v, -2))


def y_before(level, v, preceding):
    lane = iota(v.shape, v.ndim - 1)
    if level == 3:
        return jnp.where((lane & 3) == 0, lane_roll(preceding, -3), lane_roll(v, 1))
    return jnp.where((lane & 2) == 0, lane_roll(preceding, -2), lane_roll(v, 2))


def slots(shape):
    lane = iota(shape, len(shape) - 1)
    return (lane & 1) | ((lane >> 2) & 2)


def tiles_from_slots(parts):
    slot = slots(parts[0].shape)
    return jnp.where(slot == 0, parts[0], jnp.where(slot == 1, parts[1], jnp.where(slot == 2, parts[2], parts[3])))


def slot_after(v, fill):
    slot = slots(v.shape)
    return jnp.where(slot == 3, fill, jnp.where(slot == 1, lane_roll(v, -7), lane_roll(v, -1)))


def slot_before(v, fill):
    slot = slots(v.shape)
    return jnp.where(slot == 0, fill, jnp.where(slot == 2, lane_roll(v, 7), lane_roll(v, 1)))


def coarse_levels(f3, e3, s3, w3, v3, s4):
    lane = iota(BLOCK, 2)
    even3 = ((lane ^ (lane >> 3)) & 1) == 0
    z_last3 = (lane >> 3) == 15
    chunks = range(0, GY, CHUNK)

    def face(scale, a, b):
        return (2.0 * scale) * a * b / (a + b)

    zero = jnp.zeros((GX, LANES), F32)
    for k in range(2):
        e3[k, 0] = lane_roll(e3[k, 1], 3)
        e3[k, 1 + GY] = lane_roll(e3[k, GY], -3)
        v3[k, 0] = zero
        v3[k, 1 + GY] = zero
    scale = 0.25**3
    e4 = []
    for g in chunks:
        here = pl.ds(1 + g, CHUNK)
        both = (e3[0, here], e3[1, here])
        inner = face(scale, both[0], both[1])
        outer = (face(scale, both[0], pair_before(both[1], both[0])),
                 face(scale, both[1], pair_after(both[0], both[1])))
        yp, ym, zp, zm, f = [], [], [], [], []
        for r in range(2):
            own = both[r]
            yp.append(face(scale, own, y_after(3, own, e3[r, pl.ds(2 + g, CHUNK)])))
            ym.append(face(scale, own, y_before(3, own, e3[r, pl.ds(g, CHUNK)])))
            z = jnp.where(z_last3, 0.0, face(scale, own, lane_roll(own, -8)))
            zp.append(z)
            zm.append(lane_roll(z, 8))
            f.append(f3[r, pl.ds(g, CHUNK)])
        for k in range(2):
            a, b = k, 1 - k
            parts = [jnp.where(even3, t[a], t[b]) for t in (outer, yp, ym, zp, zm)]
            weight_sum = inner
            for t in parts:
                weight_sum = weight_sum + t
            inverse = 1.0 / weight_sum
            source = jnp.where(even3, f[a], f[b]) * inverse
            s3[k, 0, pl.ds(g, CHUNK)] = source
            s3[k, 1, pl.ds(g, CHUNK)] = inner * inverse
            for i in range(5):
                s3[k, 2 + i, pl.ds(g, CHUNK)] = parts[i] * inverse
            if k == 0:
                w3[pl.ds(g, CHUNK)] = weight_sum
                v3[0, here] = source
        t = both[0] + both[1]
        t = t + flip(t, 1)
        e4.append((t + flip(t, 8)) * 0.125)

    def update3(k, g):
        o = 1 - k
        own = v3[o, pl.ds(1 + g, CHUNK)]
        before, after = pair_before(own, 0.0), pair_after(own, 0.0)
        outer = jnp.where(even3, before, after) if k == 0 else jnp.where(even3, after, before)
        sides = (own, outer, y_after(3, own, v3[o, pl.ds(2 + g, CHUNK)]),
                 y_before(3, own, v3[o, pl.ds(g, CHUNK)]), lane_roll(own, -8), lane_roll(own, 8))
        part = [s3[k, 1 + i, pl.ds(g, CHUNK)] * sides[i] for i in range(6)]
        return ((s3[k, 0, pl.ds(g, CHUNK)] + part[0]) + (part[1] + part[2])) + ((part[3] + part[4]) + part[5])

    def sweep3(k):
        for g in chunks:
            v3[k, pl.ds(1 + g, CHUNK)] = update3(k, g)

    sweep3(1)
    sweep3(0)
    sweep3(1)
    f4 = []
    for g in chunks:
        t = (update3(0, g) - v3[0, pl.ds(1 + g, CHUNK)]) * w3[pl.ds(g, CHUNK)]
        t = t + flip(t, 1)
        f4.append((t + flip(t, 8)) * 0.125)

    e4 = tiles_from_slots(e4)
    f4 = tiles_from_slots(f4)
    e4 = [e4[b] for b in range(CHUNK)]
    tile = (GX, LANES)
    lane = iota(tile, 1)
    even4 = (((lane >> 1) ^ (lane >> 2) ^ (lane >> 4)) & 1) == 0
    z_last4 = (lane >> 4) == 7
    scale = 0.25**4
    e_after = e4[1:] + [slot_after(e4[0], lane_roll(e4[-1], -2))]
    e_before = [slot_before(e4[-1], lane_roll(e4[0], 2))] + e4[:-1]
    v = []
    for b in range(CHUNK):
        own = e4[b]
        z = jnp.where(z_last4, 0.0, face(scale, own, lane_roll(own, -16)))
        parts = [face(scale, own, pair_before(own, own)), face(scale, own, pair_after(own, own)),
                 face(scale, own, y_after(4, own, e_after[b])), face(scale, own, y_before(4, own, e_before[b])),
                 z, lane_roll(z, 16)]
        weight_sum = parts[0]
        for t in parts[1:]:
            weight_sum = weight_sum + t
        inverse = 1.0 / weight_sum
        source = f4[b] * inverse
        s4[0, b] = source
        for i in range(6):
            s4[1 + i, b] = parts[i] * inverse
        v.append(jnp.where(even4, source, 0.0))

    def sweep4(k, v):
        v = list(v)
        after = v[1:] + [slot_after(v[0], 0.0)]
        before = [slot_before(v[-1], 0.0)] + v[:-1]
        new = []
        for b in range(CHUNK):
            own = v[b]
            x = s4[1, b] * pair_before(own, 0.0) + s4[2, b] * pair_after(own, 0.0)
            y = s4[3, b] * y_after(4, own, after[b]) + s4[4, b] * y_before(4, own, before[b])
            z = s4[5, b] * lane_roll(own, -16) + s4[6, b] * lane_roll(own, 16)
            value = (s4[0, b] + z) + (x + y)
            new.append(jnp.where(even4, value, own) if k == 0 else jnp.where(even4, own, value))
        return tuple(new)

    v = sweep4(1, v)
    if STOP >= 11:
        v = lax.fori_loop(0, COARSE_SWEEPS - 1, lambda i, v: sweep4(1, sweep4(0, v)), v)
    v = jnp.stack(v)
    slot = slots(BLOCK)
    for a, g in enumerate(chunks):
        here = pl.ds(1 + g, CHUNK)
        u = jnp.where(slot == a, v, 0.0)
        u = u + flip(u, 1)
        u = u + flip(u, 8)
        v3[0, here] = v3[0, here] + u
        v3[1, here] = v3[1, here] + u
    if STOP < 12:
        return
    sweep3(0)
    sweep3(1)
    sweep3(0)
    sweep3(1)


def around_from_level3(v3, up, gx, gy):
    shape = (GX, LANES)
    lane, sub = iota(shape, 1), iota(shape, 0)
    even3 = ((lane ^ (lane >> 3)) & 1) == 0
    head = (lane & 7) == 0
    outside = ((sub == 0) & (gx == 0)) | ((sub == 2) & (gx == GX - 1))
    up[...] = jnp.zeros(up.shape, F32)
    for dy in range(3):
        red = v3[0, gy + dy]
        black = v3[1, gy + dy]
        for r in range(2):
            t = jnp.where(even3, red, black) if r == 0 else jnp.where(even3, black, red)
            t = jnp.where(outside, 0.0, pltpu.roll(t, lax.rem(GX + 1 - gx, GX), 0))
            for s in range(8):
                w = jnp.where(head, lane_roll(t, -s), 0.0)
                w = w + lane_roll(w, 1)
                w = w + lane_roll(w, 2)
                w = w + lane_roll(w, 4)
                for dx in range(3):
                    x = 4 * dx + 2 * (s // 4) + r
                    y = 4 + 2 * (4 * dy + s % 4)
                    up[x, y : y + 2, :] = jnp.broadcast_to(w[dx : dx + 1], (2, LANES))


def climb(near, far, k0, kv0, k1, kv1, k2, kv2, out, f3, e3, s3, w3, v3, s4, v2, v1, v0,
          up3, up, s0, s1, s2, i0, i1, i2, sems, v_sems):
    gx, gy = lax.axis_index("gx"), lax.axis_index("gy")
    loads = []
    for level, kept, kept_v, state, v_in in ((2, k2, kv2, s2, i2), (1, k1, kv1, s1, i1), (0, k0, kv0, s0, i0)):
        first, last, low, high = KEPT[level]
        loads.append((
            pltpu.make_async_copy(kept, state.at[pl.ds(first, last - first), :, :, pl.ds(low, high - low), :],
                                  sems.at[level]),
            pltpu.make_async_copy(kept_v, v_in, v_sems.at[level]),
        ))
    for pair in loads:
        start_all(pair)
    clear(v2, 32)
    clear(v1, 48)
    clear(v0, 48)
    for c, held in enumerate((near, far)):
        for dx in range(4):
            for dy in range(4):
                g = (((gy // 8 + dx) & 3) * 4 + ((gy // 2 + dy) & 3)) * 2 + (gy & 1 if c == 0 else 1 - (gy & 1))
                for r in range(2):
                    f3[r, g] = held[dx, dy, pl.ds(r, GX, stride=4), :]
                    e3[r, 1 + g] = held[dx, dy, pl.ds(2 + r, GX, stride=4), :]
    coarse_levels(f3, e3, s3, w3, v3, s4)
    around_from_level3(v3, up3, gx, gy)

    wait_all(loads[0])
    if STOP >= 13:

        def add2(p):
            new = [i2[k, p - KEPT_V[2][0], 8:40, :] + up3[p - 2] for k in range(2)]

            def store():
                for k in range(2):
                    v2[k, p, 8:40, :] = new[k]

            return store

        loop(2, 14, add2, UNROLL["add"])
        half_sweep(2, 0, 6, v2, s2)
        half_sweep(2, 1, 5, v2, s2)
        half_sweep(2, 0, 4, v2, s2)
        half_sweep(2, 1, 3, v2, s2)

    def raised(level, first, last, offset, coarse_v, v_in, v):
        base = KEPT_V[level][0]

        def doubled(c):
            rows = 24
            even = pair_is_even(level + 1, rows)
            start = 8 + (12 if level == 0 else 4)
            red = coarse_v[0, c, start : start + rows, :]
            black = coarse_v[1, c, start : start + rows, :]
            both = (jnp.where(even, red, black), jnp.where(even, black, red))

            def store():
                for s in range(2):
                    for twice in range(2):
                        up[c, s, pl.ds(twice, rows, stride=2), :] = both[s]

            return store

        loop(first, last, doubled, 2)

        def add(c):
            new = [(k, 2 * c - offset + s, v_in[k, 2 * c - offset + s - base, 8:56, :] + up[c, s])
                   for s in range(2) for k in range(2)]

            def store():
                for k, p, value in new:
                    v[k, p, 8:56, :] = value

            return store

        loop(first, last, add, 1)

    wait_all(loads[1])
    if STOP >= 14:
        raised(1, 4, 12, 4, v2, i1, v1)
        half_sweep(1, 0, 5, v1, s1)
        half_sweep(1, 1, 4, v1, s1)
        half_sweep(1, 0, 3, v1, s1)
        half_sweep(1, 1, 2, v1, s1)

    wait_all(loads[2])
    if STOP >= 15:
        raised(0, 7, 17, 12, v1, i0, v0)
        half_sweep(0, 0, 3, v0, s0)
        half_sweep(0, 1, 2, v0, s0)
        half_sweep(0, 0, 1, v0, s0)
        half_sweep(0, 1, 0, v0, s0)
    even = pair_is_even(0, 32)

    def finish(q):
        red = v0[0, 4 + q, 16:48, :]
        black = v0[1, 4 + q, 16:48, :]

        def store():
            out[2 * q] = jnp.where(even, red, black)
            out[2 * q + 1] = jnp.where(even, black, red)

        return store

    loop(0, 16, finish, 4)


def shaped(*dims):
    return jax.ShapeDtypeStruct(dims, F32)


def kept_shapes(level):
    first, last, low, high = KEPT[level]
    v_first, v_last = KEPT_V[level]
    return (shaped(last - first, 2, 7, high - low, LANES),
            shaped(2, v_last - v_first, EXT[level] + 16, LANES))


def down_scratch(level):
    ext = EXT[level]
    vmem = [(ext // 2, 2, 7, ext, LANES), (2, ext // 2, ext + 16, LANES), (ext + 2, ext + 16, LANES),
            (ext, ext, LANES), (ext // 2, ext, LANES), (2, 16, ext, LANES)]
    return [pltpu.VMEM(s, F32) for s in vmem] + [pltpu.SemaphoreType.DMA((GROUPS + 1,))]


def kernel_call(body, in_spaces, out_shape, out_spaces, scratch, mib, *operands):
    def specs(spaces):
        return [pl.BlockSpec(memory_space=pltpu.VMEM if s == "v" else pl.ANY) for s in spaces]

    return pl.pallas_call(
        body,
        in_specs=specs(in_spaces),
        out_specs=tuple(specs(out_spaces)),
        out_shape=tuple(out_shape),
        scratch_shapes=scratch,
        compiler_params=pltpu.CompilerParams(vmem_limit_bytes=mib << 20),
        name=body.__name__,
    )(*operands)


def exchange(axis, to_next, to_previous):
    count = lax.axis_size(axis)
    onward = [(i, (i + 1) % count) for i in range(count)]
    backward = [((i + 1) % count, i) for i in range(count)]
    return lax.ppermute(to_next, axis, onward), lax.ppermute(to_previous, axis, backward)


def from_offset(values, dx, dy, dc):
    moves = []
    for g in range(GY):
        x, y, c = g // 8, (g // 2) % 4, g % 2
        moves.append((((x + dx) % 4 * 4 + (y + dy) % 4) * 2 + (c ^ dc), g))
    return lax.ppermute(values, "gy", moves)


def per_device(right_side, permittivity):
    both = (right_side, permittivity)
    xl, xr = exchange("gx", jnp.stack([b[24:] for b in both]), jnp.stack([b[:8] for b in both]))

    def y_slab(rows):
        middle = jnp.stack([b[:, rows] for b in both])
        return jnp.concatenate([xl[:, :, rows], middle, xr[:, :, rows]], axis=1)

    yl, yr = exchange("gy", y_slab(slice(24, 32)), y_slab(slice(0, 8)))
    p1, s0, v0 = kernel_call(
        down0, "aavvvv", (shaped(16, 16, LANES),) + kept_shapes(0), "vaa",
        down_scratch(0) + [pltpu.SemaphoreType.DMA((10,))], 24,
        right_side, permittivity, xl, xr, yl, yr)

    xl, xr = exchange("gx", p1, p1)
    wide = jnp.concatenate([xl, p1, xr], axis=0)
    yl, yr = exchange("gy", wide, wide)
    p2, s1, v1 = kernel_call(
        down1, "vvvvv", (shaped(16, 16, LANES),) + kept_shapes(1), "vaa", down_scratch(1), 24, p1, xl, xr, yl, yr)

    xl, xr = exchange("gx", p2[:8], p2[8:])
    wide = jnp.concatenate([xl, p2, xr], axis=0)
    yl, yr = exchange("gy", wide[:, :8], wide[:, 8:])
    p3, s2, v2 = kernel_call(
        down2, "vvvvv", (shaped(GX, 4, LANES),) + kept_shapes(2), "vaa",
        down_scratch(2) + [pltpu.VMEM((2, 4, 8, LANES), F32)], 14, p2, xl, xr, yl, yr)

    column = lax.all_to_all(p3, "gx", 0, 0, tiled=True).reshape(4 * GX, LANES)
    along_y = jnp.stack([column] + [from_offset(column, 0, d, 0) for d in (1, 2, 3)])
    near = jnp.stack([along_y] + [from_offset(along_y, d, 0, 0) for d in (1, 2, 3)])
    far = from_offset(near, 0, 0, 1)
    return climb_call(near, far, s0, v0, s1, v1, s2, v2)


def climb_call(*operands):
    rows = GY + 2
    vmem = [
        (2, GY, GX, LANES), (2, rows, GX, LANES), (2, 7, GY, GX, LANES), (GY, GX, LANES), (2, rows, GX, LANES),
        (7, CHUNK, GX, LANES),
        (2, 16, 48, LANES), (2, 24, 64, LANES), (2, 24, 64, LANES), (12, 32, LANES), (17, 2, 48, LANES),
    ]
    vmem += [(EXT[l] // 2, 2, 7, EXT[l], LANES) for l in range(3)]
    vmem += [kept_shapes(l)[1].shape for l in range(3)]
    scratch = [pltpu.VMEM(s, F32) for s in vmem] + [pltpu.SemaphoreType.DMA((3,))] * 2
    return kernel_call(climb, "vvaaaaaa", (shaped(32, 32, LANES),), "v", scratch, 36, *operands)[0]


def solution(mesh):
    placed = (P("gx", "gy", None), P("gx", "gy", None))
    return jax.shard_map(
        per_device, mesh=mesh, in_specs=placed, out_specs=P("gx", "gy", None), check_vma=False
    )
```

time: 195 us -> 128 us (0.66)
  Pallas kernels: 101 us -> 39.6 us
  blocking collectives: 34.2 us -> 11.1 us
  starting transfers between devices: 28.2 us -> 42.8 us
  waiting for transfers between devices: 23.1 us -> 31.4 us
  local copies, waits for them, and re-layouts: 7.93 us -> 2.46 us
    pallas_call x4, Pallas kernels: 101 us -> 39.6 us  [kernel_call(): pl.pallas_call(body, in_specs=specs(in_spaces), out_specs=tuple(specs(out...]
    all_to_all x1 -> x0, blocking collectives: 22.4 us -> none  [per_device(): lax.all_to_all(jnp.broadcast_to(column[None], (GY, 4 * GX, LANES)), 'gy',...]
    ppermute x0 -> x7, starting transfers between devices: none -> 14.1 us  [from_offset(): return lax.ppermute(values, 'gy', moves)]
    ppermute x0 -> x7, waiting for transfers between devices: none -> 7.16 us  [from_offset(): return lax.ppermute(values, 'gy', moves)]
    unnamed x28 -> x8, local copies, waits for them, and re-layouts: 4.68 us -> 0.04 us
  transfers between devices with their start and end apart: 12 -> 19, of which waited for: 9 -> 16; matrix products, arithmetic and copies ran while one was open for 2% -> 1% of each run, Pallas kernels for 0% -> 0%
where the time goes in v2:
time: 128 us
  starting transfers between devices  42.8 us (33%)
  Pallas kernels  39.6 us (31%)
  waiting for transfers between devices  31.4 us (25%)
  blocking collectives  11.1 us (9%)
  local copies, waits for them, and re-layouts  2.46 us (2%)
    pallas_call x4, Pallas kernels, kernel_call(): pl.pallas_call(body, in_specs=specs(in_spaces), out_specs=tuple(specs(out...  39.6 us
    ppermute x6, starting transfers between devices, exchange(): lax.ppermute(to_previous, axis, backward)  21.4 us
    ppermute x6, waiting for transfers between devices, exchange(): lax.ppermute(to_next, axis, onward)  15.1 us
    ppermute x7, starting transfers between devices, from_offset(): return lax.ppermute(values, 'gy', moves)  14.1 us
    all_to_all x1, blocking collectives, per_device(): column = lax.all_to_all(p3, 'gx', 0, 0, tiled=True).reshape(4 * GX, LANES)  11.1 us
    ppermute x6, waiting for transfers between devices, exchange(): lax.ppermute(to_previous, axis, backward)  9.07 us
    ppermute x6, starting transfers between devices, exchange(): lax.ppermute(to_next, axis, onward)  7.31 us
    ppermute x7, waiting for transfers between devices, from_offset(): return lax.ppermute(values, 'gy', moves)  7.16 us
  transfers between devices with their start and end apart: 19, of which 16 were waited for; matrix products, arithmetic and copies ran while one was open for 1% of the time, Pallas kernels for 0%

profile of v2, /device:TPU:1, one launch (start us, length us, event | category | flops | bytes accessed | tf_op | source)
XLA Modules:
  0.0 127.7 jit_solution(4582290053756704605)
XLA Ops:
  0.0 0.0 copy-start.1
  0.0 1.2 slice_bitcast_fusion.4
  1.3 2.5 %collective-permute-start = (f32[2,8,32,128]{3,2,1,0:T(8,128)S(1)}, f32[2,8,32,128]{3,2,1,0:T(8,128)S(1)}, u32[]{:S(2)}, u32[]{:S(2)}) collective-permute-start(f32[2,8,32,128]{3,2,1,0:T(8,128)S(1)} %pad_maximum_fusion.2), channel_id=1, source_target_pairs={{0,32},{32,64},{64,96},{96,128},{128,160},{160,192},{192,224},{224... | collective-permute-start | bytes 786440 | tf_op jit(solution)/shard_map/ppermute | solution.py:747
  3.8 4.0 %collective-permute-start.1 = (f32[2,8,32,128]{3,2,1,0:T(8,128)S(1)}, f32[2,8,32,128]{3,2,1,0:T(8,128)S(1)}, u32[]{:S(2)}, u32[]{:S(2)}) collective-permute-start(f32[2,8,32,128]{3,2,1,0:T(8,128)S(1)} %pad_maximum_fusion.3), channel_id=1, source_target_pairs={{32,0},{64,32},{96,64},{128,96},{160,128},{192,160},{224,192},{0,2... | collective-permute-start | bytes 786440 | tf_op jit(solution)/shard_map/ppermute | solution.py:747
  7.9 1.1 slice_bitcast_fusion
  9.0 4.8 %collective-permute-done.xl = f32[2,8,32,128]{3,2,1,0:T(8,128)S(1)} collective-permute-done((f32[2,8,32,128]{3,2,1,0:T(8,128)S(1)}, f32[2,8,32,128]{3,2,1,0:T(8,128)S(1)}, u32[]{:S(2)}, u32[]{:S(2)}) %collective-permute-start) | collective-permute-done | bytes 262176 | tf_op jit(solution)/shard_map/ppermute | solution.py:747
  13.8 0.0 collective-permute-done.1.xr
  13.8 2.5 %collective-permute-start.2 = (f32[2,48,8,128]{3,2,1,0:T(8,128)S(1)}, f32[2,48,8,128]{3,2,1,0:T(8,128)S(1)}, u32[]{:S(2)}, u32[]{:S(2)}) collective-permute-start(f32[2,48,8,128]{3,2,1,0:T(8,128)S(1)} %pad_maximum_fusion), channel_id=1, source_target_pairs={{0,1},{1,2},{2,3},{3,4},{4,5},{5,6},{6,7},{7,8},{8,9},{9,10},{10,1... | collective-permute-start | bytes 1179656 | tf_op jit(solution)/shard_map/ppermute | solution.py:747
  16.4 0.1 collective-permute-start.3
  16.5 4.6 %collective-permute-done.2.yl = f32[2,48,8,128]{3,2,1,0:T(8,128)S(1)} collective-permute-done((f32[2,48,8,128]{3,2,1,0:T(8,128)S(1)}, f32[2,48,8,128]{3,2,1,0:T(8,128)S(1)}, u32[]{:S(2)}, u32[]{:S(2)}) %collective-permute-start.2) | collective-permute-done | bytes 393248 | tf_op jit(solution)/shard_map/ppermute | solution.py:747
  21.1 2.9 %collective-permute-done.3.yr = f32[2,48,8,128]{3,2,1,0:T(8,128)S(1)} collective-permute-done((f32[2,48,8,128]{3,2,1,0:T(8,128)S(1)}, f32[2,48,8,128]{3,2,1,0:T(8,128)S(1)}, u32[]{:S(2)}, u32[]{:S(2)}) %collective-permute-start.3) | collective-permute-done | bytes 393248 | tf_op jit(solution)/shard_map/ppermute | solution.py:747
  23.9 0.0 copy-done.1
  23.9 0.0 copy-done
  23.9 9.2 %down0.1 = (f32[16,16,128]{2,1,0:T(8,128)S(1)}, f32[20,2,7,48,128]{4,3,2,1,0:T(8,128)S(1)}, f32[2,22,64,128]{3,2,1,0:T(8,128)S(1)}) custom-call(f32[32,32,128]{2,1,0:T(8,128)S(1)} %copy-done, f32[32,32,128]{2,1,0:T(8,128)S(1)} %copy-done.1, f32[2,8,32,128]{3,2,1,0:T(8,128)S(1)} %collective-permute-done.xl, f32[2,8,32,128]{3,2,1,0:T(8,128)S(1)} %collective-permute-done.1.xr, ...), custom_call_target="tpu_custom_call" | custom-call | tf_op jit(solution)/shard_map/down0/pallas_call | solution.py:732
  33.1 0.1 collective-permute-start.4
  33.2 2.8 %collective-permute-start.5 = (f32[16,16,128]{2,1,0:T(8,128)S(1)}, f32[16,16,128]{2,1,0:T(8,128)S(1)}, u32[]{:S(2)}, u32[]{:S(2)}) collective-permute-start(f32[16,16,128]{2,1,0:T(8,128)S(1)} %get-tuple-element.14.own), channel_id=1, source_target_pairs={{32,0},{64,32},{96,64},{128,96},{160,128},{192,160},{224,192},{0,2... | collective-permute-start | bytes 393224 | tf_op jit(solution)/shard_map/ppermute | solution.py:747
  36.1 2.3 %collective-permute-done.4.xl = f32[16,16,128]{2,1,0:T(8,128)S(1)} collective-permute-done((f32[16,16,128]{2,1,0:T(8,128)S(1)}, f32[16,16,128]{2,1,0:T(8,128)S(1)}, u32[]{:S(2)}, u32[]{:S(2)}) %collective-permute-start.4) | collective-permute-done | bytes 131104 | tf_op jit(solution)/shard_map/ppermute | solution.py:747
  38.4 0.0 collective-permute-done.5.xr
  38.4 2.9 %collective-permute-start.7 = (f32[48,16,128]{2,1,0:T(8,128)S(1)}, f32[48,16,128]{2,1,0:T(8,128)S(1)}, u32[]{:S(2)}, u32[]{:S(2)}) collective-permute-start(f32[48,16,128]{2,1,0:T(8,128)S(1)} %constant_dynamic-update-slice_fusion), channel_id=1, source_target_pairs={{1,0},{2,1},{3,2},{4,3},{5,4},{6,5},{7,6},{8,7},{9,8},{10,9},{11,1... | collective-permute-start | bytes 1179656 | tf_op jit(solution)/shard_map/ppermute | solution.py:747
  41.3 0.0 collective-permute-start.6
  41.3 4.3 %collective-permute-done.7.yr = f32[48,16,128]{2,1,0:T(8,128)S(1)} collective-permute-done((f32[48,16,128]{2,1,0:T(8,128)S(1)}, f32[48,16,128]{2,1,0:T(8,128)S(1)}, u32[]{:S(2)}, u32[]{:S(2)}) %collective-permute-start.7) | collective-permute-done | bytes 393248 | tf_op jit(solution)/shard_map/ppermute | solution.py:747
  45.7 0.9 collective-permute-done.6.yl
  46.6 7.8 %down1.1 = (f32[16,16,128]{2,1,0:T(8,128)S(1)}, f32[14,2,7,32,128]{4,3,2,1,0:T(8,128)S(1)}, f32[2,16,64,128]{3,2,1,0:T(8,128)S(1)}) custom-call(f32[16,16,128]{2,1,0:T(8,128)S(1)} %get-tuple-element.14.own, f32[16,16,128]{2,1,0:T(8,128)S(1)} %collective-permute-done.4.xl, f32[16,16,128]{2,1,0:T(8,128)S(1)} %collective-permute-done.5.xr, ...), custom_call_target="tpu_custom_call" | custom-call | tf_op jit(solution)/shard_map/down1/pallas_call | solution.py:732
  54.4 2.2 %collective-permute-start.8 = (f32[8,16,128]{2,1,0:T(8,128)S(1)}, f32[8,16,128]{2,1,0:T(8,128)S(1)}, u32[]{:S(2)}, u32[]{:S(2)}) collective-permute-start(f32[8,16,128]{2,1,0:T(8,128)S(1)} %get-tuple-element.38), channel_id=1, source_target_pairs={{0,32},{32,64},{64,96},{96,128},{128,160},{160,192},{192,224},{224... | collective-permute-start | bytes 196616 | tf_op jit(solution)/shard_map/ppermute | solution.py:747
  56.6 0.7 collective-permute-start.9
  57.3 1.6 %collective-permute-done.8.xl = f32[8,16,128]{2,1,0:T(8,128)S(1)} collective-permute-done((f32[8,16,128]{2,1,0:T(8,128)S(1)}, f32[8,16,128]{2,1,0:T(8,128)S(1)}, u32[]{:S(2)}, u32[]{:S(2)}) %collective-permute-start.8) | collective-permute-done | bytes 65568 | tf_op jit(solution)/shard_map/ppermute | solution.py:747
  58.9 0.8 collective-permute-done.9.xr
  59.7 10.8 %collective-permute-start.11 = (f32[32,8,128]{2,1,0:T(8,128)S(1)}, f32[32,8,128]{2,1,0:T(8,128)S(1)}, u32[]{:S(2)}, u32[]{:S(2)}) collective-permute-start(f32[32,8,128]{2,1,0:T(8,128)S(1)} %get-tuple-element.31), channel_id=1, source_target_pairs={{1,0},{2,1},{3,2},{4,3},{5,4},{6,5},{7,6},{8,7},{9,8},{10,9},{11,1... | collective-permute-start | bytes 393224 | tf_op jit(solution)/shard_map/ppermute | solution.py:747
  70.6 0.0 collective-permute-start.10
  70.6 1.0 collective-permute-done.11.yr
  71.6 1.0 collective-permute-done.10.yl
  72.5 5.6 %down2.1 = (f32[8,4,128]{2,1,0:T(4,128)S(1)}, f32[10,2,7,32,128]{4,3,2,1,0:T(8,128)S(1)}, f32[2,12,48,128]{3,2,1,0:T(8,128)S(1)}) custom-call(f32[16,16,128]{2,1,0:T(8,128)S(1)} %get-tuple-element.15.own, f32[8,16,128]{2,1,0:T(8,128)S(1)} %collective-permute-done.8.xl, f32[8,16,128]{2,1,0:T(8,128)S(1)} %collective-permute-done.9.xr, ...), custom_call_target="tpu_custom_call" | custom-call | tf_op jit(solution)/shard_map/down2/pallas_call | solution.py:732
  78.2 11.1 %all_to_all.5 = f32[8,4,128]{2,1,0:T(4,128)S(1)} all-to-all(f32[8,4,128]{2,1,0:T(4,128)S(1)} %get-tuple-element.16), channel_id=1, replica_groups=mesh['gx'=8,'gy'=32] {'gx'}, dimensions={0} | all-to-all | bytes 32768 | tf_op jit(solution)/shard_map/all_to_all | solution.py:785
  89.2 0.0 collective-permute-start.14
  89.2 1.7 %collective-permute-start.13 = (f32[32,128]{1,0:T(8,128)S(1)}, f32[32,128]{1,0:T(8,128)S(1)}, u32[]{:S(2)}, u32[]{:S(2)}) collective-permute-start(f32[32,128]{1,0:T(8,128)S(1)} %bitcast.27), channel_id=1, source_target_pairs={{4,0},{5,1},{6,2},{7,3},{0,4},{1,5},{2,6},{3,7},{12,8},{13,9},{14,... | collective-permute-start | bytes 49160 | tf_op jit(solution)/shard_map/ppermute | solution.py:755
  90.9 1.0 collective-permute-start.12
  91.9 1.1 collective-permute-done.14
  93.0 0.3 collective-permute-done.13
  93.3 0.8 collective-permute-done.12
  94.1 2.0 %collective-permute-start.16 = (f32[4,32,128]{2,1,0:T(8,128)S(1)}, f32[4,32,128]{2,1,0:T(8,128)S(1)}, u32[]{:S(2)}, u32[]{:S(2)}) collective-permute-start(f32[4,32,128]{2,1,0:T(8,128)S(1)} %get-tuple-element.40), channel_id=1, source_target_pairs={{16,0},{17,1},{18,2},{19,3},{20,4},{21,5},{22,6},{23,7},{24,8},{25... | collective-permute-start | bytes 196616 | tf_op jit(solution)/shard_map/ppermute | solution.py:755
  96.1 3.1 %collective-permute-start.15 = (f32[4,32,128]{2,1,0:T(8,128)S(1)}, f32[4,32,128]{2,1,0:T(8,128)S(1)}, u32[]{:S(2)}, u32[]{:S(2)}) collective-permute-start(f32[4,32,128]{2,1,0:T(8,128)S(1)} %get-tuple-element.40), channel_id=1, source_target_pairs={{8,0},{9,1},{10,2},{11,3},{12,4},{13,5},{14,6},{15,7},{16,8},{17,9... | collective-permute-start | bytes 196616 | tf_op jit(solution)/shard_map/ppermute | solution.py:755
  99.2 0.5 collective-permute-start.17
  99.6 0.0 collective-permute-done.16
  99.6 2.6 %collective-permute-done.15 = f32[4,32,128]{2,1,0:T(8,128)S(1)} collective-permute-done((f32[4,32,128]{2,1,0:T(8,128)S(1)}, f32[4,32,128]{2,1,0:T(8,128)S(1)}, u32[]{:S(2)}, u32[]{:S(2)}) %collective-permute-start.15) | collective-permute-done | bytes 65568 | tf_op jit(solution)/shard_map/ppermute | solution.py:755
  102.3 1.2 collective-permute-done.17
  103.5 5.9 %collective-permute-start.18 = (f32[4,4,32,128]{3,2,1,0:T(8,128)S(1)}, f32[4,4,32,128]{3,2,1,0:T(8,128)S(1)}, u32[]{:S(2)}, u32[]{:S(2)}) collective-permute-start(f32[4,4,32,128]{3,2,1,0:T(8,128)S(1)} %pad_maximum_fusion.4.near), channel_id=1, source_target_pairs={{1,0},{0,1},{3,2},{2,3},{5,4},{4,5},{7,6},{6,7},{9,8},{8,9},{11,10... | collective-permute-start | bytes 786440 | tf_op jit(solution)/shard_map/ppermute | solution.py:755
  109.4 1.2 collective-permute-done.18.far
  110.5 17.0 %climb.1 = f32[32,32,128]{2,1,0:T(8,128)} custom-call(f32[4,4,32,128]{3,2,1,0:T(8,128)S(1)} %pad_maximum_fusion.4.near, f32[4,4,32,128]{3,2,1,0:T(8,128)S(1)} %collective-permute-done.18.far, f32[20,2,7,48,128]{4,3,2,1,0:T(8,128)S(1)} %get-tuple-element.17.k0, f32[2,22,64,128]{3,2,1,0:T(8,128)S(1)} %get-tuple-element.18.kv0, ...), custom_call_target="tpu_custom_call" | custom-call | tf_op jit(solution)/shard_map/climb/pallas_call | solution.py:732
  (17 shorter events, 0.2 us)
Async XLA Ops:
  0.0 23.9 %copy-start.1 = (f32[32,32,128]{2,1,0:T(8,128)S(1)}, f32[32,32,128]{2,1,0:T(8,128)}, u32[]{:S(2)}) copy-start(f32[32,32,128]{2,1,0:T(8,128)} %e_in.1) | copy-start | bytes 1572868
  0.0 23.9 %copy-start = (f32[32,32,128]{2,1,0:T(8,128)S(1)}, f32[32,32,128]{2,1,0:T(8,128)}, u32[]{:S(2)}) copy-start(f32[32,32,128]{2,1,0:T(8,128)} %f_in.1) | copy-start | bytes 1572868
  1.3 12.5 %collective-permute-start = (f32[2,8,32,128]{3,2,1,0:T(8,128)S(1)}, f32[2,8,32,128]{3,2,1,0:T(8,128)S(1)}, u32[]{:S(2)}, u32[]{:S(2)}) collective-permute-start(f32[2,8,32,128]{3,2,1,0:T(8,128)S(1)} %pad_maximum_fusion.2), channel_id=1, source_target_pairs={{0,32},{32,64},{64,96},{96,128},{128,160},{160,192},{192,224},{224... | collective-permute-start | bytes 786440 | tf_op jit(solution)/shard_map/ppermute | solution.py:747
  3.8 10.0 %collective-permute-start.1 = (f32[2,8,32,128]{3,2,1,0:T(8,128)S(1)}, f32[2,8,32,128]{3,2,1,0:T(8,128)S(1)}, u32[]{:S(2)}, u32[]{:S(2)}) collective-permute-start(f32[2,8,32,128]{3,2,1,0:T(8,128)S(1)} %pad_maximum_fusion.3), channel_id=1, source_target_pairs={{32,0},{64,32},{96,64},{128,96},{160,128},{192,160},{224,192},{0,2... | collective-permute-start | bytes 786440 | tf_op jit(solution)/shard_map/ppermute | solution.py:747
  13.8 7.2 %collective-permute-start.2 = (f32[2,48,8,128]{3,2,1,0:T(8,128)S(1)}, f32[2,48,8,128]{3,2,1,0:T(8,128)S(1)}, u32[]{:S(2)}, u32[]{:S(2)}) collective-permute-start(f32[2,48,8,128]{3,2,1,0:T(8,128)S(1)} %pad_maximum_fusion), channel_id=1, source_target_pairs={{0,1},{1,2},{2,3},{3,4},{4,5},{5,6},{6,7},{7,8},{8,9},{9,10},{10,1... | collective-permute-start | bytes 1179656 | tf_op jit(solution)/shard_map/ppermute | solution.py:747
  16.4 7.6 %collective-permute-start.3 = (f32[2,48,8,128]{3,2,1,0:T(8,128)S(1)}, f32[2,48,8,128]{3,2,1,0:T(8,128)S(1)}, u32[]{:S(2)}, u32[]{:S(2)}) collective-permute-start(f32[2,48,8,128]{3,2,1,0:T(8,128)S(1)} %pad_maximum_fusion.1), channel_id=1, source_target_pairs={{1,0},{2,1},{3,2},{4,3},{5,4},{6,5},{7,6},{8,7},{9,8},{10,9},{11,1... | collective-permute-start | bytes 1179656 | tf_op jit(solution)/shard_map/ppermute | solution.py:747
  33.1 5.2 %collective-permute-start.4 = (f32[16,16,128]{2,1,0:T(8,128)S(1)}, f32[16,16,128]{2,1,0:T(8,128)S(1)}, u32[]{:S(2)}, u32[]{:S(2)}) collective-permute-start(f32[16,16,128]{2,1,0:T(8,128)S(1)} %get-tuple-element.14.own), channel_id=1, source_target_pairs={{0,32},{32,64},{64,96},{96,128},{128,160},{160,192},{192,224},{224... | collective-permute-start | bytes 393224 | tf_op jit(solution)/shard_map/ppermute | solution.py:747
  33.2 5.1 %collective-permute-start.5 = (f32[16,16,128]{2,1,0:T(8,128)S(1)}, f32[16,16,128]{2,1,0:T(8,128)S(1)}, u32[]{:S(2)}, u32[]{:S(2)}) collective-permute-start(f32[16,16,128]{2,1,0:T(8,128)S(1)} %get-tuple-element.14.own), channel_id=1, source_target_pairs={{32,0},{64,32},{96,64},{128,96},{160,128},{192,160},{224,192},{0,2... | collective-permute-start | bytes 393224 | tf_op jit(solution)/shard_map/ppermute | solution.py:747
  38.4 7.3 %collective-permute-start.7 = (f32[48,16,128]{2,1,0:T(8,128)S(1)}, f32[48,16,128]{2,1,0:T(8,128)S(1)}, u32[]{:S(2)}, u32[]{:S(2)}) collective-permute-start(f32[48,16,128]{2,1,0:T(8,128)S(1)} %constant_dynamic-update-slice_fusion), channel_id=1, source_target_pairs={{1,0},{2,1},{3,2},{4,3},{5,4},{6,5},{7,6},{8,7},{9,8},{10,9},{11,1... | collective-permute-start | bytes 1179656 | tf_op jit(solution)/shard_map/ppermute | solution.py:747
  41.3 5.3 %collective-permute-start.6 = (f32[48,16,128]{2,1,0:T(8,128)S(1)}, f32[48,16,128]{2,1,0:T(8,128)S(1)}, u32[]{:S(2)}, u32[]{:S(2)}) collective-permute-start(f32[48,16,128]{2,1,0:T(8,128)S(1)} %constant_dynamic-update-slice_fusion), channel_id=1, source_target_pairs={{0,1},{1,2},{2,3},{3,4},{4,5},{5,6},{6,7},{7,8},{8,9},{9,10},{10,1... | collective-permute-start | bytes 1179656 | tf_op jit(solution)/shard_map/ppermute | solution.py:747
  54.4 4.4 %collective-permute-start.8 = (f32[8,16,128]{2,1,0:T(8,128)S(1)}, f32[8,16,128]{2,1,0:T(8,128)S(1)}, u32[]{:S(2)}, u32[]{:S(2)}) collective-permute-start(f32[8,16,128]{2,1,0:T(8,128)S(1)} %get-tuple-element.38), channel_id=1, source_target_pairs={{0,32},{32,64},{64,96},{96,128},{128,160},{160,192},{192,224},{224... | collective-permute-start | bytes 196616 | tf_op jit(solution)/shard_map/ppermute | solution.py:747
  56.6 3.1 %collective-permute-start.9 = (f32[8,16,128]{2,1,0:T(8,128)S(1)}, f32[8,16,128]{2,1,0:T(8,128)S(1)}, u32[]{:S(2)}, u32[]{:S(2)}) collective-permute-start(f32[8,16,128]{2,1,0:T(8,128)S(1)} %get-tuple-element.37), channel_id=1, source_target_pairs={{32,0},{64,32},{96,64},{128,96},{160,128},{192,160},{224,192},{0,2... | collective-permute-start | bytes 196616 | tf_op jit(solution)/shard_map/ppermute | solution.py:747
  59.7 11.8 %collective-permute-start.11 = (f32[32,8,128]{2,1,0:T(8,128)S(1)}, f32[32,8,128]{2,1,0:T(8,128)S(1)}, u32[]{:S(2)}, u32[]{:S(2)}) collective-permute-start(f32[32,8,128]{2,1,0:T(8,128)S(1)} %get-tuple-element.31), channel_id=1, source_target_pairs={{1,0},{2,1},{3,2},{4,3},{5,4},{6,5},{7,6},{8,7},{9,8},{10,9},{11,1... | collective-permute-start | bytes 393224 | tf_op jit(solution)/shard_map/ppermute | solution.py:747
  70.6 2.0 %collective-permute-start.10 = (f32[32,8,128]{2,1,0:T(8,128)S(1)}, f32[32,8,128]{2,1,0:T(8,128)S(1)}, u32[]{:S(2)}, u32[]{:S(2)}) collective-permute-start(f32[32,8,128]{2,1,0:T(8,128)S(1)} %get-tuple-element.32), channel_id=1, source_target_pairs={{0,1},{1,2},{2,3},{3,4},{4,5},{5,6},{6,7},{7,8},{8,9},{9,10},{10,1... | collective-permute-start | bytes 393224 | tf_op jit(solution)/shard_map/ppermute | solution.py:747
  89.2 3.8 %collective-permute-start.14 = (f32[32,128]{1,0:T(8,128)S(1)}, f32[32,128]{1,0:T(8,128)S(1)}, u32[]{:S(2)}, u32[]{:S(2)}) collective-permute-start(f32[32,128]{1,0:T(8,128)S(1)} %bitcast.26), channel_id=1, source_target_pairs={{6,0},{7,1},{0,2},{1,3},{2,4},{3,5},{4,6},{5,7},{14,8},{15,9},{8,1... | collective-permute-start | bytes 49160 | tf_op jit(solution)/shard_map/ppermute | solution.py:755
  89.2 4.1 %collective-permute-start.13 = (f32[32,128]{1,0:T(8,128)S(1)}, f32[32,128]{1,0:T(8,128)S(1)}, u32[]{:S(2)}, u32[]{:S(2)}) collective-permute-start(f32[32,128]{1,0:T(8,128)S(1)} %bitcast.27), channel_id=1, source_target_pairs={{4,0},{5,1},{6,2},{7,3},{0,4},{1,5},{2,6},{3,7},{12,8},{13,9},{14,... | collective-permute-start | bytes 49160 | tf_op jit(solution)/shard_map/ppermute | solution.py:755
  90.9 3.2 %collective-permute-start.12 = (f32[32,128]{1,0:T(8,128)S(1)}, f32[32,128]{1,0:T(8,128)S(1)}, u32[]{:S(2)}, u32[]{:S(2)}) collective-permute-start(f32[32,128]{1,0:T(8,128)S(1)} %bitcast.28), channel_id=1, source_target_pairs={{2,0},{3,1},{4,2},{5,3},{6,4},{7,5},{0,6},{1,7},{10,8},{11,9},{12,... | collective-permute-start | bytes 49160 | tf_op jit(solution)/shard_map/ppermute | solution.py:755
  94.1 5.6 %collective-permute-start.16 = (f32[4,32,128]{2,1,0:T(8,128)S(1)}, f32[4,32,128]{2,1,0:T(8,128)S(1)}, u32[]{:S(2)}, u32[]{:S(2)}) collective-permute-start(f32[4,32,128]{2,1,0:T(8,128)S(1)} %get-tuple-element.40), channel_id=1, source_target_pairs={{16,0},{17,1},{18,2},{19,3},{20,4},{21,5},{22,6},{23,7},{24,8},{25... | collective-permute-start | bytes 196616 | tf_op jit(solution)/shard_map/ppermute | solution.py:755
  96.1 6.2 %collective-permute-start.15 = (f32[4,32,128]{2,1,0:T(8,128)S(1)}, f32[4,32,128]{2,1,0:T(8,128)S(1)}, u32[]{:S(2)}, u32[]{:S(2)}) collective-permute-start(f32[4,32,128]{2,1,0:T(8,128)S(1)} %get-tuple-element.40), channel_id=1, source_target_pairs={{8,0},{9,1},{10,2},{11,3},{12,4},{13,5},{14,6},{15,7},{16,8},{17,9... | collective-permute-start | bytes 196616 | tf_op jit(solution)/shard_map/ppermute | solution.py:755
  99.2 4.3 %collective-permute-start.17 = (f32[4,32,128]{2,1,0:T(8,128)S(1)}, f32[4,32,128]{2,1,0:T(8,128)S(1)}, u32[]{:S(2)}, u32[]{:S(2)}) collective-permute-start(f32[4,32,128]{2,1,0:T(8,128)S(1)} %get-tuple-element.40), channel_id=1, source_target_pairs={{24,0},{25,1},{26,2},{27,3},{28,4},{29,5},{30,6},{31,7},{0,8},{1,9... | collective-permute-start | bytes 196616 | tf_op jit(solution)/shard_map/ppermute | solution.py:755
  103.5 7.0 %collective-permute-start.18 = (f32[4,4,32,128]{3,2,1,0:T(8,128)S(1)}, f32[4,4,32,128]{3,2,1,0:T(8,128)S(1)}, u32[]{:S(2)}, u32[]{:S(2)}) collective-permute-start(f32[4,4,32,128]{3,2,1,0:T(8,128)S(1)} %pad_maximum_fusion.4.near), channel_id=1, source_target_pairs={{1,0},{0,1},{3,2},{2,3},{5,4},{4,5},{7,6},{6,7},{9,8},{8,9},{11,10... | collective-permute-start | bytes 786440 | tf_op jit(solution)/shard_map/ppermute | solution.py:755

commit v3 on v2

--- a/solution.py
+++ b/solution.py
@@ -14,10 +14,14 @@
 GX = 8
 GY = 32
 CHUNK = 8
+C3 = 1
+KEPT = (5, 19, 8, 40)
+GROUPS = 4
 
 
 UNROLL = {"sweep": 6, "restrict": 4, "put": 16, "add": 4}
 STOP = 99
+KEPT_SPEC = "vvv"
 
 
 def loop(first, last, body, step):
@@ -76,7 +80,7 @@
 
             @pl.when(gy == back)
             def _():
-                e[:, 8 + low - 1 : 8 + low, :] = e[:, 8 + low : 8 + low + 1, :]
+                e[0:ext, 8 + low - 1 : 8 + low, :] = e[0:ext, 8 + low : 8 + low + 1, :]
 
         if high < ext:
 
@@ -86,16 +90,27 @@
 
             @pl.when(gy == GY - 1 - back)
             def _():
-                e[:, 8 + high : 8 + high + 1, :] = e[:, 8 + high - 1 : 8 + high, :]
+                e[0:ext, 8 + high : 8 + high + 1, :] = e[0:ext, 8 + high - 1 : 8 + high, :]
+
+
+def faces(pairs):
+    sums = [a + b for a, b in pairs]
+    first = sums[0] * sums[1]
+    whole = 1.0 / (first * sums[2])
+    rest = whole * sums[2]
+    inverse = (rest * sums[1], rest * sums[0], whole * first)
+    return [a * b * i for (a, b), i in zip(pairs, inverse)]
+
+
+def inverses(a, b):
+    whole = 1.0 / (a * b)
+    return whole * b, whole * a
 
 
 def prepare(level, first, last, e, f, state, total, v, gx, gy, after_pair=None):
     ext = EXT[level]
     step = 1 << level
-    scale = 2.0 * 0.25**level
-
-    def face(a, b):
-        return scale * a * b / (a + b)
+    source_scale = 0.5 * 4.0**level
 
     xlow, xhigh = bounds(level, gx, GX)
     ylow, yhigh = bounds(level, gy, GY)
@@ -103,7 +118,7 @@
     lane = iota(shape, 1)
     z_last = (lane >> level) == (LANES >> level) - 1
     even = pair_is_even(level, 8)
-    x_odd = jnp.where(even, 0, 1)
+    aligned = all((HALO[level] + i * OWN[level]) % 8 == 0 for i in range(2))
 
     def tile(p, r, before, below):
         mid = slice(8 + r, 16 + r)
@@ -111,41 +126,41 @@
         e0 = e[2 * p, mid, :]
         e1 = e[2 * p + 1, mid, :]
         after = e[2 * p + 2, mid, :]
-        inner = face(e0, e1)
         outer0 = before
-        outer1 = face(e1, after)
-        yp0 = face(e0, e[2 * p, up, :])
-        yp1 = face(e1, e[2 * p + 1, up, :])
+        inner, outer1, yp0 = faces(((e0, e1), (e1, after), (e0, e[2 * p, up, :])))
+        yp1, zp0, zp1 = faces(((e1, e[2 * p + 1, up, :]), (e0, lane_roll(e0, -step)), (e1, lane_roll(e1, -step))))
+        zp0 = jnp.where(z_last, 0.0, zp0)
+        zp1 = jnp.where(z_last, 0.0, zp1)
         turned = pltpu.roll(yp0, 1, 0), pltpu.roll(yp1, 1, 0)
         if below is None:
             below = turned
         ym0, ym1 = (jnp.where(top, below[i], turned[i]) for i in range(2))
-        zp0 = jnp.where(z_last, 0.0, face(e0, lane_roll(e0, -step)))
-        zp1 = jnp.where(z_last, 0.0, face(e1, lane_roll(e1, -step)))
         zm0 = lane_roll(zp0, step)
         zm1 = lane_roll(zp1, step)
         f0 = f[2 * p, r : r + 8, :]
         f1 = f[2 * p + 1, r : r + 8, :]
-        row = r + iota(shape, 0)
-        y_ok = (row >= ylow) & (row < yhigh)
+        ok = (2 * p >= xlow) & (2 * p < xhigh)
+        if aligned:
+            ok = jnp.where(ok & (r >= ylow) & (r < yhigh), 1.0, 0.0)
+        else:
+            row = r + iota(shape, 0)
+            ok = jnp.where(ok, 1.0, 0.0) * jnp.where((row >= ylow) & (row < yhigh), 1.0, 0.0)
+        sides, sums = [], []
         for k in range(2):
             pick = even if k == 0 else jnp.logical_not(even)
-            outer = jnp.where(pick, outer0, outer1)
-            yp = jnp.where(pick, yp0, yp1)
-            ym = jnp.where(pick, ym0, ym1)
-            zp = jnp.where(pick, zp0, zp1)
-            zm = jnp.where(pick, zm0, zm1)
-            weight_sum = (inner + outer) + (yp + ym) + (zp + zm)
-            x_at = 2 * p + (x_odd if k == 0 else 1 - x_odd)
-            ok = y_ok & (x_at >= xlow) & (x_at < xhigh)
-            inverse = jnp.where(ok, 1.0 / weight_sum, 0.0)
-            source = jnp.where(pick, f0, f1) * inverse
-            parts = (source, inner * inverse, outer * inverse, yp * inverse, ym * inverse,
-                     zp * inverse, zm * inverse)
-            for i in range(7):
-                state[p, k, i, r : r + 8, :] = parts[i]
+            side = [inner] + [jnp.where(pick, a, b) for a, b in (
+                (outer0, outer1), (yp0, yp1), (ym0, ym1), (zp0, zp1), (zm0, zm1))]
+            sides.append(side)
+            sums.append((side[0] + side[1]) + (side[2] + side[3]) + (side[4] + side[5]))
+        inverse = inverses(*sums)
+        for k in range(2):
+            scaled = inverse[k] * ok
+            source = (jnp.where(even, f0, f1) if k == 0 else jnp.where(even, f1, f0)) * (scaled * source_scale)
+            state[p, k, 0, r : r + 8, :] = source
+            for i in range(6):
+                state[p, k, 1 + i, r : r + 8, :] = sides[k][i] * scaled
             if k == 0:
-                total[p, r : r + 8, :] = weight_sum
+                total[p, r : r + 8, :] = sums[0]
                 v[0, p, mid, :] = source
         return outer1, turned
 
@@ -161,8 +176,11 @@
         return tuple(new)
 
     start = max(2 * first - 1, 0)
-    init = tuple(face(e[start, 8 + 8 * c : 16 + 8 * c, :], e[2 * first, 8 + 8 * c : 16 + 8 * c, :])
-                 for c in range(ext // 8))
+    init = []
+    for c in range(ext // 8):
+        a, b = e[start, 8 + 8 * c : 16 + 8 * c, :], e[2 * first, 8 + 8 * c : 16 + 8 * c, :]
+        init.append(a * b / (a + b))
+    init = tuple(init)
     lax.fori_loop(first, last, body, init)
 
 
@@ -176,7 +194,7 @@
     lax.fori_loop(0, ext // 8, body, 0)
 
 
-def updated(level, k, p, v, state, low, high):
+def updated(level, k, p, v, state, low, high, base=(0, 0)):
     step = 1 << level
     even = pair_is_even(level, high - low)
     mid = slice(8 + low, 8 + high)
@@ -185,14 +203,15 @@
     before = v[other, p - 1, mid, :]
     after = v[other, p + 1, mid, :]
     outer = jnp.where(even, before, after) if k == 0 else jnp.where(even, after, before)
-    part = [state[p, k, 1 + i, low:high, :] for i in range(6)]
+    rows = slice(low - base[1], high - base[1])
+    part = [state[p - base[0], k, 1 + i, rows, :] for i in range(6)]
     x = part[0] * here + part[1] * outer
     y = part[2] * v[other, p, 9 + low : 9 + high, :] + part[3] * v[other, p, 7 + low : 7 + high, :]
     z = part[4] * lane_roll(here, -step) + part[5] * lane_roll(here, step)
-    return (state[p, k, 0, low:high, :] + x) + (y + z)
-
-
-def half_sweep(level, k, reach, v, state):
+    return (state[p - base[0], k, 0, rows, :] + x) + (y + z)
+
+
+def half_sweep(level, k, reach, v, state, base=(0, 0)):
     own, halo, ext = OWN[level], HALO[level], EXT[level]
     first = (halo - reach) // 2
     last = (halo + own + reach + 1) // 2
@@ -200,7 +219,7 @@
     high = -(-(halo + own + reach) // 8) * 8
 
     def body(p):
-        value = updated(level, k, p, v, state, low, high)
+        value = updated(level, k, p, v, state, low, high, base)
 
         def store():
             v[k, p, 8 + low : 8 + high, :] = value
@@ -231,7 +250,7 @@
         out = []
         for i in range(2):
             a = tmp[i, q, pl.ds(row, count, stride=2), :] + tmp[i, q, pl.ds(row + 1, count, stride=2), :]
-            out.append((a + flip(a, step)) * 0.125)
+            out.append((a + flip(a, step)) * (0.125 if i else 0.25 * 0.25**level))
         return lambda: put(q, out[0], out[1])
 
     loop(0, pairs, fine, UNROLL["restrict"])
@@ -263,124 +282,114 @@
         copy.wait()
 
 
-KEPT = ((2, 22, 0, 48), (5, 19, 8, 40), (3, 13, 0, 32))
-KEPT_V = ((1, 23), (4, 20), (2, 14))
-GROUPS = 4
-
-
-def state_copies(level, kept, vmem, sems):
-    first, last, low, high = KEPT[level]
-    copies = []
-    for g in range(GROUPS):
-        a = first + (last - first) * g // GROUPS
-        b = first + (last - first) * (g + 1) // GROUPS
-        copies.append((vmem.at[pl.ds(a, b - a), :, :, pl.ds(low, high - low), :],
-                       kept.at[pl.ds(a - first, b - a)], sems.at[g], b - 1))
-    return copies
-
-
-def v_copy(level, kept_v, v, sem):
-    first, last = KEPT_V[level]
-    return v.at[:, pl.ds(first, last - first)], kept_v, sem
-
-
-def sweep_down(level, pairs, reaches, inner, e, f, kept, kept_v, state, v, total, tmp, sems, gx, gy, put):
+def sweep_down(level, pairs, reaches, inner, e, f, state, v, total, tmp, gx, gy, put, after_pair=None):
     clamp_edges(level, e, gx, gy)
-    clear(v, EXT[level])
-    outgoing = state_copies(level, kept, state, sems)
-
-    def after_pair(p):
-        for source, target, sem, last in outgoing:
-
-            @pl.when(p == last)
-            def _():
-                pltpu.make_async_copy(source, target, sem).start()
-
     prepare(level, pairs[0], pairs[1], e, f, state, total, v, gx, gy, after_pair)
     if STOP >= 2:
         half_sweep(level, 1, reaches[0], v, state)
         half_sweep(level, 0, reaches[1], v, state)
         half_sweep(level, 1, reaches[2], v, state)
-    source, target, sem = v_copy(level, kept_v, v, sems.at[GROUPS])
-    v_out = pltpu.make_async_copy(source, target, sem)
-    v_out.start()
     if STOP >= 3:
         restrict(level, *inner, v, state, total, e, tmp, put)
-    for source, target, sem, last in outgoing:
-        pltpu.make_async_copy(source, target, sem).wait()
-    v_out.wait()
-
-
-def down0(f_in, e_in, xl, xr, yl, yr, out, kept, kept_v, state, v, e, f, total, tmp, sems, in_sems):
+
+
+def down0(f_in, e_in, xl, xr, yl, yr, cl, cr, out, state, v, e, f, total, tmp, in_sems):
     gx, gy = lax.axis_index("gx"), lax.axis_index("gy")
+    ya, yb = 0, 40
     copies = []
     for i, (target, own, off) in enumerate(((f, f_in, 0), (e, e_in, 8))):
         parts = (
             (xl.at[i], target.at[pl.ds(0, 8), pl.ds(off + 8, 32)]),
             (own, target.at[pl.ds(8, 32), pl.ds(off + 8, 32)]),
             (xr.at[i], target.at[pl.ds(40, 8), pl.ds(off + 8, 32)]),
-            (yl.at[i], target.at[pl.ds(0, 48), pl.ds(off, 8)]),
-            (yr.at[i], target.at[pl.ds(0, 48), pl.ds(off + 40, 8)]),
+            (yl.at[i], target.at[pl.ds(8, 32), pl.ds(off + ya, 8)]),
+            (yr.at[i], target.at[pl.ds(8, 32), pl.ds(off + yb, 8)]),
+            (cl.at[i, pl.ds(0, 8)], target.at[pl.ds(0, 8), pl.ds(off + ya, 8)]),
+            (cl.at[i, pl.ds(8, 8)], target.at[pl.ds(40, 8), pl.ds(off + ya, 8)]),
+            (cr.at[i, pl.ds(0, 8)], target.at[pl.ds(0, 8), pl.ds(off + yb, 8)]),
+            (cr.at[i, pl.ds(8, 8)], target.at[pl.ds(40, 8), pl.ds(off + yb, 8)]),
         )
         for j, (source, to) in enumerate(parts):
-            copies.append(pltpu.make_async_copy(source, to, in_sems.at[5 * i + j]))
+            copies.append(pltpu.make_async_copy(source, to, in_sems.at[9 * i + j]))
     start_all(copies)
     fill_rim(e, 48)
+    clear(v, 48)
     wait_all(copies)
 
     def put(q, fc, ec):
         out[q] = interleave(fc, ec)
 
     if STOP >= 1:
-        sweep_down(0, (0, 24), (6, 5, 4), (4, 16, 8, 16), e, f, kept, kept_v, state, v, total, tmp, sems, gx, gy, put)
-
-
-def put_split(source, count, x, y, e, f):
+        sweep_down(0, (0, 24), (6, 5, 4), (4, 16, 8, 16), e, f, state, v, total, tmp, gx, gy, put)
+
+
+def put_split(source, start, count, x, y, e, f):
     height = source.shape[1]
 
     def body(i):
-        fi, ei = split(source[i])
+        fi, ei = split(source[start + i])
 
         def store():
-            f[x + i, y : y + height, :] = fi
-            e[x + i, 8 + y : 8 + y + height, :] = ei
+            f[x + i, pl.ds(y, height), :] = fi
+            e[x + i, pl.ds(8 + y, height), :] = ei
 
         return store
 
     loop(0, count, body, UNROLL["put"])
 
 
-def down1(own, xl, xr, yl, yr, out, kept, kept_v, state, v, e, f, total, tmp, sems):
+def down1(own, xl, xr, yl, yr, cl, cr, out, kept, v, e, f, total, tmp, state, sems):
     gx, gy = lax.axis_index("gx"), lax.axis_index("gy")
     fill_rim(e, 48)
-    put_split(xl, 16, 0, 16, e, f)
-    put_split(own, 16, 16, 16, e, f)
-    put_split(xr, 16, 32, 16, e, f)
-    put_split(yl, 48, 0, 0, e, f)
-    put_split(yr, 48, 0, 32, e, f)
+    clear(v, 48)
+    put_split(xl, 0, 13, 3, 16, e, f)
+    put_split(own, 0, 16, 16, 16, e, f)
+    put_split(xr, 0, 13, 32, 16, e, f)
+    for side, corner, y in ((yl, cl, 0), (yr, cr, 32)):
+        put_split(corner, 0, 13, 3, y, e, f)
+        put_split(side, 0, 16, 16, y, e, f)
+        put_split(corner, 13, 13, 32, y, e, f)
 
     def put(q, fc, ec):
         out[q] = interleave(fc, ec)
 
-    if STOP >= 1:
-        sweep_down(1, (2, 22), (11, 10, 9), (4, 16, 8, 16), e, f, kept, kept_v, state, v, total, tmp, sems, gx, gy, put)
-
-
-def down2(own, xl, xr, yl, yr, out, kept, kept_v, state, v, e, f, total, tmp, sems, coarse):
+    first, last, low, high = KEPT
+    copies = []
+    for g in range(GROUPS):
+        a = first + (last - first) * g // GROUPS
+        b = first + (last - first) * (g + 1) // GROUPS
+        copies.append((b - 1, pltpu.make_async_copy(
+            state.at[pl.ds(a, b - a), :, :, pl.ds(low, high - low), :], kept.at[pl.ds(a - first, b - a)], sems.at[g])))
+
+    def after_pair(p):
+        for end, copy in copies:
+
+            @pl.when(p == end)
+            def _():
+                copy.start()
+
+    sweep_down(1, (2, 22), (11, 10, 9), (4, 16, 8, 16), e, f, state, v, total, tmp, gx, gy, put, after_pair)
+    wait_all([copy for _, copy in copies])
+
+
+def down2(own, xl, xr, yl, yr, cl, cr, out, state, v, e, f, total, tmp, coarse):
     gx, gy = lax.axis_index("gx"), lax.axis_index("gy")
     fill_rim(e, 32)
-    put_split(xl, 8, 0, 8, e, f)
-    put_split(own, 16, 8, 8, e, f)
-    put_split(xr, 8, 24, 8, e, f)
-    put_split(yl, 32, 0, 0, e, f)
-    put_split(yr, 32, 0, 24, e, f)
+    clear(v, 32)
+    put_split(xl, 0, 8, 0, 8, e, f)
+    put_split(own, 0, 16, 8, 8, e, f)
+    put_split(xr, 0, 8, 24, 8, e, f)
+    for side, corner, y in ((yl, cl, 0), (yr, cr, 24)):
+        put_split(corner, 0, 8, 0, y, e, f)
+        put_split(side, 0, 16, 8, y, e, f)
+        put_split(corner, 8, 8, 24, y, e, f)
 
     def put(q, fc, ec):
         coarse[0, q, 0:4, :] = fc
         coarse[1, q, 0:4, :] = ec
 
     if STOP >= 1:
-        sweep_down(2, (1, 15), (9, 8, 7), (6, 4, 12, 4), e, f, kept, kept_v, state, v, total, tmp, sems, gx, gy, put)
+        sweep_down(2, (1, 15), (9, 8, 7), (6, 4, 12, 4), e, f, state, v, total, tmp, gx, gy, put)
     slot = iota((1, LANES), 1) & 7
     for i in range(2):
         for r in range(2):
@@ -443,10 +452,10 @@
 
 
 def coarse_levels(f3, e3, s3, w3, v3, s4):
-    lane = iota(BLOCK, 2)
+    lane = iota((C3, GX, LANES), 2)
     even3 = ((lane ^ (lane >> 3)) & 1) == 0
     z_last3 = (lane >> 3) == 15
-    chunks = range(0, GY, CHUNK)
+    chunks = range(0, GY, C3)
 
     def face(scale, a, b):
         return (2.0 * scale) * a * b / (a + b)
@@ -460,7 +469,7 @@
     scale = 0.25**3
     e4 = []
     for g in chunks:
-        here = pl.ds(1 + g, CHUNK)
+        here = pl.ds(1 + g, C3)
         both = (e3[0, here], e3[1, here])
         inner = face(scale, both[0], both[1])
         outer = (face(scale, both[0], pair_before(both[1], both[0])),
@@ -468,12 +477,12 @@
         yp, ym, zp, zm, f = [], [], [], [], []
         for r in range(2):
             own = both[r]
-            yp.append(face(scale, own, y_after(3, own, e3[r, pl.ds(2 + g, CHUNK)])))
-            ym.append(face(scale, own, y_before(3, own, e3[r, pl.ds(g, CHUNK)])))
+            yp.append(face(scale, own, y_after(3, own, e3[r, pl.ds(2 + g, C3)])))
+            ym.append(face(scale, own, y_before(3, own, e3[r, pl.ds(g, C3)])))
             z = jnp.where(z_last3, 0.0, face(scale, own, lane_roll(own, -8)))
             zp.append(z)
             zm.append(lane_roll(z, 8))
-            f.append(f3[r, pl.ds(g, CHUNK)])
+            f.append(f3[r, pl.ds(g, C3)])
         for k in range(2):
             a, b = k, 1 - k
             parts = [jnp.where(even3, t[a], t[b]) for t in (outer, yp, ym, zp, zm)]
@@ -482,12 +491,12 @@
                 weight_sum = weight_sum + t
             inverse = 1.0 / weight_sum
             source = jnp.where(even3, f[a], f[b]) * inverse
-            s3[k, 0, pl.ds(g, CHUNK)] = source
-            s3[k, 1, pl.ds(g, CHUNK)] = inner * inverse
+            s3[k, 0, pl.ds(g, C3)] = source
+            s3[k, 1, pl.ds(g, C3)] = inner * inverse
             for i in range(5):
-                s3[k, 2 + i, pl.ds(g, CHUNK)] = parts[i] * inverse
+                s3[k, 2 + i, pl.ds(g, C3)] = parts[i] * inverse
             if k == 0:
-                w3[pl.ds(g, CHUNK)] = weight_sum
+                w3[pl.ds(g, C3)] = weight_sum
                 v3[0, here] = source
         t = both[0] + both[1]
         t = t + flip(t, 1)
@@ -495,30 +504,32 @@
 
     def update3(k, g):
         o = 1 - k
-        own = v3[o, pl.ds(1 + g, CHUNK)]
+        own = v3[o, pl.ds(1 + g, C3)]
         before, after = pair_before(own, 0.0), pair_after(own, 0.0)
         outer = jnp.where(even3, before, after) if k == 0 else jnp.where(even3, after, before)
-        sides = (own, outer, y_after(3, own, v3[o, pl.ds(2 + g, CHUNK)]),
-                 y_before(3, own, v3[o, pl.ds(g, CHUNK)]), lane_roll(own, -8), lane_roll(own, 8))
-        part = [s3[k, 1 + i, pl.ds(g, CHUNK)] * sides[i] for i in range(6)]
-        return ((s3[k, 0, pl.ds(g, CHUNK)] + part[0]) + (part[1] + part[2])) + ((part[3] + part[4]) + part[5])
+        sides = (own, outer, y_after(3, own, v3[o, pl.ds(2 + g, C3)]),
+                 y_before(3, own, v3[o, pl.ds(g, C3)]), lane_roll(own, -8), lane_roll(own, 8))
+        part = [s3[k, 1 + i, pl.ds(g, C3)] * sides[i] for i in range(6)]
+        return ((s3[k, 0, pl.ds(g, C3)] + part[0]) + (part[1] + part[2])) + ((part[3] + part[4]) + part[5])
 
     def sweep3(k):
         for g in chunks:
-            v3[k, pl.ds(1 + g, CHUNK)] = update3(k, g)
+            v3[k, pl.ds(1 + g, C3)] = update3(k, g)
 
     sweep3(1)
     sweep3(0)
     sweep3(1)
     f4 = []
     for g in chunks:
-        t = (update3(0, g) - v3[0, pl.ds(1 + g, CHUNK)]) * w3[pl.ds(g, CHUNK)]
+        t = (update3(0, g) - v3[0, pl.ds(1 + g, C3)]) * w3[pl.ds(g, C3)]
         t = t + flip(t, 1)
         f4.append((t + flip(t, 8)) * 0.125)
 
-    e4 = tiles_from_slots(e4)
-    f4 = tiles_from_slots(f4)
-    e4 = [e4[b] for b in range(CHUNK)]
+    def regroup(parts):
+        tiles = [part[i] for part in parts for i in range(C3)]
+        return [tiles_from_slots(tiles[b::CHUNK]) for b in range(CHUNK)]
+
+    e4, f4 = regroup(e4), regroup(f4)
     tile = (GX, LANES)
     lane = iota(tile, 1)
     even4 = (((lane >> 1) ^ (lane >> 2) ^ (lane >> 4)) & 1) == 0
@@ -560,15 +571,15 @@
     v = sweep4(1, v)
     if STOP >= 11:
         v = lax.fori_loop(0, COARSE_SWEEPS - 1, lambda i, v: sweep4(1, sweep4(0, v)), v)
-    v = jnp.stack(v)
-    slot = slots(BLOCK)
-    for a, g in enumerate(chunks):
-        here = pl.ds(1 + g, CHUNK)
-        u = jnp.where(slot == a, v, 0.0)
-        u = u + flip(u, 1)
-        u = u + flip(u, 8)
-        v3[0, here] = v3[0, here] + u
-        v3[1, here] = v3[1, here] + u
+    slot = slots(tile)
+    for a in range(GY // CHUNK):
+        for b in range(CHUNK):
+            u = jnp.where(slot == a, v[b], 0.0)
+            u = u + flip(u, 1)
+            u = u + flip(u, 8)
+            g = 1 + CHUNK * a + b
+            v3[0, g] = v3[0, g] + u
+            v3[1, g] = v3[1, g] + u
     if STOP < 12:
         return
     sweep3(0)
@@ -601,19 +612,9 @@
                     up[x, y : y + 2, :] = jnp.broadcast_to(w[dx : dx + 1], (2, LANES))
 
 
-def climb(near, far, k0, kv0, k1, kv1, k2, kv2, out, f3, e3, s3, w3, v3, s4, v2, v1, v0,
-          up3, up, s0, s1, s2, i0, i1, i2, sems, v_sems):
+def climb(near, far, s0, i0, s1, i1, s2, i2, out, f3, e3, s3, w3, v3, s4, v2, v1, v0,
+          up3, up):
     gx, gy = lax.axis_index("gx"), lax.axis_index("gy")
-    loads = []
-    for level, kept, kept_v, state, v_in in ((2, k2, kv2, s2, i2), (1, k1, kv1, s1, i1), (0, k0, kv0, s0, i0)):
-        first, last, low, high = KEPT[level]
-        loads.append((
-            pltpu.make_async_copy(kept, state.at[pl.ds(first, last - first), :, :, pl.ds(low, high - low), :],
-                                  sems.at[level]),
-            pltpu.make_async_copy(kept_v, v_in, v_sems.at[level]),
-        ))
-    for pair in loads:
-        start_all(pair)
     clear(v2, 32)
     clear(v1, 48)
     clear(v0, 48)
@@ -624,14 +625,14 @@
                 for r in range(2):
                     f3[r, g] = held[dx, dy, pl.ds(r, GX, stride=4), :]
                     e3[r, 1 + g] = held[dx, dy, pl.ds(2 + r, GX, stride=4), :]
-    coarse_levels(f3, e3, s3, w3, v3, s4)
+    if STOP >= 10:
+        coarse_levels(f3, e3, s3, w3, v3, s4)
     around_from_level3(v3, up3, gx, gy)
 
-    wait_all(loads[0])
     if STOP >= 13:
 
         def add2(p):
-            new = [i2[k, p - KEPT_V[2][0], 8:40, :] + up3[p - 2] for k in range(2)]
+            new = [i2[k, p, 8:40, :] + up3[p - 2] for k in range(2)]
 
             def store():
                 for k in range(2):
@@ -646,8 +647,6 @@
         half_sweep(2, 1, 3, v2, s2)
 
     def raised(level, first, last, offset, coarse_v, v_in, v):
-        base = KEPT_V[level][0]
-
         def doubled(c):
             rows = 24
             even = pair_is_even(level + 1, rows)
@@ -666,7 +665,7 @@
         loop(first, last, doubled, 2)
 
         def add(c):
-            new = [(k, 2 * c - offset + s, v_in[k, 2 * c - offset + s - base, 8:56, :] + up[c, s])
+            new = [(k, 2 * c - offset + s, v_in[k, 2 * c - offset + s, 8:56, :] + up[c, s])
                    for s in range(2) for k in range(2)]
 
             def store():
@@ -677,15 +676,13 @@
 
         loop(first, last, add, 1)
 
-    wait_all(loads[1])
     if STOP >= 14:
         raised(1, 4, 12, 4, v2, i1, v1)
-        half_sweep(1, 0, 5, v1, s1)
-        half_sweep(1, 1, 4, v1, s1)
-        half_sweep(1, 0, 3, v1, s1)
-        half_sweep(1, 1, 2, v1, s1)
-
-    wait_all(loads[2])
+        half_sweep(1, 0, 5, v1, s1, (KEPT[0], KEPT[2]))
+        half_sweep(1, 1, 4, v1, s1, (KEPT[0], KEPT[2]))
+        half_sweep(1, 0, 3, v1, s1, (KEPT[0], KEPT[2]))
+        half_sweep(1, 1, 2, v1, s1, (KEPT[0], KEPT[2]))
+
     if STOP >= 15:
         raised(0, 7, 17, 12, v1, i0, v0)
         half_sweep(0, 0, 3, v0, s0)
@@ -712,17 +709,17 @@
 
 
 def kept_shapes(level):
-    first, last, low, high = KEPT[level]
-    v_first, v_last = KEPT_V[level]
-    return (shaped(last - first, 2, 7, high - low, LANES),
-            shaped(2, v_last - v_first, EXT[level] + 16, LANES))
+    ext = EXT[level]
+    kept = shaped(ext // 2, 2, 7, ext, LANES)
+    if level == 1:
+        kept = shaped(KEPT[1] - KEPT[0], 2, 7, KEPT[3] - KEPT[2], LANES)
+    return kept, shaped(2, ext // 2, ext + 16, LANES)
 
 
 def down_scratch(level):
     ext = EXT[level]
-    vmem = [(ext // 2, 2, 7, ext, LANES), (2, ext // 2, ext + 16, LANES), (ext + 2, ext + 16, LANES),
-            (ext, ext, LANES), (ext // 2, ext, LANES), (2, 16, ext, LANES)]
-    return [pltpu.VMEM(s, F32) for s in vmem] + [pltpu.SemaphoreType.DMA((GROUPS + 1,))]
+    vmem = [(ext + 2, ext + 16, LANES), (ext, ext, LANES), (ext // 2, ext, LANES), (2, 16, ext, LANES)]
+    return [pltpu.VMEM(s, F32) for s in vmem]
 
 
 def kernel_call(body, in_spaces, out_shape, out_spaces, scratch, mib, *operands):
@@ -758,29 +755,33 @@
 def per_device(right_side, permittivity):
     both = (right_side, permittivity)
     xl, xr = exchange("gx", jnp.stack([b[24:] for b in both]), jnp.stack([b[:8] for b in both]))
-
-    def y_slab(rows):
-        middle = jnp.stack([b[:, rows] for b in both])
-        return jnp.concatenate([xl[:, :, rows], middle, xr[:, :, rows]], axis=1)
-
-    yl, yr = exchange("gy", y_slab(slice(24, 32)), y_slab(slice(0, 8)))
+    yl, yr = exchange("gy", jnp.stack([b[:, 24:] for b in both]), jnp.stack([b[:, :8] for b in both]))
+    xl, xr, yl, yr = lax.optimization_barrier((xl, xr, yl, yr))
+    corners = jnp.concatenate([xl, xr], axis=1)
+    cl, cr = exchange("gy", corners[:, :, 24:], corners[:, :, :8])
     p1, s0, v0 = kernel_call(
-        down0, "aavvvv", (shaped(16, 16, LANES),) + kept_shapes(0), "vaa",
-        down_scratch(0) + [pltpu.SemaphoreType.DMA((10,))], 24,
-        right_side, permittivity, xl, xr, yl, yr)
-
-    xl, xr = exchange("gx", p1, p1)
-    wide = jnp.concatenate([xl, p1, xr], axis=0)
-    yl, yr = exchange("gy", wide, wide)
+        down0, "aavvvvvv", (shaped(16, 16, LANES),) + kept_shapes(0), KEPT_SPEC,
+        down_scratch(0) + [pltpu.SemaphoreType.DMA((18,))], 8,
+        right_side, permittivity, xl, xr, yl, yr, cl, cr)
+
+    xl, xr = exchange("gx", p1[3:], p1[:13])
+    yl, yr = exchange("gy", p1, p1)
+    xl, xr, yl, yr = lax.optimization_barrier((xl, xr, yl, yr))
+    corners = jnp.concatenate([xl, xr], axis=0)
+    cl, cr = exchange("gy", corners, corners)
     p2, s1, v1 = kernel_call(
-        down1, "vvvvv", (shaped(16, 16, LANES),) + kept_shapes(1), "vaa", down_scratch(1), 24, p1, xl, xr, yl, yr)
+        down1, "vvvvvvv", (shaped(16, 16, LANES),) + kept_shapes(1), "vav", down_scratch(1)
+        + [pltpu.VMEM((EXT[1] // 2, 2, 7, EXT[1], LANES), F32), pltpu.SemaphoreType.DMA((GROUPS,))], 16,
+        p1, xl, xr, yl, yr, cl, cr)
 
     xl, xr = exchange("gx", p2[:8], p2[8:])
-    wide = jnp.concatenate([xl, p2, xr], axis=0)
-    yl, yr = exchange("gy", wide[:, :8], wide[:, 8:])
+    yl, yr = exchange("gy", p2[:, :8], p2[:, 8:])
+    xl, xr, yl, yr = lax.optimization_barrier((xl, xr, yl, yr))
+    corners = jnp.concatenate([xl, xr], axis=0)
+    cl, cr = exchange("gy", corners[:, :8], corners[:, 8:])
     p3, s2, v2 = kernel_call(
-        down2, "vvvvv", (shaped(GX, 4, LANES),) + kept_shapes(2), "vaa",
-        down_scratch(2) + [pltpu.VMEM((2, 4, 8, LANES), F32)], 14, p2, xl, xr, yl, yr)
+        down2, "vvvvvvv", (shaped(GX, 4, LANES),) + kept_shapes(2), KEPT_SPEC,
+        down_scratch(2) + [pltpu.VMEM((2, 4, 8, LANES), F32)], 8, p2, xl, xr, yl, yr, cl, cr)
 
     column = lax.all_to_all(p3, "gx", 0, 0, tiled=True).reshape(4 * GX, LANES)
     along_y = jnp.stack([column] + [from_offset(column, 0, d, 0) for d in (1, 2, 3)])
@@ -796,10 +797,8 @@
         (7, CHUNK, GX, LANES),
         (2, 16, 48, LANES), (2, 24, 64, LANES), (2, 24, 64, LANES), (12, 32, LANES), (17, 2, 48, LANES),
     ]
-    vmem += [(EXT[l] // 2, 2, 7, EXT[l], LANES) for l in range(3)]
-    vmem += [kept_shapes(l)[1].shape for l in range(3)]
-    scratch = [pltpu.VMEM(s, F32) for s in vmem] + [pltpu.SemaphoreType.DMA((3,))] * 2
-    return kernel_call(climb, "vvaaaaaa", (shaped(32, 32, LANES),), "v", scratch, 36, *operands)[0]
+    scratch = [pltpu.VMEM(s, F32) for s in vmem]
+    return kernel_call(climb, "vvvvvvvv", (shaped(32, 32, LANES),), "v", scratch, 14, *operands)[0]
 
 
 def solution(mesh):

time: 128 us -> 137 us (1.070)
  starting transfers between devices: 42.8 us -> 51 us
  Pallas kernels: 39.6 us -> 41.7 us
    ppermute x6 -> x9, starting transfers between devices: 21.4 us -> 30.7 us  [exchange(): lax.ppermute(to_previous, axis, backward)]
    ppermute x6 -> x9, waiting for transfers between devices: 15.1 us -> 10.7 us  [exchange(): lax.ppermute(to_next, axis, onward)]
    ppermute x6 -> x9, waiting for transfers between devices: 9.07 us -> 13.1 us  [exchange(): lax.ppermute(to_previous, axis, backward)]
    pallas_call x4, Pallas kernels: 39.6 us -> 41.7 us  [kernel_call(): pl.pallas_call(body, in_specs=specs(in_spaces), out_specs=tuple(specs(out...]
    ppermute x6 -> x9, starting transfers between devices: 7.31 us -> 6.33 us  [exchange(): lax.ppermute(to_next, axis, onward)]
  transfers between devices with their start and end apart: 19 -> 25, of which waited for: 16 -> 18; matrix products, arithmetic and copies ran while one was open for 1% -> 1% of each run, Pallas kernels for 0% -> 0%
where the time goes in v3:
time: 137 us
  starting transfers between devices  51 us (37%)
  Pallas kernels  41.7 us (30%)
  waiting for transfers between devices  31 us (23%)
  blocking collectives  10.3 us (8%)
  local copies, waits for them, and re-layouts  2.49 us (2%)
    pallas_call x4, Pallas kernels, kernel_call(): pl.pallas_call(body, in_specs=specs(in_spaces), out_specs=tuple(specs(out...  41.7 us
    ppermute x9, starting transfers between devices, exchange(): lax.ppermute(to_previous, axis, backward)  30.7 us
    ppermute x7, starting transfers between devices, from_offset(): return lax.ppermute(values, 'gy', moves)  14 us
    ppermute x9, waiting for transfers between devices, exchange(): lax.ppermute(to_previous, axis, backward)  13.1 us
    ppermute x9, waiting for transfers between devices, exchange(): lax.ppermute(to_next, axis, onward)  10.7 us
    all_to_all x1, blocking collectives, per_device(): column = lax.all_to_all(p3, 'gx', 0, 0, tiled=True).reshape(4 * GX, LANES)  10.3 us
    ppermute x7, waiting for transfers between devices, from_offset(): return lax.ppermute(values, 'gy', moves)  7.16 us
    ppermute x9, starting transfers between devices, exchange(): lax.ppermute(to_next, axis, onward)  6.33 us
  transfers between devices with their start and end apart: 25, of which 18 were waited for; matrix products, arithmetic and copies ran while one was open for 1% of the time, Pallas kernels for 0%

profile of v3, /device:TPU:1, one launch (start us, length us, event | category | flops | bytes accessed | tf_op | source)
XLA Modules:
  0.0 136.8 jit_solution(9953435694573041514)
XLA Ops:
  0.0 1.2 slice_bitcast_fusion.4
  1.3 2.5 %collective-permute-start = (f32[2,8,32,128]{3,2,1,0:T(8,128)S(1)}, f32[2,8,32,128]{3,2,1,0:T(8,128)S(1)}, u32[]{:S(2)}, u32[]{:S(2)}) collective-permute-start(f32[2,8,32,128]{3,2,1,0:T(8,128)S(1)} %pad_maximum_fusion), channel_id=1, source_target_pairs={{0,32},{32,64},{64,96},{96,128},{128,160},{160,192},{192,224},{224... | collective-permute-start | bytes 786440 | tf_op jit(solution)/shard_map/ppermute | solution.py:744
  3.8 4.0 %collective-permute-start.1 = (f32[2,8,32,128]{3,2,1,0:T(8,128)S(1)}, f32[2,8,32,128]{3,2,1,0:T(8,128)S(1)}, u32[]{:S(2)}, u32[]{:S(2)}) collective-permute-start(f32[2,8,32,128]{3,2,1,0:T(8,128)S(1)} %pad_maximum_fusion.1), channel_id=1, source_target_pairs={{32,0},{64,32},{96,64},{128,96},{160,128},{192,160},{224,192},{0,2... | collective-permute-start | bytes 786440 | tf_op jit(solution)/shard_map/ppermute | solution.py:744
  7.9 1.1 slice_bitcast_fusion
  9.0 2.2 %collective-permute-start.2 = (f32[2,32,8,128]{3,2,1,0:T(8,128)S(1)}, f32[2,32,8,128]{3,2,1,0:T(8,128)S(1)}, u32[]{:S(2)}, u32[]{:S(2)}) collective-permute-start(f32[2,32,8,128]{3,2,1,0:T(8,128)S(1)} %pad_maximum_fusion.2), channel_id=1, source_target_pairs={{0,1},{1,2},{2,3},{3,4},{4,5},{5,6},{6,7},{7,8},{8,9},{9,10},{10,1... | collective-permute-start | bytes 786440 | tf_op jit(solution)/shard_map/ppermute | solution.py:744
  11.3 0.1 collective-permute-start.3
  11.3 2.4 %collective-permute-done.xl = f32[2,8,32,128]{3,2,1,0:T(8,128)S(1)} collective-permute-done((f32[2,8,32,128]{3,2,1,0:T(8,128)S(1)}, f32[2,8,32,128]{3,2,1,0:T(8,128)S(1)}, u32[]{:S(2)}, u32[]{:S(2)}) %collective-permute-start) | collective-permute-done | bytes 262176 | tf_op jit(solution)/shard_map/ppermute | solution.py:744
  13.8 0.0 collective-permute-done.1.xr
  13.8 0.8 collective-permute-done.2.yl
  14.6 2.9 %collective-permute-done.3.yr = f32[2,32,8,128]{3,2,1,0:T(8,128)S(1)} collective-permute-done((f32[2,32,8,128]{3,2,1,0:T(8,128)S(1)}, f32[2,32,8,128]{3,2,1,0:T(8,128)S(1)}, u32[]{:S(2)}, u32[]{:S(2)}) %collective-permute-start.3) | collective-permute-done | bytes 262176 | tf_op jit(solution)/shard_map/ppermute | solution.py:744
  17.5 1.8 %collective-permute-start.5 = (f32[2,16,8,128]{3,2,1,0:T(8,128)S(1)}, f32[2,16,8,128]{3,2,1,0:T(8,128)S(1)}, u32[]{:S(2)}, u32[]{:S(2)}) collective-permute-start(f32[2,16,8,128]{3,2,1,0:T(8,128)S(1)} %get-tuple-element.47), channel_id=1, source_target_pairs={{1,0},{2,1},{3,2},{4,3},{5,4},{6,5},{7,6},{8,7},{9,8},{10,9},{11,1... | collective-permute-start | bytes 393224 | tf_op jit(solution)/shard_map/ppermute | solution.py:744
  19.3 2.6 %collective-permute-done.5.cr = f32[2,16,8,128]{3,2,1,0:T(8,128)S(1)} collective-permute-done((f32[2,16,8,128]{3,2,1,0:T(8,128)S(1)}, f32[2,16,8,128]{3,2,1,0:T(8,128)S(1)}, u32[]{:S(2)}, u32[]{:S(2)}) %collective-permute-start.5) | collective-permute-done | bytes 131104 | tf_op jit(solution)/shard_map/ppermute | solution.py:744
  22.0 3.4 %collective-permute-done.4.cl = f32[2,16,8,128]{3,2,1,0:T(8,128)S(1)} collective-permute-done((f32[2,16,8,128]{3,2,1,0:T(8,128)S(1)}, f32[2,16,8,128]{3,2,1,0:T(8,128)S(1)}, u32[]{:S(2)}, u32[]{:S(2)}) %collective-permute-start.4) | collective-permute-done | bytes 131104 | tf_op jit(solution)/shard_map/ppermute | solution.py:744
  25.3 7.6 %down0.1 = (f32[16,16,128]{2,1,0:T(8,128)S(1)}, f32[24,2,7,48,128]{4,3,2,1,0:T(8,128)S(1)}, f32[2,24,64,128]{3,2,1,0:T(8,128)S(1)}) custom-call(f32[32,32,128]{2,1,0:T(8,128)S(1)} %copy-done, f32[32,32,128]{2,1,0:T(8,128)S(1)} %copy-done.1, f32[2,8,32,128]{3,2,1,0:T(8,128)S(1)} %collective-permute-done.xl, f32[2,8,32,128]{3,2,1,0:T(8,128)S(1)} %collective-permute-done.1.xr, ...), custom_call_target="tpu_custom_call" | custom-call | tf_op jit(solution)/shard_map/down0/pallas_call | solution.py:729
  33.0 7.0 %collective-permute-start.9 = (f32[16,16,128]{2,1,0:T(8,128)S(1)}, f32[16,16,128]{2,1,0:T(8,128)S(1)}, u32[]{:S(2)}, u32[]{:S(2)}) collective-permute-start(f32[16,16,128]{2,1,0:T(8,128)S(1)} %get-tuple-element.30.own), channel_id=1, source_target_pairs={{1,0},{2,1},{3,2},{4,3},{5,4},{6,5},{7,6},{8,7},{9,8},{10,9},{11,1... | collective-permute-start | bytes 393224 | tf_op jit(solution)/shard_map/ppermute | solution.py:744
  40.0 1.8 %collective-permute-start.7 = (f32[13,16,128]{2,1,0:T(8,128)S(1)}, f32[13,16,128]{2,1,0:T(8,128)S(1)}, u32[]{:S(2)}, u32[]{:S(2)}) collective-permute-start(f32[13,16,128]{2,1,0:T(8,128)S(1)} %get-tuple-element.63), channel_id=1, source_target_pairs={{32,0},{64,32},{96,64},{128,96},{160,128},{192,160},{224,192},{0,2... | collective-permute-start | bytes 319496 | tf_op jit(solution)/shard_map/ppermute | solution.py:744
  41.7 0.0 collective-permute-start.6
  41.8 2.3 %collective-permute-done.7.xr = f32[13,16,128]{2,1,0:T(8,128)S(1)} collective-permute-done((f32[13,16,128]{2,1,0:T(8,128)S(1)}, f32[13,16,128]{2,1,0:T(8,128)S(1)}, u32[]{:S(2)}, u32[]{:S(2)}) %collective-permute-start.7) | collective-permute-done | bytes 106528 | tf_op jit(solution)/shard_map/ppermute | solution.py:744
  44.1 2.8 %collective-permute-done.6.xl = f32[13,16,128]{2,1,0:T(8,128)S(1)} collective-permute-done((f32[13,16,128]{2,1,0:T(8,128)S(1)}, f32[13,16,128]{2,1,0:T(8,128)S(1)}, u32[]{:S(2)}, u32[]{:S(2)}) %collective-permute-start.6) | collective-permute-done | bytes 106528 | tf_op jit(solution)/shard_map/ppermute | solution.py:744
  46.8 0.0 collective-permute-done.8.yl
  46.8 1.7 %collective-permute-start.11 = (f32[26,16,128]{2,1,0:T(8,128)S(1)}, f32[26,16,128]{2,1,0:T(8,128)S(1)}, u32[]{:S(2)}, u32[]{:S(2)}) collective-permute-start(f32[26,16,128]{2,1,0:T(8,128)S(1)} %constant_dynamic-update-slice_fusion.2), channel_id=1, source_target_pairs={{1,0},{2,1},{3,2},{4,3},{5,4},{6,5},{7,6},{8,7},{9,8},{10,9},{11,1... | collective-permute-start | bytes 638984 | tf_op jit(solution)/shard_map/ppermute | solution.py:744
  48.6 0.1 collective-permute-start.10
  48.7 3.5 %collective-permute-done.11.cr = f32[26,16,128]{2,1,0:T(8,128)S(1)} collective-permute-done((f32[26,16,128]{2,1,0:T(8,128)S(1)}, f32[26,16,128]{2,1,0:T(8,128)S(1)}, u32[]{:S(2)}, u32[]{:S(2)}) %collective-permute-start.11) | collective-permute-done | bytes 213024 | tf_op jit(solution)/shard_map/ppermute | solution.py:744
  52.2 0.5 collective-permute-done.10.cl
  52.7 7.4 %down1.1 = (f32[16,16,128]{2,1,0:T(8,128)S(1)}, f32[14,2,7,32,128]{4,3,2,1,0:T(8,128)S(1)}, f32[2,24,64,128]{3,2,1,0:T(8,128)S(1)}) custom-call(f32[16,16,128]{2,1,0:T(8,128)S(1)} %get-tuple-element.30.own, f32[13,16,128]{2,1,0:T(8,128)S(1)} %collective-permute-done.6.xl, f32[13,16,128]{2,1,0:T(8,128)S(1)} %collective-permute-done.7.xr, ...), custom_call_target="tpu_custom_call" | custom-call | tf_op jit(solution)/shard_map/down1/pallas_call | solution.py:729
  60.1 0.3 collective-permute-start.13
  60.4 1.5 %collective-permute-start.12 = (f32[8,16,128]{2,1,0:T(8,128)S(1)}, f32[8,16,128]{2,1,0:T(8,128)S(1)}, u32[]{:S(2)}, u32[]{:S(2)}) collective-permute-start(f32[8,16,128]{2,1,0:T(8,128)S(1)} %get-tuple-element.62), channel_id=1, source_target_pairs={{0,32},{32,64},{64,96},{96,128},{128,160},{160,192},{192,224},{224... | collective-permute-start | bytes 196616 | tf_op jit(solution)/shard_map/ppermute | solution.py:744
  61.9 8.2 %collective-permute-start.15 = (f32[16,8,128]{2,1,0:T(8,128)S(1)}, f32[16,8,128]{2,1,0:T(8,128)S(1)}, u32[]{:S(2)}, u32[]{:S(2)}) collective-permute-start(f32[16,8,128]{2,1,0:T(8,128)S(1)} %get-tuple-element.59), channel_id=1, source_target_pairs={{1,0},{2,1},{3,2},{4,3},{5,4},{6,5},{7,6},{8,7},{9,8},{10,9},{11,1... | collective-permute-start | bytes 196616 | tf_op jit(solution)/shard_map/ppermute | solution.py:744
  70.1 0.0 collective-permute-done.12.xl
  70.1 0.9 collective-permute-done.15.yr
  71.0 0.4 collective-permute-done.14.yl
  71.5 5.8 %collective-permute-start.17 = (f32[16,8,128]{2,1,0:T(8,128)S(1)}, f32[16,8,128]{2,1,0:T(8,128)S(1)}, u32[]{:S(2)}, u32[]{:S(2)}) collective-permute-start(f32[16,8,128]{2,1,0:T(8,128)S(1)} %get-tuple-element.57), channel_id=1, source_target_pairs={{1,0},{2,1},{3,2},{4,3},{5,4},{6,5},{7,6},{8,7},{9,8},{10,9},{11,1... | collective-permute-start | bytes 196616 | tf_op jit(solution)/shard_map/ppermute | solution.py:744
  77.2 0.9 collective-permute-done.17.cr
  78.1 0.4 collective-permute-done.16.cl
  78.5 4.1 %down2.1 = (f32[8,4,128]{2,1,0:T(4,128)S(1)}, f32[16,2,7,32,128]{4,3,2,1,0:T(8,128)S(1)}, f32[2,16,48,128]{3,2,1,0:T(8,128)S(1)}) custom-call(f32[16,16,128]{2,1,0:T(8,128)S(1)} %get-tuple-element.35.own, f32[8,16,128]{2,1,0:T(8,128)S(1)} %collective-permute-done.12.xl, f32[8,16,128]{2,1,0:T(8,128)S(1)} %collective-permute-done.13.xr, ...), custom_call_target="tpu_custom_call" | custom-call | tf_op jit(solution)/shard_map/down2/pallas_call | solution.py:729
  82.7 10.3 %all_to_all.5 = f32[8,4,128]{2,1,0:T(4,128)S(1)} all-to-all(f32[8,4,128]{2,1,0:T(4,128)S(1)} %get-tuple-element.40), channel_id=1, replica_groups=mesh['gx'=8,'gy'=32] {'gx'}, dimensions={0} | all-to-all | bytes 32768 | tf_op jit(solution)/shard_map/all_to_all | solution.py:786
  93.0 2.7 %collective-permute-start.18 = (f32[32,128]{1,0:T(8,128)S(1)}, f32[32,128]{1,0:T(8,128)S(1)}, u32[]{:S(2)}, u32[]{:S(2)}) collective-permute-start(f32[32,128]{1,0:T(8,128)S(1)} %bitcast.28), channel_id=1, source_target_pairs={{2,0},{3,1},{4,2},{5,3},{6,4},{7,5},{0,6},{1,7},{10,8},{11,9},{12,... | collective-permute-start | bytes 49160 | tf_op jit(solution)/shard_map/ppermute | solution.py:752
  95.7 1.4 %collective-permute-done.20 = f32[32,128]{1,0:T(8,128)S(1)} collective-permute-done((f32[32,128]{1,0:T(8,128)S(1)}, f32[32,128]{1,0:T(8,128)S(1)}, u32[]{:S(2)}, u32[]{:S(2)}) %collective-permute-start.20) | collective-permute-done | bytes 16416 | tf_op jit(solution)/shard_map/ppermute | solution.py:752
  97.1 0.0 collective-permute-done.19
  97.1 0.8 collective-permute-done.18
  97.9 0.1 collective-permute-start.22
  98.0 4.6 %collective-permute-start.21 = (f32[4,32,128]{2,1,0:T(8,128)S(1)}, f32[4,32,128]{2,1,0:T(8,128)S(1)}, u32[]{:S(2)}, u32[]{:S(2)}) collective-permute-start(f32[4,32,128]{2,1,0:T(8,128)S(1)} %get-tuple-element.66), channel_id=1, source_target_pairs={{8,0},{9,1},{10,2},{11,3},{12,4},{13,5},{14,6},{15,7},{16,8},{17,9... | collective-permute-start | bytes 196616 | tf_op jit(solution)/shard_map/ppermute | solution.py:752
  102.6 0.5 collective-permute-start.23
  103.0 2.6 %collective-permute-done.21 = f32[4,32,128]{2,1,0:T(8,128)S(1)} collective-permute-done((f32[4,32,128]{2,1,0:T(8,128)S(1)}, f32[4,32,128]{2,1,0:T(8,128)S(1)}, u32[]{:S(2)}, u32[]{:S(2)}) %collective-permute-start.21) | collective-permute-done | bytes 65568 | tf_op jit(solution)/shard_map/ppermute | solution.py:752
  105.7 1.2 collective-permute-done.23
  106.9 6.2 %collective-permute-start.24 = (f32[4,4,32,128]{3,2,1,0:T(8,128)S(1)}, f32[4,4,32,128]{3,2,1,0:T(8,128)S(1)}, u32[]{:S(2)}, u32[]{:S(2)}) collective-permute-start(f32[4,4,32,128]{3,2,1,0:T(8,128)S(1)} %pad_maximum_fusion.4.near), channel_id=1, source_target_pairs={{1,0},{0,1},{3,2},{2,3},{5,4},{4,5},{7,6},{6,7},{9,8},{8,9},{11,10... | collective-permute-start | bytes 786440 | tf_op jit(solution)/shard_map/ppermute | solution.py:752
  113.1 1.2 collective-permute-done.24.far
  114.3 22.6 %climb.1 = f32[32,32,128]{2,1,0:T(8,128)} custom-call(f32[4,4,32,128]{3,2,1,0:T(8,128)S(1)} %pad_maximum_fusion.4.near, f32[4,4,32,128]{3,2,1,0:T(8,128)S(1)} %collective-permute-done.24.far, f32[24,2,7,48,128]{4,3,2,1,0:T(8,128)S(1)} %get-tuple-element.41.s0, f32[2,24,64,128]{3,2,1,0:T(8,128)S(1)} %get-tuple-element.42.i0, ...), custom_call_target="tpu_custom_call" | custom-call | tf_op jit(solution)/shard_map/climb/pallas_call | solution.py:729
  (30 shorter events, 0.3 us)
Async XLA Ops:
  0.0 25.3 %copy-start.1 = (f32[32,32,128]{2,1,0:T(8,128)S(1)}, f32[32,32,128]{2,1,0:T(8,128)}, u32[]{:S(2)}) copy-start(f32[32,32,128]{2,1,0:T(8,128)} %e_in.1) | copy-start | bytes 1572868
  0.0 25.3 %copy-start = (f32[32,32,128]{2,1,0:T(8,128)S(1)}, f32[32,32,128]{2,1,0:T(8,128)}, u32[]{:S(2)}) copy-start(f32[32,32,128]{2,1,0:T(8,128)} %f_in.1) | copy-start | bytes 1572868
  1.3 12.5 %collective-permute-start = (f32[2,8,32,128]{3,2,1,0:T(8,128)S(1)}, f32[2,8,32,128]{3,2,1,0:T(8,128)S(1)}, u32[]{:S(2)}, u32[]{:S(2)}) collective-permute-start(f32[2,8,32,128]{3,2,1,0:T(8,128)S(1)} %pad_maximum_fusion), channel_id=1, source_target_pairs={{0,32},{32,64},{64,96},{96,128},{128,160},{160,192},{192,224},{224... | collective-permute-start | bytes 786440 | tf_op jit(solution)/shard_map/ppermute | solution.py:744
  3.8 10.0 %collective-permute-start.1 = (f32[2,8,32,128]{3,2,1,0:T(8,128)S(1)}, f32[2,8,32,128]{3,2,1,0:T(8,128)S(1)}, u32[]{:S(2)}, u32[]{:S(2)}) collective-permute-start(f32[2,8,32,128]{3,2,1,0:T(8,128)S(1)} %pad_maximum_fusion.1), channel_id=1, source_target_pairs={{32,0},{64,32},{96,64},{128,96},{160,128},{192,160},{224,192},{0,2... | collective-permute-start | bytes 786440 | tf_op jit(solution)/shard_map/ppermute | solution.py:744
  9.0 5.5 %collective-permute-start.2 = (f32[2,32,8,128]{3,2,1,0:T(8,128)S(1)}, f32[2,32,8,128]{3,2,1,0:T(8,128)S(1)}, u32[]{:S(2)}, u32[]{:S(2)}) collective-permute-start(f32[2,32,8,128]{3,2,1,0:T(8,128)S(1)} %pad_maximum_fusion.2), channel_id=1, source_target_pairs={{0,1},{1,2},{2,3},{3,4},{4,5},{5,6},{6,7},{7,8},{8,9},{9,10},{10,1... | collective-permute-start | bytes 786440 | tf_op jit(solution)/shard_map/ppermute | solution.py:744
  11.3 6.2 %collective-permute-start.3 = (f32[2,32,8,128]{3,2,1,0:T(8,128)S(1)}, f32[2,32,8,128]{3,2,1,0:T(8,128)S(1)}, u32[]{:S(2)}, u32[]{:S(2)}) collective-permute-start(f32[2,32,8,128]{3,2,1,0:T(8,128)S(1)} %pad_maximum_fusion.3), channel_id=1, source_target_pairs={{1,0},{2,1},{3,2},{4,3},{5,4},{6,5},{7,6},{8,7},{9,8},{10,9},{11,1... | collective-permute-start | bytes 786440 | tf_op jit(solution)/shard_map/ppermute | solution.py:744
  17.5 4.5 %collective-permute-start.5 = (f32[2,16,8,128]{3,2,1,0:T(8,128)S(1)}, f32[2,16,8,128]{3,2,1,0:T(8,128)S(1)}, u32[]{:S(2)}, u32[]{:S(2)}) collective-permute-start(f32[2,16,8,128]{3,2,1,0:T(8,128)S(1)} %get-tuple-element.47), channel_id=1, source_target_pairs={{1,0},{2,1},{3,2},{4,3},{5,4},{6,5},{7,6},{8,7},{9,8},{10,9},{11,1... | collective-permute-start | bytes 393224 | tf_op jit(solution)/shard_map/ppermute | solution.py:744
  19.3 6.0 %collective-permute-start.4 = (f32[2,16,8,128]{3,2,1,0:T(8,128)S(1)}, f32[2,16,8,128]{3,2,1,0:T(8,128)S(1)}, u32[]{:S(2)}, u32[]{:S(2)}) collective-permute-start(f32[2,16,8,128]{3,2,1,0:T(8,128)S(1)} %get-tuple-element.48), channel_id=1, source_target_pairs={{0,1},{1,2},{2,3},{3,4},{4,5},{5,6},{6,7},{7,8},{8,9},{9,10},{10,1... | collective-permute-start | bytes 393224 | tf_op jit(solution)/shard_map/ppermute | solution.py:744
  33.0 13.9 %collective-permute-start.9 = (f32[16,16,128]{2,1,0:T(8,128)S(1)}, f32[16,16,128]{2,1,0:T(8,128)S(1)}, u32[]{:S(2)}, u32[]{:S(2)}) collective-permute-start(f32[16,16,128]{2,1,0:T(8,128)S(1)} %get-tuple-element.30.own), channel_id=1, source_target_pairs={{1,0},{2,1},{3,2},{4,3},{5,4},{6,5},{7,6},{8,7},{9,8},{10,9},{11,1... | collective-permute-start | bytes 393224 | tf_op jit(solution)/shard_map/ppermute | solution.py:744
  39.9 6.9 %collective-permute-start.8 = (f32[16,16,128]{2,1,0:T(8,128)S(1)}, f32[16,16,128]{2,1,0:T(8,128)S(1)}, u32[]{:S(2)}, u32[]{:S(2)}) collective-permute-start(f32[16,16,128]{2,1,0:T(8,128)S(1)} %get-tuple-element.30.own), channel_id=1, source_target_pairs={{0,1},{1,2},{2,3},{3,4},{4,5},{5,6},{6,7},{7,8},{8,9},{9,10},{10,1... | collective-permute-start | bytes 393224 | tf_op jit(solution)/shard_map/ppermute | solution.py:744
  40.0 4.1 %collective-permute-start.7 = (f32[13,16,128]{2,1,0:T(8,128)S(1)}, f32[13,16,128]{2,1,0:T(8,128)S(1)}, u32[]{:S(2)}, u32[]{:S(2)}) collective-permute-start(f32[13,16,128]{2,1,0:T(8,128)S(1)} %get-tuple-element.63), channel_id=1, source_target_pairs={{32,0},{64,32},{96,64},{128,96},{160,128},{192,160},{224,192},{0,2... | collective-permute-start | bytes 319496 | tf_op jit(solution)/shard_map/ppermute | solution.py:744
  41.7 5.1 %collective-permute-start.6 = (f32[13,16,128]{2,1,0:T(8,128)S(1)}, f32[13,16,128]{2,1,0:T(8,128)S(1)}, u32[]{:S(2)}, u32[]{:S(2)}) collective-permute-start(f32[13,16,128]{2,1,0:T(8,128)S(1)} %get-tuple-element.64), channel_id=1, source_target_pairs={{0,32},{32,64},{64,96},{96,128},{128,160},{160,192},{192,224},{224... | collective-permute-start | bytes 319496 | tf_op jit(solution)/shard_map/ppermute | solution.py:744
  46.8 5.3 %collective-permute-start.11 = (f32[26,16,128]{2,1,0:T(8,128)S(1)}, f32[26,16,128]{2,1,0:T(8,128)S(1)}, u32[]{:S(2)}, u32[]{:S(2)}) collective-permute-start(f32[26,16,128]{2,1,0:T(8,128)S(1)} %constant_dynamic-update-slice_fusion.2), channel_id=1, source_target_pairs={{1,0},{2,1},{3,2},{4,3},{5,4},{6,5},{7,6},{8,7},{9,8},{10,9},{11,1... | collective-permute-start | bytes 638984 | tf_op jit(solution)/shard_map/ppermute | solution.py:744
  48.6 4.2 %collective-permute-start.10 = (f32[26,16,128]{2,1,0:T(8,128)S(1)}, f32[26,16,128]{2,1,0:T(8,128)S(1)}, u32[]{:S(2)}, u32[]{:S(2)}) collective-permute-start(f32[26,16,128]{2,1,0:T(8,128)S(1)} %constant_dynamic-update-slice_fusion.2), channel_id=1, source_target_pairs={{0,1},{1,2},{2,3},{3,4},{4,5},{5,6},{6,7},{7,8},{8,9},{9,10},{10,1... | collective-permute-start | bytes 638984 | tf_op jit(solution)/shard_map/ppermute | solution.py:744
  60.1 9.9 %collective-permute-start.13 = (f32[8,16,128]{2,1,0:T(8,128)S(1)}, f32[8,16,128]{2,1,0:T(8,128)S(1)}, u32[]{:S(2)}, u32[]{:S(2)}) collective-permute-start(f32[8,16,128]{2,1,0:T(8,128)S(1)} %get-tuple-element.61), channel_id=1, source_target_pairs={{32,0},{64,32},{96,64},{128,96},{160,128},{192,160},{224,192},{0,2... | collective-permute-start | bytes 196616 | tf_op jit(solution)/shard_map/ppermute | solution.py:744
  60.4 9.7 %collective-permute-start.12 = (f32[8,16,128]{2,1,0:T(8,128)S(1)}, f32[8,16,128]{2,1,0:T(8,128)S(1)}, u32[]{:S(2)}, u32[]{:S(2)}) collective-permute-start(f32[8,16,128]{2,1,0:T(8,128)S(1)} %get-tuple-element.62), channel_id=1, source_target_pairs={{0,32},{32,64},{64,96},{96,128},{128,160},{160,192},{192,224},{224... | collective-permute-start | bytes 196616 | tf_op jit(solution)/shard_map/ppermute | solution.py:744
  61.9 9.1 %collective-permute-start.15 = (f32[16,8,128]{2,1,0:T(8,128)S(1)}, f32[16,8,128]{2,1,0:T(8,128)S(1)}, u32[]{:S(2)}, u32[]{:S(2)}) collective-permute-start(f32[16,8,128]{2,1,0:T(8,128)S(1)} %get-tuple-element.59), channel_id=1, source_target_pairs={{1,0},{2,1},{3,2},{4,3},{5,4},{6,5},{7,6},{8,7},{9,8},{10,9},{11,1... | collective-permute-start | bytes 196616 | tf_op jit(solution)/shard_map/ppermute | solution.py:744
  70.1 1.3 collective-permute-start.14
  71.5 6.7 %collective-permute-start.17 = (f32[16,8,128]{2,1,0:T(8,128)S(1)}, f32[16,8,128]{2,1,0:T(8,128)S(1)}, u32[]{:S(2)}, u32[]{:S(2)}) collective-permute-start(f32[16,8,128]{2,1,0:T(8,128)S(1)} %get-tuple-element.57), channel_id=1, source_target_pairs={{1,0},{2,1},{3,2},{4,3},{5,4},{6,5},{7,6},{8,7},{9,8},{10,9},{11,1... | collective-permute-start | bytes 196616 | tf_op jit(solution)/shard_map/ppermute | solution.py:744
  77.2 1.3 collective-permute-start.16
  93.0 4.1 %collective-permute-start.20 = (f32[32,128]{1,0:T(8,128)S(1)}, f32[32,128]{1,0:T(8,128)S(1)}, u32[]{:S(2)}, u32[]{:S(2)}) collective-permute-start(f32[32,128]{1,0:T(8,128)S(1)} %bitcast.26), channel_id=1, source_target_pairs={{6,0},{7,1},{0,2},{1,3},{2,4},{3,5},{4,6},{5,7},{14,8},{15,9},{8,1... | collective-permute-start | bytes 49160 | tf_op jit(solution)/shard_map/ppermute | solution.py:752
  93.0 4.1 %collective-permute-start.19 = (f32[32,128]{1,0:T(8,128)S(1)}, f32[32,128]{1,0:T(8,128)S(1)}, u32[]{:S(2)}, u32[]{:S(2)}) collective-permute-start(f32[32,128]{1,0:T(8,128)S(1)} %bitcast.27), channel_id=1, source_target_pairs={{4,0},{5,1},{6,2},{7,3},{0,4},{1,5},{2,6},{3,7},{12,8},{13,9},{14,... | collective-permute-start | bytes 49160 | tf_op jit(solution)/shard_map/ppermute | solution.py:752
  93.0 4.8 %collective-permute-start.18 = (f32[32,128]{1,0:T(8,128)S(1)}, f32[32,128]{1,0:T(8,128)S(1)}, u32[]{:S(2)}, u32[]{:S(2)}) collective-permute-start(f32[32,128]{1,0:T(8,128)S(1)} %bitcast.28), channel_id=1, source_target_pairs={{2,0},{3,1},{4,2},{5,3},{6,4},{7,5},{0,6},{1,7},{10,8},{11,9},{12,... | collective-permute-start | bytes 49160 | tf_op jit(solution)/shard_map/ppermute | solution.py:752
  97.9 5.2 %collective-permute-start.22 = (f32[4,32,128]{2,1,0:T(8,128)S(1)}, f32[4,32,128]{2,1,0:T(8,128)S(1)}, u32[]{:S(2)}, u32[]{:S(2)}) collective-permute-start(f32[4,32,128]{2,1,0:T(8,128)S(1)} %get-tuple-element.66), channel_id=1, source_target_pairs={{16,0},{17,1},{18,2},{19,3},{20,4},{21,5},{22,6},{23,7},{24,8},{25... | collective-permute-start | bytes 196616 | tf_op jit(solution)/shard_map/ppermute | solution.py:752
  98.0 7.7 %collective-permute-start.21 = (f32[4,32,128]{2,1,0:T(8,128)S(1)}, f32[4,32,128]{2,1,0:T(8,128)S(1)}, u32[]{:S(2)}, u32[]{:S(2)}) collective-permute-start(f32[4,32,128]{2,1,0:T(8,128)S(1)} %get-tuple-element.66), channel_id=1, source_target_pairs={{8,0},{9,1},{10,2},{11,3},{12,4},{13,5},{14,6},{15,7},{16,8},{17,9... | collective-permute-start | bytes 196616 | tf_op jit(solution)/shard_map/ppermute | solution.py:752
  102.6 4.3 %collective-permute-start.23 = (f32[4,32,128]{2,1,0:T(8,128)S(1)}, f32[4,32,128]{2,1,0:T(8,128)S(1)}, u32[]{:S(2)}, u32[]{:S(2)}) collective-permute-start(f32[4,32,128]{2,1,0:T(8,128)S(1)} %get-tuple-element.66), channel_id=1, source_target_pairs={{24,0},{25,1},{26,2},{27,3},{28,4},{29,5},{30,6},{31,7},{0,8},{1,9... | collective-permute-start | bytes 196616 | tf_op jit(solution)/shard_map/ppermute | solution.py:752
  106.9 7.4 %collective-permute-start.24 = (f32[4,4,32,128]{3,2,1,0:T(8,128)S(1)}, f32[4,4,32,128]{3,2,1,0:T(8,128)S(1)}, u32[]{:S(2)}, u32[]{:S(2)}) collective-permute-start(f32[4,4,32,128]{3,2,1,0:T(8,128)S(1)} %pad_maximum_fusion.4.near), channel_id=1, source_target_pairs={{1,0},{0,1},{3,2},{2,3},{5,4},{4,5},{7,6},{6,7},{9,8},{8,9},{11,10... | collective-permute-start | bytes 786440 | tf_op jit(solution)/shard_map/ppermute | solution.py:752

commit v4 on v3

--- a/solution.py
+++ b/solution.py
@@ -14,7 +14,6 @@
 GX = 8
 GY = 32
 CHUNK = 8
-C3 = 1
 KEPT = (5, 19, 8, 40)
 GROUPS = 4
 
@@ -338,17 +337,15 @@
     loop(0, count, body, UNROLL["put"])
 
 
-def down1(own, xl, xr, yl, yr, cl, cr, out, kept, v, e, f, total, tmp, state, sems):
+def down1(own, xl, xr, yl, yr, out, kept, v, e, f, total, tmp, state, sems):
     gx, gy = lax.axis_index("gx"), lax.axis_index("gy")
     fill_rim(e, 48)
     clear(v, 48)
     put_split(xl, 0, 13, 3, 16, e, f)
     put_split(own, 0, 16, 16, 16, e, f)
     put_split(xr, 0, 13, 32, 16, e, f)
-    for side, corner, y in ((yl, cl, 0), (yr, cr, 32)):
-        put_split(corner, 0, 13, 3, y, e, f)
-        put_split(side, 0, 16, 16, y, e, f)
-        put_split(corner, 13, 13, 32, y, e, f)
+    put_split(yl, 0, 42, 3, 0, e, f)
+    put_split(yr, 0, 42, 3, 32, e, f)
 
     def put(q, fc, ec):
         out[q] = interleave(fc, ec)
@@ -372,17 +369,15 @@
     wait_all([copy for _, copy in copies])
 
 
-def down2(own, xl, xr, yl, yr, cl, cr, out, state, v, e, f, total, tmp, coarse):
+def down2(own, xl, xr, yl, yr, out, state, v, e, f, total, tmp, coarse):
     gx, gy = lax.axis_index("gx"), lax.axis_index("gy")
     fill_rim(e, 32)
     clear(v, 32)
     put_split(xl, 0, 8, 0, 8, e, f)
     put_split(own, 0, 16, 8, 8, e, f)
     put_split(xr, 0, 8, 24, 8, e, f)
-    for side, corner, y in ((yl, cl, 0), (yr, cr, 24)):
-        put_split(corner, 0, 8, 0, y, e, f)
-        put_split(side, 0, 16, 8, y, e, f)
-        put_split(corner, 8, 8, 24, y, e, f)
+    put_split(yl, 0, 32, 0, 0, e, f)
+    put_split(yr, 0, 32, 0, 24, e, f)
 
     def put(q, fc, ec):
         coarse[0, q, 0:4, :] = fc
@@ -452,82 +447,78 @@
 
 
 def coarse_levels(f3, e3, s3, w3, v3, s4):
-    lane = iota((C3, GX, LANES), 2)
+    tile = (GX, LANES)
+    lane = iota(tile, 1)
     even3 = ((lane ^ (lane >> 3)) & 1) == 0
     z_last3 = (lane >> 3) == 15
-    chunks = range(0, GY, C3)
+    zero = jnp.zeros(tile, F32)
+    everywhere = range(GY)
 
     def face(scale, a, b):
         return (2.0 * scale) * a * b / (a + b)
 
-    zero = jnp.zeros((GX, LANES), F32)
-    for k in range(2):
-        e3[k, 0] = lane_roll(e3[k, 1], 3)
-        e3[k, 1 + GY] = lane_roll(e3[k, GY], -3)
-        v3[k, 0] = zero
-        v3[k, 1 + GY] = zero
-    scale = 0.25**3
-    e4 = []
-    for g in chunks:
-        here = pl.ds(1 + g, C3)
-        both = (e3[0, here], e3[1, here])
-        inner = face(scale, both[0], both[1])
-        outer = (face(scale, both[0], pair_before(both[1], both[0])),
-                 face(scale, both[1], pair_after(both[0], both[1])))
-        yp, ym, zp, zm, f = [], [], [], [], []
+    e = [[e3[r, g] for g in everywhere] for r in range(2)]
+    after = [e[r][1:] + [lane_roll(e[r][-1], -3)] for r in range(2)]
+    before = [[lane_roll(e[r][0], 3)] + e[r][:-1] for r in range(2)]
+    red, e4 = [], []
+    for g in everywhere:
+        both = (e[0][g], e[1][g])
+        inner, outer0, outer1 = faces((
+            both, (both[0], pair_before(both[1], both[0])), (both[1], pair_after(both[0], both[1]))))
+        yp, ym, zp, zm = [], [], [], []
         for r in range(2):
             own = both[r]
-            yp.append(face(scale, own, y_after(3, own, e3[r, pl.ds(2 + g, C3)])))
-            ym.append(face(scale, own, y_before(3, own, e3[r, pl.ds(g, C3)])))
-            z = jnp.where(z_last3, 0.0, face(scale, own, lane_roll(own, -8)))
+            up, down, z = faces((
+                (own, y_after(3, own, after[r][g])), (own, y_before(3, own, before[r][g])), (own, lane_roll(own, -8))))
+            z = jnp.where(z_last3, 0.0, z)
+            yp.append(up)
+            ym.append(down)
             zp.append(z)
             zm.append(lane_roll(z, 8))
-            f.append(f3[r, pl.ds(g, C3)])
+        f = (f3[0, g], f3[1, g])
+        sides, sums = [], []
         for k in range(2):
-            a, b = k, 1 - k
-            parts = [jnp.where(even3, t[a], t[b]) for t in (outer, yp, ym, zp, zm)]
-            weight_sum = inner
-            for t in parts:
-                weight_sum = weight_sum + t
-            inverse = 1.0 / weight_sum
-            source = jnp.where(even3, f[a], f[b]) * inverse
-            s3[k, 0, pl.ds(g, C3)] = source
-            s3[k, 1, pl.ds(g, C3)] = inner * inverse
-            for i in range(5):
-                s3[k, 2 + i, pl.ds(g, C3)] = parts[i] * inverse
+            side = [inner] + [jnp.where(even3, t[k], t[1 - k]) for t in ((outer0, outer1), yp, ym, zp, zm)]
+            sides.append(side)
+            sums.append((side[0] + side[1]) + (side[2] + side[3]) + (side[4] + side[5]))
+        inverse = inverses(*sums)
+        for k in range(2):
+            source = jnp.where(even3, f[k], f[1 - k]) * (inverse[k] * (0.5 * 4.0**3))
+            s3[k, 0, g] = source
+            for i in range(6):
+                s3[k, 1 + i, g] = sides[k][i] * inverse[k]
             if k == 0:
-                w3[pl.ds(g, C3)] = weight_sum
-                v3[0, here] = source
+                w3[g] = sums[0]
+                red.append(source)
         t = both[0] + both[1]
         t = t + flip(t, 1)
         e4.append((t + flip(t, 8)) * 0.125)
 
-    def update3(k, g):
-        o = 1 - k
-        own = v3[o, pl.ds(1 + g, C3)]
-        before, after = pair_before(own, 0.0), pair_after(own, 0.0)
-        outer = jnp.where(even3, before, after) if k == 0 else jnp.where(even3, after, before)
-        sides = (own, outer, y_after(3, own, v3[o, pl.ds(2 + g, C3)]),
-                 y_before(3, own, v3[o, pl.ds(g, C3)]), lane_roll(own, -8), lane_roll(own, 8))
-        part = [s3[k, 1 + i, pl.ds(g, C3)] * sides[i] for i in range(6)]
-        return ((s3[k, 0, pl.ds(g, C3)] + part[0]) + (part[1] + part[2])) + ((part[3] + part[4]) + part[5])
-
-    def sweep3(k):
-        for g in chunks:
-            v3[k, pl.ds(1 + g, C3)] = update3(k, g)
-
-    sweep3(1)
-    sweep3(0)
-    sweep3(1)
+    def update3(k, other, g):
+        own = other[g]
+        following = other[g + 1] if g + 1 < GY else zero
+        preceding = other[g - 1] if g else zero
+        low, high = pair_before(own, 0.0), pair_after(own, 0.0)
+        outer = jnp.where(even3, low, high) if k == 0 else jnp.where(even3, high, low)
+        sides = (own, outer, y_after(3, own, following), y_before(3, own, preceding),
+                 lane_roll(own, -8), lane_roll(own, 8))
+        part = [s3[k, 1 + i, g] * sides[i] for i in range(6)]
+        return ((s3[k, 0, g] + part[0]) + (part[1] + part[2])) + ((part[3] + part[4]) + part[5])
+
+    def sweep3(k, other):
+        return [update3(k, other, g) for g in everywhere]
+
+    black = sweep3(1, red)
+    red = sweep3(0, black)
+    black = sweep3(1, red)
     f4 = []
-    for g in chunks:
-        t = (update3(0, g) - v3[0, pl.ds(1 + g, C3)]) * w3[pl.ds(g, C3)]
+    for g in everywhere:
+        t = (update3(0, black, g) - red[g]) * w3[g]
         t = t + flip(t, 1)
-        f4.append((t + flip(t, 8)) * 0.125)
+        f4.append((t + flip(t, 8)) * (0.25 * 0.25**3))
 
     def regroup(parts):
-        tiles = [part[i] for part in parts for i in range(C3)]
-        return [tiles_from_slots(tiles[b::CHUNK]) for b in range(CHUNK)]
+        return [tiles_from_slots(parts[b::CHUNK]) for b in range(CHUNK)]
 
     e4, f4 = regroup(e4), regroup(f4)
     tile = (GX, LANES)
@@ -577,15 +568,17 @@
             u = jnp.where(slot == a, v[b], 0.0)
             u = u + flip(u, 1)
             u = u + flip(u, 8)
-            g = 1 + CHUNK * a + b
-            v3[0, g] = v3[0, g] + u
-            v3[1, g] = v3[1, g] + u
-    if STOP < 12:
-        return
-    sweep3(0)
-    sweep3(1)
-    sweep3(0)
-    sweep3(1)
+            g = CHUNK * a + b
+            red[g] = red[g] + u
+            black[g] = black[g] + u
+    for _ in range(2):
+        red = sweep3(0, black)
+        black = sweep3(1, red)
+    for k, values in enumerate((red, black)):
+        v3[k, 0] = zero
+        v3[k, 1 + GY] = zero
+        for g in everywhere:
+            v3[k, 1 + g] = values[g]
 
 
 def around_from_level3(v3, up, gx, gy):
@@ -624,7 +617,7 @@
                 g = (((gy // 8 + dx) & 3) * 4 + ((gy // 2 + dy) & 3)) * 2 + (gy & 1 if c == 0 else 1 - (gy & 1))
                 for r in range(2):
                     f3[r, g] = held[dx, dy, pl.ds(r, GX, stride=4), :]
-                    e3[r, 1 + g] = held[dx, dy, pl.ds(2 + r, GX, stride=4), :]
+                    e3[r, g] = held[dx, dy, pl.ds(2 + r, GX, stride=4), :]
     if STOP >= 10:
         coarse_levels(f3, e3, s3, w3, v3, s4)
     around_from_level3(v3, up3, gx, gy)
@@ -756,7 +749,6 @@
     both = (right_side, permittivity)
     xl, xr = exchange("gx", jnp.stack([b[24:] for b in both]), jnp.stack([b[:8] for b in both]))
     yl, yr = exchange("gy", jnp.stack([b[:, 24:] for b in both]), jnp.stack([b[:, :8] for b in both]))
-    xl, xr, yl, yr = lax.optimization_barrier((xl, xr, yl, yr))
     corners = jnp.concatenate([xl, xr], axis=1)
     cl, cr = exchange("gy", corners[:, :, 24:], corners[:, :, :8])
     p1, s0, v0 = kernel_call(
@@ -765,23 +757,19 @@
         right_side, permittivity, xl, xr, yl, yr, cl, cr)
 
     xl, xr = exchange("gx", p1[3:], p1[:13])
-    yl, yr = exchange("gy", p1, p1)
-    xl, xr, yl, yr = lax.optimization_barrier((xl, xr, yl, yr))
-    corners = jnp.concatenate([xl, xr], axis=0)
-    cl, cr = exchange("gy", corners, corners)
+    wide = jnp.concatenate([xl, p1, xr], axis=0)
+    yl, yr = exchange("gy", wide, wide)
     p2, s1, v1 = kernel_call(
-        down1, "vvvvvvv", (shaped(16, 16, LANES),) + kept_shapes(1), "vav", down_scratch(1)
+        down1, "vvvvv", (shaped(16, 16, LANES),) + kept_shapes(1), "vav", down_scratch(1)
         + [pltpu.VMEM((EXT[1] // 2, 2, 7, EXT[1], LANES), F32), pltpu.SemaphoreType.DMA((GROUPS,))], 16,
-        p1, xl, xr, yl, yr, cl, cr)
+        p1, xl, xr, yl, yr)
 
     xl, xr = exchange("gx", p2[:8], p2[8:])
-    yl, yr = exchange("gy", p2[:, :8], p2[:, 8:])
-    xl, xr, yl, yr = lax.optimization_barrier((xl, xr, yl, yr))
-    corners = jnp.concatenate([xl, xr], axis=0)
-    cl, cr = exchange("gy", corners[:, :8], corners[:, 8:])
+    wide = jnp.concatenate([xl, p2, xr], axis=0)
+    yl, yr = exchange("gy", wide[:, :8], wide[:, 8:])
     p3, s2, v2 = kernel_call(
-        down2, "vvvvvvv", (shaped(GX, 4, LANES),) + kept_shapes(2), KEPT_SPEC,
-        down_scratch(2) + [pltpu.VMEM((2, 4, 8, LANES), F32)], 8, p2, xl, xr, yl, yr, cl, cr)
+        down2, "vvvvv", (shaped(GX, 4, LANES),) + kept_shapes(2), KEPT_SPEC,
+        down_scratch(2) + [pltpu.VMEM((2, 4, 8, LANES), F32)], 8, p2, xl, xr, yl, yr)
 
     column = lax.all_to_all(p3, "gx", 0, 0, tiled=True).reshape(4 * GX, LANES)
     along_y = jnp.stack([column] + [from_offset(column, 0, d, 0) for d in (1, 2, 3)])

time: 137 us -> 129 us (0.942)
  waiting for transfers between devices: 31 us -> 23.4 us
  starting transfers between devices: 51 us -> 46.8 us
  Pallas kernels: 41.7 us -> 44.5 us
    ppermute x9 -> x7, waiting for transfers between devices: 13.1 us -> 5.19 us  [exchange(): lax.ppermute(to_previous, axis, backward)]
    ppermute x9 -> x7, starting transfers between devices: 30.7 us -> 25.2 us  [exchange(): lax.ppermute(to_previous, axis, backward)]
    pallas_call x4, Pallas kernels: 41.7 us -> 44.5 us  [kernel_call(): pl.pallas_call(body, in_specs=specs(in_spaces), out_specs=tuple(specs(out...]
    ppermute x9 -> x7, starting transfers between devices: 6.33 us -> 7.52 us  [exchange(): lax.ppermute(to_next, axis, onward)]
    ppermute x9 -> x7, waiting for transfers between devices: 10.7 us -> 11.1 us  [exchange(): lax.ppermute(to_next, axis, onward)]
  transfers between devices with their start and end apart: 25 -> 21, of which waited for: 18 -> 17; matrix products, arithmetic and copies ran while one was open for 1% -> 1% of each run, Pallas kernels for 0% -> 0%
where the time goes in v4:
time: 129 us
  starting transfers between devices  46.8 us (36%)
  Pallas kernels  44.5 us (34%)
  waiting for transfers between devices  23.4 us (18%)
  blocking collectives  11.4 us (9%)
  local copies, waits for them, and re-layouts  2.51 us (2%)
    pallas_call x4, Pallas kernels, kernel_call(): pl.pallas_call(body, in_specs=specs(in_spaces), out_specs=tuple(specs(out...  44.5 us
    ppermute x7, starting transfers between devices, exchange(): lax.ppermute(to_previous, axis, backward)  25.2 us
    ppermute x7, starting transfers between devices, from_offset(): return lax.ppermute(values, 'gy', moves)  14.1 us
    all_to_all x1, blocking collectives, per_device(): column = lax.all_to_all(p3, 'gx', 0, 0, tiled=True).reshape(4 * GX, LANES)  11.4 us
    ppermute x7, waiting for transfers between devices, exchange(): lax.ppermute(to_next, axis, onward)  11.1 us
    ppermute x7, starting transfers between devices, exchange(): lax.ppermute(to_next, axis, onward)  7.52 us
    ppermute x7, waiting for transfers between devices, from_offset(): return lax.ppermute(values, 'gy', moves)  7.16 us
    ppermute x7, waiting for transfers between devices, exchange(): lax.ppermute(to_previous, axis, backward)  5.19 us
  transfers between devices with their start and end apart: 21, of which 17 were waited for; matrix products, arithmetic and copies ran while one was open for 1% of the time, Pallas kernels for 0%

profile of v4, /device:TPU:1, one launch (start us, length us, event | category | flops | bytes accessed | tf_op | source)
XLA Modules:
  0.0 128.9 jit_solution(1347130366879934668)
XLA Ops:
  0.0 1.2 slice_bitcast_fusion.4
  1.3 2.5 %collective-permute-start = (f32[2,8,32,128]{3,2,1,0:T(8,128)S(1)}, f32[2,8,32,128]{3,2,1,0:T(8,128)S(1)}, u32[]{:S(2)}, u32[]{:S(2)}) collective-permute-start(f32[2,8,32,128]{3,2,1,0:T(8,128)S(1)} %pad_maximum_fusion), channel_id=1, source_target_pairs={{0,32},{32,64},{64,96},{96,128},{128,160},{160,192},{192,224},{224... | collective-permute-start | bytes 786440 | tf_op jit(solution)/shard_map/ppermute | solution.py:737
  3.8 4.0 %collective-permute-start.1 = (f32[2,8,32,128]{3,2,1,0:T(8,128)S(1)}, f32[2,8,32,128]{3,2,1,0:T(8,128)S(1)}, u32[]{:S(2)}, u32[]{:S(2)}) collective-permute-start(f32[2,8,32,128]{3,2,1,0:T(8,128)S(1)} %pad_maximum_fusion.1), channel_id=1, source_target_pairs={{32,0},{64,32},{96,64},{128,96},{160,128},{192,160},{224,192},{0,2... | collective-permute-start | bytes 786440 | tf_op jit(solution)/shard_map/ppermute | solution.py:737
  7.9 1.1 slice_bitcast_fusion
  9.0 2.2 %collective-permute-start.2 = (f32[2,32,8,128]{3,2,1,0:T(8,128)S(1)}, f32[2,32,8,128]{3,2,1,0:T(8,128)S(1)}, u32[]{:S(2)}, u32[]{:S(2)}) collective-permute-start(f32[2,32,8,128]{3,2,1,0:T(8,128)S(1)} %pad_maximum_fusion.2), channel_id=1, source_target_pairs={{0,1},{1,2},{2,3},{3,4},{4,5},{5,6},{6,7},{7,8},{8,9},{9,10},{10,1... | collective-permute-start | bytes 786440 | tf_op jit(solution)/shard_map/ppermute | solution.py:737
  11.3 0.1 collective-permute-start.3
  11.3 2.4 %collective-permute-done.xl = f32[2,8,32,128]{3,2,1,0:T(8,128)S(1)} collective-permute-done((f32[2,8,32,128]{3,2,1,0:T(8,128)S(1)}, f32[2,8,32,128]{3,2,1,0:T(8,128)S(1)}, u32[]{:S(2)}, u32[]{:S(2)}) %collective-permute-start) | collective-permute-done | bytes 262176 | tf_op jit(solution)/shard_map/ppermute | solution.py:737
  13.8 0.0 collective-permute-done.1.xr
  13.9 1.5 %collective-permute-start.5 = (f32[2,16,8,128]{3,2,1,0:T(8,128)S(1)}, f32[2,16,8,128]{3,2,1,0:T(8,128)S(1)}, u32[]{:S(2)}, u32[]{:S(2)}) collective-permute-start(f32[2,16,8,128]{3,2,1,0:T(8,128)S(1)} %get-tuple-element.23), channel_id=1, source_target_pairs={{1,0},{2,1},{3,2},{4,3},{5,4},{6,5},{7,6},{8,7},{9,8},{10,9},{11,1... | collective-permute-start | bytes 393224 | tf_op jit(solution)/shard_map/ppermute | solution.py:737
  15.4 1.0 collective-permute-start.4
  16.4 0.0 collective-permute-done.2.yl
  16.4 1.0 collective-permute-done.3.yr
  17.4 1.6 %collective-permute-done.5.cr = f32[2,16,8,128]{3,2,1,0:T(8,128)S(1)} collective-permute-done((f32[2,16,8,128]{3,2,1,0:T(8,128)S(1)}, f32[2,16,8,128]{3,2,1,0:T(8,128)S(1)}, u32[]{:S(2)}, u32[]{:S(2)}) %collective-permute-start.5) | collective-permute-done | bytes 131104 | tf_op jit(solution)/shard_map/ppermute | solution.py:737
  19.0 1.1 collective-permute-done.4.cl
  20.1 7.6 %down0.1 = (f32[16,16,128]{2,1,0:T(8,128)S(1)}, f32[24,2,7,48,128]{4,3,2,1,0:T(8,128)S(1)}, f32[2,24,64,128]{3,2,1,0:T(8,128)S(1)}) custom-call(f32[32,32,128]{2,1,0:T(8,128)S(1)} %copy-done, f32[32,32,128]{2,1,0:T(8,128)S(1)} %copy-done.1, f32[2,8,32,128]{3,2,1,0:T(8,128)S(1)} %collective-permute-done.xl, f32[2,8,32,128]{3,2,1,0:T(8,128)S(1)} %collective-permute-done.1.xr, ...), custom_call_target="tpu_custom_call" | custom-call | tf_op jit(solution)/shard_map/down0/pallas_call | solution.py:722
  27.7 0.1 collective-permute-start.6
  27.8 2.7 %collective-permute-start.7 = (f32[13,16,128]{2,1,0:T(8,128)S(1)}, f32[13,16,128]{2,1,0:T(8,128)S(1)}, u32[]{:S(2)}, u32[]{:S(2)}) collective-permute-start(f32[13,16,128]{2,1,0:T(8,128)S(1)} %get-tuple-element.37), channel_id=1, source_target_pairs={{32,0},{64,32},{96,64},{128,96},{160,128},{192,160},{224,192},{0,2... | collective-permute-start | bytes 319496 | tf_op jit(solution)/shard_map/ppermute | solution.py:737
  30.5 2.1 %collective-permute-done.6.xl = f32[13,16,128]{2,1,0:T(8,128)S(1)} collective-permute-done((f32[13,16,128]{2,1,0:T(8,128)S(1)}, f32[13,16,128]{2,1,0:T(8,128)S(1)}, u32[]{:S(2)}, u32[]{:S(2)}) %collective-permute-start.6) | collective-permute-done | bytes 106528 | tf_op jit(solution)/shard_map/ppermute | solution.py:737
  32.6 0.0 collective-permute-done.7.xr
  32.6 8.1 %collective-permute-start.9 = (f32[42,16,128]{2,1,0:T(8,128)S(1)}, f32[42,16,128]{2,1,0:T(8,128)S(1)}, u32[]{:S(2)}, u32[]{:S(2)}) collective-permute-start(f32[42,16,128]{2,1,0:T(8,128)S(1)} %constant_dynamic-update-slice_fusion.2), channel_id=1, source_target_pairs={{1,0},{2,1},{3,2},{4,3},{5,4},{6,5},{7,6},{8,7},{9,8},{10,9},{11,1... | collective-permute-start | bytes 1032200 | tf_op jit(solution)/shard_map/ppermute | solution.py:737
  40.8 0.0 collective-permute-start.8
  40.8 1.3 collective-permute-done.9.yr
  42.1 2.9 %collective-permute-done.8.yl = f32[42,16,128]{2,1,0:T(8,128)S(1)} collective-permute-done((f32[42,16,128]{2,1,0:T(8,128)S(1)}, f32[42,16,128]{2,1,0:T(8,128)S(1)}, u32[]{:S(2)}, u32[]{:S(2)}) %collective-permute-start.8) | collective-permute-done | bytes 344096 | tf_op jit(solution)/shard_map/ppermute | solution.py:737
  45.0 7.8 %down1.1 = (f32[16,16,128]{2,1,0:T(8,128)S(1)}, f32[14,2,7,32,128]{4,3,2,1,0:T(8,128)S(1)}, f32[2,24,64,128]{3,2,1,0:T(8,128)S(1)}) custom-call(f32[16,16,128]{2,1,0:T(8,128)S(1)} %get-tuple-element.14.own, f32[13,16,128]{2,1,0:T(8,128)S(1)} %collective-permute-done.6.xl, f32[13,16,128]{2,1,0:T(8,128)S(1)} %collective-permute-done.7.xr, ...), custom_call_target="tpu_custom_call" | custom-call | tf_op jit(solution)/shard_map/down1/pallas_call | solution.py:722
  52.7 1.6 %collective-permute-start.10 = (f32[8,16,128]{2,1,0:T(8,128)S(1)}, f32[8,16,128]{2,1,0:T(8,128)S(1)}, u32[]{:S(2)}, u32[]{:S(2)}) collective-permute-start(f32[8,16,128]{2,1,0:T(8,128)S(1)} %get-tuple-element.36), channel_id=1, source_target_pairs={{0,32},{32,64},{64,96},{96,128},{128,160},{160,192},{192,224},{224... | collective-permute-start | bytes 196616 | tf_op jit(solution)/shard_map/ppermute | solution.py:737
  54.4 1.4 %collective-permute-start.11 = (f32[8,16,128]{2,1,0:T(8,128)S(1)}, f32[8,16,128]{2,1,0:T(8,128)S(1)}, u32[]{:S(2)}, u32[]{:S(2)}) collective-permute-start(f32[8,16,128]{2,1,0:T(8,128)S(1)} %get-tuple-element.35), channel_id=1, source_target_pairs={{32,0},{64,32},{96,64},{128,96},{160,128},{192,160},{224,192},{0,2... | collective-permute-start | bytes 196616 | tf_op jit(solution)/shard_map/ppermute | solution.py:737
  55.8 1.6 %collective-permute-done.10.xl = f32[8,16,128]{2,1,0:T(8,128)S(1)} collective-permute-done((f32[8,16,128]{2,1,0:T(8,128)S(1)}, f32[8,16,128]{2,1,0:T(8,128)S(1)}, u32[]{:S(2)}, u32[]{:S(2)}) %collective-permute-start.10) | collective-permute-done | bytes 65568 | tf_op jit(solution)/shard_map/ppermute | solution.py:737
  57.4 0.4 collective-permute-done.11.xr
  57.8 7.3 %collective-permute-start.13 = (f32[32,8,128]{2,1,0:T(8,128)S(1)}, f32[32,8,128]{2,1,0:T(8,128)S(1)}, u32[]{:S(2)}, u32[]{:S(2)}) collective-permute-start(f32[32,8,128]{2,1,0:T(8,128)S(1)} %get-tuple-element.33), channel_id=1, source_target_pairs={{1,0},{2,1},{3,2},{4,3},{5,4},{6,5},{7,6},{8,7},{9,8},{10,9},{11,1... | collective-permute-start | bytes 393224 | tf_op jit(solution)/shard_map/ppermute | solution.py:737
  65.1 0.0 collective-permute-start.12
  65.1 1.0 collective-permute-done.13.yr
  66.1 1.0 collective-permute-done.12.yl
  67.1 4.4 %down2.1 = (f32[8,4,128]{2,1,0:T(4,128)S(1)}, f32[16,2,7,32,128]{4,3,2,1,0:T(8,128)S(1)}, f32[2,16,48,128]{3,2,1,0:T(8,128)S(1)}) custom-call(f32[16,16,128]{2,1,0:T(8,128)S(1)} %get-tuple-element.15.own, f32[8,16,128]{2,1,0:T(8,128)S(1)} %collective-permute-done.10.xl, f32[8,16,128]{2,1,0:T(8,128)S(1)} %collective-permute-done.11.xr, ...), custom_call_target="tpu_custom_call" | custom-call | tf_op jit(solution)/shard_map/down2/pallas_call | solution.py:722
  71.5 11.4 %all_to_all.5 = f32[8,4,128]{2,1,0:T(4,128)S(1)} all-to-all(f32[8,4,128]{2,1,0:T(4,128)S(1)} %get-tuple-element.16), channel_id=1, replica_groups=mesh['gx'=8,'gy'=32] {'gx'}, dimensions={0} | all-to-all | bytes 32768 | tf_op jit(solution)/shard_map/all_to_all | solution.py:774
  82.8 0.7 collective-permute-start.15
  83.6 1.9 %collective-permute-start.14 = (f32[32,128]{1,0:T(8,128)S(1)}, f32[32,128]{1,0:T(8,128)S(1)}, u32[]{:S(2)}, u32[]{:S(2)}) collective-permute-start(f32[32,128]{1,0:T(8,128)S(1)} %bitcast.28), channel_id=1, source_target_pairs={{2,0},{3,1},{4,2},{5,3},{6,4},{7,5},{0,6},{1,7},{10,8},{11,9},{12,... | collective-permute-start | bytes 49160 | tf_op jit(solution)/shard_map/ppermute | solution.py:745
  85.5 1.1 collective-permute-done.16
  86.7 0.3 collective-permute-done.15
  86.9 0.8 collective-permute-done.14
  87.7 1.3 collective-permute-start.18
  89.0 3.9 %collective-permute-start.17 = (f32[4,32,128]{2,1,0:T(8,128)S(1)}, f32[4,32,128]{2,1,0:T(8,128)S(1)}, u32[]{:S(2)}, u32[]{:S(2)}) collective-permute-start(f32[4,32,128]{2,1,0:T(8,128)S(1)} %get-tuple-element.40), channel_id=1, source_target_pairs={{8,0},{9,1},{10,2},{11,3},{12,4},{13,5},{14,6},{15,7},{16,8},{17,9... | collective-permute-start | bytes 196616 | tf_op jit(solution)/shard_map/ppermute | solution.py:745
  92.9 0.5 collective-permute-start.19
  93.4 0.0 collective-permute-done.18
  93.4 2.9 %collective-permute-done.17 = f32[4,32,128]{2,1,0:T(8,128)S(1)} collective-permute-done((f32[4,32,128]{2,1,0:T(8,128)S(1)}, f32[4,32,128]{2,1,0:T(8,128)S(1)}, u32[]{:S(2)}, u32[]{:S(2)}) %collective-permute-start.17) | collective-permute-done | bytes 65568 | tf_op jit(solution)/shard_map/ppermute | solution.py:745
  96.3 1.0 collective-permute-done.19
  97.3 5.7 %collective-permute-start.20 = (f32[4,4,32,128]{3,2,1,0:T(8,128)S(1)}, f32[4,4,32,128]{3,2,1,0:T(8,128)S(1)}, u32[]{:S(2)}, u32[]{:S(2)}) collective-permute-start(f32[4,4,32,128]{3,2,1,0:T(8,128)S(1)} %pad_maximum_fusion.4.near), channel_id=1, source_target_pairs={{1,0},{0,1},{3,2},{2,3},{5,4},{4,5},{7,6},{6,7},{9,8},{8,9},{11,10... | collective-permute-start | bytes 786440 | tf_op jit(solution)/shard_map/ppermute | solution.py:745
  103.0 1.2 collective-permute-done.20.far
  104.2 24.8 %climb.1 = f32[32,32,128]{2,1,0:T(8,128)} custom-call(f32[4,4,32,128]{3,2,1,0:T(8,128)S(1)} %pad_maximum_fusion.4.near, f32[4,4,32,128]{3,2,1,0:T(8,128)S(1)} %collective-permute-done.20.far, f32[24,2,7,48,128]{4,3,2,1,0:T(8,128)S(1)} %get-tuple-element.17.s0, f32[2,24,64,128]{3,2,1,0:T(8,128)S(1)} %get-tuple-element.18.i0, ...), custom_call_target="tpu_custom_call" | custom-call | tf_op jit(solution)/shard_map/climb/pallas_call | solution.py:722
  (23 shorter events, 0.3 us)
Async XLA Ops:
  0.0 20.1 %copy-start.1 = (f32[32,32,128]{2,1,0:T(8,128)S(1)}, f32[32,32,128]{2,1,0:T(8,128)}, u32[]{:S(2)}) copy-start(f32[32,32,128]{2,1,0:T(8,128)} %e_in.1) | copy-start | bytes 1572868
  0.0 20.1 %copy-start = (f32[32,32,128]{2,1,0:T(8,128)S(1)}, f32[32,32,128]{2,1,0:T(8,128)}, u32[]{:S(2)}) copy-start(f32[32,32,128]{2,1,0:T(8,128)} %f_in.1) | copy-start | bytes 1572868
  1.3 12.5 %collective-permute-start = (f32[2,8,32,128]{3,2,1,0:T(8,128)S(1)}, f32[2,8,32,128]{3,2,1,0:T(8,128)S(1)}, u32[]{:S(2)}, u32[]{:S(2)}) collective-permute-start(f32[2,8,32,128]{3,2,1,0:T(8,128)S(1)} %pad_maximum_fusion), channel_id=1, source_target_pairs={{0,32},{32,64},{64,96},{96,128},{128,160},{160,192},{192,224},{224... | collective-permute-start | bytes 786440 | tf_op jit(solution)/shard_map/ppermute | solution.py:737
  3.8 10.0 %collective-permute-start.1 = (f32[2,8,32,128]{3,2,1,0:T(8,128)S(1)}, f32[2,8,32,128]{3,2,1,0:T(8,128)S(1)}, u32[]{:S(2)}, u32[]{:S(2)}) collective-permute-start(f32[2,8,32,128]{3,2,1,0:T(8,128)S(1)} %pad_maximum_fusion.1), channel_id=1, source_target_pairs={{32,0},{64,32},{96,64},{128,96},{160,128},{192,160},{224,192},{0,2... | collective-permute-start | bytes 786440 | tf_op jit(solution)/shard_map/ppermute | solution.py:737
  9.0 7.4 %collective-permute-start.2 = (f32[2,32,8,128]{3,2,1,0:T(8,128)S(1)}, f32[2,32,8,128]{3,2,1,0:T(8,128)S(1)}, u32[]{:S(2)}, u32[]{:S(2)}) collective-permute-start(f32[2,32,8,128]{3,2,1,0:T(8,128)S(1)} %pad_maximum_fusion.2), channel_id=1, source_target_pairs={{0,1},{1,2},{2,3},{3,4},{4,5},{5,6},{6,7},{7,8},{8,9},{9,10},{10,1... | collective-permute-start | bytes 786440 | tf_op jit(solution)/shard_map/ppermute | solution.py:737
  11.3 6.2 %collective-permute-start.3 = (f32[2,32,8,128]{3,2,1,0:T(8,128)S(1)}, f32[2,32,8,128]{3,2,1,0:T(8,128)S(1)}, u32[]{:S(2)}, u32[]{:S(2)}) collective-permute-start(f32[2,32,8,128]{3,2,1,0:T(8,128)S(1)} %pad_maximum_fusion.3), channel_id=1, source_target_pairs={{1,0},{2,1},{3,2},{4,3},{5,4},{6,5},{7,6},{8,7},{9,8},{10,9},{11,1... | collective-permute-start | bytes 786440 | tf_op jit(solution)/shard_map/ppermute | solution.py:737
  13.9 5.1 %collective-permute-start.5 = (f32[2,16,8,128]{3,2,1,0:T(8,128)S(1)}, f32[2,16,8,128]{3,2,1,0:T(8,128)S(1)}, u32[]{:S(2)}, u32[]{:S(2)}) collective-permute-start(f32[2,16,8,128]{3,2,1,0:T(8,128)S(1)} %get-tuple-element.23), channel_id=1, source_target_pairs={{1,0},{2,1},{3,2},{4,3},{5,4},{6,5},{7,6},{8,7},{9,8},{10,9},{11,1... | collective-permute-start | bytes 393224 | tf_op jit(solution)/shard_map/ppermute | solution.py:737
  15.4 4.7 %collective-permute-start.4 = (f32[2,16,8,128]{3,2,1,0:T(8,128)S(1)}, f32[2,16,8,128]{3,2,1,0:T(8,128)S(1)}, u32[]{:S(2)}, u32[]{:S(2)}) collective-permute-start(f32[2,16,8,128]{3,2,1,0:T(8,128)S(1)} %get-tuple-element.24), channel_id=1, source_target_pairs={{0,1},{1,2},{2,3},{3,4},{4,5},{5,6},{6,7},{7,8},{8,9},{9,10},{10,1... | collective-permute-start | bytes 393224 | tf_op jit(solution)/shard_map/ppermute | solution.py:737
  27.7 4.8 %collective-permute-start.6 = (f32[13,16,128]{2,1,0:T(8,128)S(1)}, f32[13,16,128]{2,1,0:T(8,128)S(1)}, u32[]{:S(2)}, u32[]{:S(2)}) collective-permute-start(f32[13,16,128]{2,1,0:T(8,128)S(1)} %get-tuple-element.38), channel_id=1, source_target_pairs={{0,32},{32,64},{64,96},{96,128},{128,160},{160,192},{192,224},{224... | collective-permute-start | bytes 319496 | tf_op jit(solution)/shard_map/ppermute | solution.py:737
  27.8 4.8 %collective-permute-start.7 = (f32[13,16,128]{2,1,0:T(8,128)S(1)}, f32[13,16,128]{2,1,0:T(8,128)S(1)}, u32[]{:S(2)}, u32[]{:S(2)}) collective-permute-start(f32[13,16,128]{2,1,0:T(8,128)S(1)} %get-tuple-element.37), channel_id=1, source_target_pairs={{32,0},{64,32},{96,64},{128,96},{160,128},{192,160},{224,192},{0,2... | collective-permute-start | bytes 319496 | tf_op jit(solution)/shard_map/ppermute | solution.py:737
  32.6 9.4 %collective-permute-start.9 = (f32[42,16,128]{2,1,0:T(8,128)S(1)}, f32[42,16,128]{2,1,0:T(8,128)S(1)}, u32[]{:S(2)}, u32[]{:S(2)}) collective-permute-start(f32[42,16,128]{2,1,0:T(8,128)S(1)} %constant_dynamic-update-slice_fusion.2), channel_id=1, source_target_pairs={{1,0},{2,1},{3,2},{4,3},{5,4},{6,5},{7,6},{8,7},{9,8},{10,9},{11,1... | collective-permute-start | bytes 1032200 | tf_op jit(solution)/shard_map/ppermute | solution.py:737
  40.8 4.2 %collective-permute-start.8 = (f32[42,16,128]{2,1,0:T(8,128)S(1)}, f32[42,16,128]{2,1,0:T(8,128)S(1)}, u32[]{:S(2)}, u32[]{:S(2)}) collective-permute-start(f32[42,16,128]{2,1,0:T(8,128)S(1)} %constant_dynamic-update-slice_fusion.2), channel_id=1, source_target_pairs={{0,1},{1,2},{2,3},{3,4},{4,5},{5,6},{6,7},{7,8},{8,9},{9,10},{10,1... | collective-permute-start | bytes 1032200 | tf_op jit(solution)/shard_map/ppermute | solution.py:737
  52.7 4.6 %collective-permute-start.10 = (f32[8,16,128]{2,1,0:T(8,128)S(1)}, f32[8,16,128]{2,1,0:T(8,128)S(1)}, u32[]{:S(2)}, u32[]{:S(2)}) collective-permute-start(f32[8,16,128]{2,1,0:T(8,128)S(1)} %get-tuple-element.36), channel_id=1, source_target_pairs={{0,32},{32,64},{64,96},{96,128},{128,160},{160,192},{192,224},{224... | collective-permute-start | bytes 196616 | tf_op jit(solution)/shard_map/ppermute | solution.py:737
  54.4 3.4 %collective-permute-start.11 = (f32[8,16,128]{2,1,0:T(8,128)S(1)}, f32[8,16,128]{2,1,0:T(8,128)S(1)}, u32[]{:S(2)}, u32[]{:S(2)}) collective-permute-start(f32[8,16,128]{2,1,0:T(8,128)S(1)} %get-tuple-element.35), channel_id=1, source_target_pairs={{32,0},{64,32},{96,64},{128,96},{160,128},{192,160},{224,192},{0,2... | collective-permute-start | bytes 196616 | tf_op jit(solution)/shard_map/ppermute | solution.py:737
  57.8 8.3 %collective-permute-start.13 = (f32[32,8,128]{2,1,0:T(8,128)S(1)}, f32[32,8,128]{2,1,0:T(8,128)S(1)}, u32[]{:S(2)}, u32[]{:S(2)}) collective-permute-start(f32[32,8,128]{2,1,0:T(8,128)S(1)} %get-tuple-element.33), channel_id=1, source_target_pairs={{1,0},{2,1},{3,2},{4,3},{5,4},{6,5},{7,6},{8,7},{9,8},{10,9},{11,1... | collective-permute-start | bytes 393224 | tf_op jit(solution)/shard_map/ppermute | solution.py:737
  65.1 2.0 %collective-permute-start.12 = (f32[32,8,128]{2,1,0:T(8,128)S(1)}, f32[32,8,128]{2,1,0:T(8,128)S(1)}, u32[]{:S(2)}, u32[]{:S(2)}) collective-permute-start(f32[32,8,128]{2,1,0:T(8,128)S(1)} %get-tuple-element.34), channel_id=1, source_target_pairs={{0,1},{1,2},{2,3},{3,4},{4,5},{5,6},{6,7},{7,8},{8,9},{9,10},{10,1... | collective-permute-start | bytes 393224 | tf_op jit(solution)/shard_map/ppermute | solution.py:737
  82.8 3.8 %collective-permute-start.16 = (f32[32,128]{1,0:T(8,128)S(1)}, f32[32,128]{1,0:T(8,128)S(1)}, u32[]{:S(2)}, u32[]{:S(2)}) collective-permute-start(f32[32,128]{1,0:T(8,128)S(1)} %bitcast.26), channel_id=1, source_target_pairs={{6,0},{7,1},{0,2},{1,3},{2,4},{3,5},{4,6},{5,7},{14,8},{15,9},{8,1... | collective-permute-start | bytes 49160 | tf_op jit(solution)/shard_map/ppermute | solution.py:745
  82.8 4.1 %collective-permute-start.15 = (f32[32,128]{1,0:T(8,128)S(1)}, f32[32,128]{1,0:T(8,128)S(1)}, u32[]{:S(2)}, u32[]{:S(2)}) collective-permute-start(f32[32,128]{1,0:T(8,128)S(1)} %bitcast.27), channel_id=1, source_target_pairs={{4,0},{5,1},{6,2},{7,3},{0,4},{1,5},{2,6},{3,7},{12,8},{13,9},{14,... | collective-permute-start | bytes 49160 | tf_op jit(solution)/shard_map/ppermute | solution.py:745
  83.6 4.1 %collective-permute-start.14 = (f32[32,128]{1,0:T(8,128)S(1)}, f32[32,128]{1,0:T(8,128)S(1)}, u32[]{:S(2)}, u32[]{:S(2)}) collective-permute-start(f32[32,128]{1,0:T(8,128)S(1)} %bitcast.28), channel_id=1, source_target_pairs={{2,0},{3,1},{4,2},{5,3},{6,4},{7,5},{0,6},{1,7},{10,8},{11,9},{12,... | collective-permute-start | bytes 49160 | tf_op jit(solution)/shard_map/ppermute | solution.py:745
  87.7 5.7 %collective-permute-start.18 = (f32[4,32,128]{2,1,0:T(8,128)S(1)}, f32[4,32,128]{2,1,0:T(8,128)S(1)}, u32[]{:S(2)}, u32[]{:S(2)}) collective-permute-start(f32[4,32,128]{2,1,0:T(8,128)S(1)} %get-tuple-element.40), channel_id=1, source_target_pairs={{16,0},{17,1},{18,2},{19,3},{20,4},{21,5},{22,6},{23,7},{24,8},{25... | collective-permute-start | bytes 196616 | tf_op jit(solution)/shard_map/ppermute | solution.py:745
  89.0 7.3 %collective-permute-start.17 = (f32[4,32,128]{2,1,0:T(8,128)S(1)}, f32[4,32,128]{2,1,0:T(8,128)S(1)}, u32[]{:S(2)}, u32[]{:S(2)}) collective-permute-start(f32[4,32,128]{2,1,0:T(8,128)S(1)} %get-tuple-element.40), channel_id=1, source_target_pairs={{8,0},{9,1},{10,2},{11,3},{12,4},{13,5},{14,6},{15,7},{16,8},{17,9... | collective-permute-start | bytes 196616 | tf_op jit(solution)/shard_map/ppermute | solution.py:745
  92.9 4.3 %collective-permute-start.19 = (f32[4,32,128]{2,1,0:T(8,128)S(1)}, f32[4,32,128]{2,1,0:T(8,128)S(1)}, u32[]{:S(2)}, u32[]{:S(2)}) collective-permute-start(f32[4,32,128]{2,1,0:T(8,128)S(1)} %get-tuple-element.40), channel_id=1, source_target_pairs={{24,0},{25,1},{26,2},{27,3},{28,4},{29,5},{30,6},{31,7},{0,8},{1,9... | collective-permute-start | bytes 196616 | tf_op jit(solution)/shard_map/ppermute | solution.py:745
  97.3 6.9 %collective-permute-start.20 = (f32[4,4,32,128]{3,2,1,0:T(8,128)S(1)}, f32[4,4,32,128]{3,2,1,0:T(8,128)S(1)}, u32[]{:S(2)}, u32[]{:S(2)}) collective-permute-start(f32[4,4,32,128]{3,2,1,0:T(8,128)S(1)} %pad_maximum_fusion.4.near), channel_id=1, source_target_pairs={{1,0},{0,1},{3,2},{2,3},{5,4},{4,5},{7,6},{6,7},{9,8},{8,9},{11,10... | collective-permute-start | bytes 786440 | tf_op jit(solution)/shard_map/ppermute | solution.py:745

commit v5 on v3

--- a/solution.py
+++ b/solution.py
@@ -14,7 +14,7 @@
 GX = 8
 GY = 32
 CHUNK = 8
-C3 = 1
+C3 = 8
 KEPT = (5, 19, 8, 40)
 GROUPS = 4
 
@@ -338,17 +338,15 @@
     loop(0, count, body, UNROLL["put"])
 
 
-def down1(own, xl, xr, yl, yr, cl, cr, out, kept, v, e, f, total, tmp, state, sems):
+def down1(own, xl, xr, yl, yr, out, kept, v, e, f, total, tmp, state, sems):
     gx, gy = lax.axis_index("gx"), lax.axis_index("gy")
     fill_rim(e, 48)
     clear(v, 48)
     put_split(xl, 0, 13, 3, 16, e, f)
     put_split(own, 0, 16, 16, 16, e, f)
     put_split(xr, 0, 13, 32, 16, e, f)
-    for side, corner, y in ((yl, cl, 0), (yr, cr, 32)):
-        put_split(corner, 0, 13, 3, y, e, f)
-        put_split(side, 0, 16, 16, y, e, f)
-        put_split(corner, 13, 13, 32, y, e, f)
+    put_split(yl, 0, 42, 3, 0, e, f)
+    put_split(yr, 0, 42, 3, 32, e, f)
 
     def put(q, fc, ec):
         out[q] = interleave(fc, ec)
@@ -372,17 +370,15 @@
     wait_all([copy for _, copy in copies])
 
 
-def down2(own, xl, xr, yl, yr, cl, cr, out, state, v, e, f, total, tmp, coarse):
+def down2(own, xl, xr, yl, yr, out, state, v, e, f, total, tmp, coarse):
     gx, gy = lax.axis_index("gx"), lax.axis_index("gy")
     fill_rim(e, 32)
     clear(v, 32)
     put_split(xl, 0, 8, 0, 8, e, f)
     put_split(own, 0, 16, 8, 8, e, f)
     put_split(xr, 0, 8, 24, 8, e, f)
-    for side, corner, y in ((yl, cl, 0), (yr, cr, 24)):
-        put_split(corner, 0, 8, 0, y, e, f)
-        put_split(side, 0, 16, 8, y, e, f)
-        put_split(corner, 8, 8, 24, y, e, f)
+    put_split(yl, 0, 32, 0, 0, e, f)
+    put_split(yr, 0, 32, 0, 24, e, f)
 
     def put(q, fc, ec):
         coarse[0, q, 0:4, :] = fc
@@ -756,7 +752,6 @@
     both = (right_side, permittivity)
     xl, xr = exchange("gx", jnp.stack([b[24:] for b in both]), jnp.stack([b[:8] for b in both]))
     yl, yr = exchange("gy", jnp.stack([b[:, 24:] for b in both]), jnp.stack([b[:, :8] for b in both]))
-    xl, xr, yl, yr = lax.optimization_barrier((xl, xr, yl, yr))
     corners = jnp.concatenate([xl, xr], axis=1)
     cl, cr = exchange("gy", corners[:, :, 24:], corners[:, :, :8])
     p1, s0, v0 = kernel_call(
@@ -765,23 +760,19 @@
         right_side, permittivity, xl, xr, yl, yr, cl, cr)
 
     xl, xr = exchange("gx", p1[3:], p1[:13])
-    yl, yr = exchange("gy", p1, p1)
-    xl, xr, yl, yr = lax.optimization_barrier((xl, xr, yl, yr))
-    corners = jnp.concatenate([xl, xr], axis=0)
-    cl, cr = exchange("gy", corners, corners)
+    wide = jnp.concatenate([xl, p1, xr], axis=0)
+    yl, yr = exchange("gy", wide, wide)
     p2, s1, v1 = kernel_call(
-        down1, "vvvvvvv", (shaped(16, 16, LANES),) + kept_shapes(1), "vav", down_scratch(1)
+        down1, "vvvvv", (shaped(16, 16, LANES),) + kept_shapes(1), "vav", down_scratch(1)
         + [pltpu.VMEM((EXT[1] // 2, 2, 7, EXT[1], LANES), F32), pltpu.SemaphoreType.DMA((GROUPS,))], 16,
-        p1, xl, xr, yl, yr, cl, cr)
+        p1, xl, xr, yl, yr)
 
     xl, xr = exchange("gx", p2[:8], p2[8:])
-    yl, yr = exchange("gy", p2[:, :8], p2[:, 8:])
-    xl, xr, yl, yr = lax.optimization_barrier((xl, xr, yl, yr))
-    corners = jnp.concatenate([xl, xr], axis=0)
-    cl, cr = exchange("gy", corners[:, :8], corners[:, 8:])
+    wide = jnp.concatenate([xl, p2, xr], axis=0)
+    yl, yr = exchange("gy", wide[:, :8], wide[:, 8:])
     p3, s2, v2 = kernel_call(
-        down2, "vvvvvvv", (shaped(GX, 4, LANES),) + kept_shapes(2), KEPT_SPEC,
-        down_scratch(2) + [pltpu.VMEM((2, 4, 8, LANES), F32)], 8, p2, xl, xr, yl, yr, cl, cr)
+        down2, "vvvvv", (shaped(GX, 4, LANES),) + kept_shapes(2), KEPT_SPEC,
+        down_scratch(2) + [pltpu.VMEM((2, 4, 8, LANES), F32)], 8, p2, xl, xr, yl, yr)
 
     column = lax.all_to_all(p3, "gx", 0, 0, tiled=True).reshape(4 * GX, LANES)
     along_y = jnp.stack([column] + [from_offset(column, 0, d, 0) for d in (1, 2, 3)])

time: 137 us -> 120 us (0.88)
  waiting for transfers between devices: 31 us -> 23.4 us
  Pallas kernels: 41.7 us -> 35.8 us
  starting transfers between devices: 51 us -> 46.8 us
    ppermute x9 -> x7, waiting for transfers between devices: 13.1 us -> 5.19 us  [exchange(): lax.ppermute(to_previous, axis, backward)]
    pallas_call x4, Pallas kernels: 41.7 us -> 35.8 us  [kernel_call(): pl.pallas_call(body, in_specs=specs(in_spaces), out_specs=tuple(specs(out...]
    ppermute x9 -> x7, starting transfers between devices: 30.7 us -> 25.2 us  [exchange(): lax.ppermute(to_previous, axis, backward)]
    ppermute x9 -> x7, starting transfers between devices: 6.33 us -> 7.52 us  [exchange(): lax.ppermute(to_next, axis, onward)]
    ppermute x9 -> x7, waiting for transfers between devices: 10.7 us -> 11.1 us  [exchange(): lax.ppermute(to_next, axis, onward)]
  transfers between devices with their start and end apart: 25 -> 21, of which waited for: 18 -> 17; matrix products, arithmetic and copies ran while one was open for 1% -> 1% of each run, Pallas kernels for 0% -> 0%
where the time goes in v5:
time: 120 us
  starting transfers between devices  46.8 us (39%)
  Pallas kernels  35.8 us (30%)
  waiting for transfers between devices  23.4 us (20%)
  blocking collectives  11.4 us (10%)
  local copies, waits for them, and re-layouts  2.51 us (2%)
    pallas_call x4, Pallas kernels, kernel_call(): pl.pallas_call(body, in_specs=specs(in_spaces), out_specs=tuple(specs(out...  35.8 us
    ppermute x7, starting transfers between devices, exchange(): lax.ppermute(to_previous, axis, backward)  25.2 us
    ppermute x7, starting transfers between devices, from_offset(): return lax.ppermute(values, 'gy', moves)  14.1 us
    all_to_all x1, blocking collectives, per_device(): column = lax.all_to_all(p3, 'gx', 0, 0, tiled=True).reshape(4 * GX, LANES)  11.4 us
    ppermute x7, waiting for transfers between devices, exchange(): lax.ppermute(to_next, axis, onward)  11.1 us
    ppermute x7, starting transfers between devices, exchange(): lax.ppermute(to_next, axis, onward)  7.52 us
    ppermute x7, waiting for transfers between devices, from_offset(): return lax.ppermute(values, 'gy', moves)  7.16 us
    ppermute x7, waiting for transfers between devices, exchange(): lax.ppermute(to_previous, axis, backward)  5.19 us
  transfers between devices with their start and end apart: 21, of which 17 were waited for; matrix products, arithmetic and copies ran while one was open for 1% of the time, Pallas kernels for 0%

profile of v5, /device:TPU:1, one launch (start us, length us, event | category | flops | bytes accessed | tf_op | source)
XLA Modules:
  0.0 120.2 jit_solution(3625129464003855452)
XLA Ops:
  0.0 1.2 %slice_bitcast_fusion.4 = (f32[1,8,32,128]{3,2,1,0:T(8,128)S(1)}, f32[1,8,32,128]{3,2,1,0:T(8,128)S(1)}, f32[1,8,32,128]{3,2,1,0:T(8,128)S(1)}, f32[1,8,32,128]{3,2,1,0:T(8,128)S(1)}) fusion(f32[32,32,128]{2,1,0:T(8,128)} %e_in.1, f32[32,32,128]{2,1,0:T(8,128)} %f_in.1), kind=kLoop, calls=%fused_computation.9 | loop fusion | bytes 1048576 | tf_op jit(solution)/shard_map/stack | solution.py:753
  1.3 2.5 %collective-permute-start = (f32[2,8,32,128]{3,2,1,0:T(8,128)S(1)}, f32[2,8,32,128]{3,2,1,0:T(8,128)S(1)}, u32[]{:S(2)}, u32[]{:S(2)}) collective-permute-start(f32[2,8,32,128]{3,2,1,0:T(8,128)S(1)} %pad_maximum_fusion), channel_id=1, source_target_pairs={{0,32},{32,64},{64,96},{96,128},{128,160},{160,192},{192,224},{224... | collective-permute-start | bytes 786440 | tf_op jit(solution)/shard_map/ppermute | solution.py:740
  3.8 4.0 %collective-permute-start.1 = (f32[2,8,32,128]{3,2,1,0:T(8,128)S(1)}, f32[2,8,32,128]{3,2,1,0:T(8,128)S(1)}, u32[]{:S(2)}, u32[]{:S(2)}) collective-permute-start(f32[2,8,32,128]{3,2,1,0:T(8,128)S(1)} %pad_maximum_fusion.1), channel_id=1, source_target_pairs={{32,0},{64,32},{96,64},{128,96},{160,128},{192,160},{224,192},{0,2... | collective-permute-start | bytes 786440 | tf_op jit(solution)/shard_map/ppermute | solution.py:740
  7.9 1.1 slice_bitcast_fusion
  9.0 2.2 %collective-permute-start.2 = (f32[2,32,8,128]{3,2,1,0:T(8,128)S(1)}, f32[2,32,8,128]{3,2,1,0:T(8,128)S(1)}, u32[]{:S(2)}, u32[]{:S(2)}) collective-permute-start(f32[2,32,8,128]{3,2,1,0:T(8,128)S(1)} %pad_maximum_fusion.2), channel_id=1, source_target_pairs={{0,1},{1,2},{2,3},{3,4},{4,5},{5,6},{6,7},{7,8},{8,9},{9,10},{10,1... | collective-permute-start | bytes 786440 | tf_op jit(solution)/shard_map/ppermute | solution.py:740
  11.3 0.1 collective-permute-start.3
  11.3 2.4 %collective-permute-done.xl = f32[2,8,32,128]{3,2,1,0:T(8,128)S(1)} collective-permute-done((f32[2,8,32,128]{3,2,1,0:T(8,128)S(1)}, f32[2,8,32,128]{3,2,1,0:T(8,128)S(1)}, u32[]{:S(2)}, u32[]{:S(2)}) %collective-permute-start) | collective-permute-done | bytes 262176 | tf_op jit(solution)/shard_map/ppermute | solution.py:740
  13.8 0.0 collective-permute-done.1.xr
  13.9 1.5 %collective-permute-start.5 = (f32[2,16,8,128]{3,2,1,0:T(8,128)S(1)}, f32[2,16,8,128]{3,2,1,0:T(8,128)S(1)}, u32[]{:S(2)}, u32[]{:S(2)}) collective-permute-start(f32[2,16,8,128]{3,2,1,0:T(8,128)S(1)} %get-tuple-element.23), channel_id=1, source_target_pairs={{1,0},{2,1},{3,2},{4,3},{5,4},{6,5},{7,6},{8,7},{9,8},{10,9},{11,1... | collective-permute-start | bytes 393224 | tf_op jit(solution)/shard_map/ppermute | solution.py:740
  15.4 1.0 collective-permute-start.4
  16.4 0.0 collective-permute-done.2.yl
  16.4 1.0 collective-permute-done.3.yr
  17.4 1.6 %collective-permute-done.5.cr = f32[2,16,8,128]{3,2,1,0:T(8,128)S(1)} collective-permute-done((f32[2,16,8,128]{3,2,1,0:T(8,128)S(1)}, f32[2,16,8,128]{3,2,1,0:T(8,128)S(1)}, u32[]{:S(2)}, u32[]{:S(2)}) %collective-permute-start.5) | collective-permute-done | bytes 131104 | tf_op jit(solution)/shard_map/ppermute | solution.py:740
  19.0 1.1 collective-permute-done.4.cl
  20.1 7.6 %down0.1 = (f32[16,16,128]{2,1,0:T(8,128)S(1)}, f32[24,2,7,48,128]{4,3,2,1,0:T(8,128)S(1)}, f32[2,24,64,128]{3,2,1,0:T(8,128)S(1)}) custom-call(f32[32,32,128]{2,1,0:T(8,128)S(1)} %copy-done, f32[32,32,128]{2,1,0:T(8,128)S(1)} %copy-done.1, f32[2,8,32,128]{3,2,1,0:T(8,128)S(1)} %collective-permute-done.xl, f32[2,8,32,128]{3,2,1,0:T(8,128)S(1)} %collective-permute-done.1.xr, ...), custom_call_target="tpu_custom_call" | custom-call | tf_op jit(solution)/shard_map/down0/pallas_call | solution.py:725
  27.7 0.1 collective-permute-start.6
  27.8 2.7 %collective-permute-start.7 = (f32[13,16,128]{2,1,0:T(8,128)S(1)}, f32[13,16,128]{2,1,0:T(8,128)S(1)}, u32[]{:S(2)}, u32[]{:S(2)}) collective-permute-start(f32[13,16,128]{2,1,0:T(8,128)S(1)} %get-tuple-element.37), channel_id=1, source_target_pairs={{32,0},{64,32},{96,64},{128,96},{160,128},{192,160},{224,192},{0,2... | collective-permute-start | bytes 319496 | tf_op jit(solution)/shard_map/ppermute | solution.py:740
  30.5 2.1 %collective-permute-done.6.xl = f32[13,16,128]{2,1,0:T(8,128)S(1)} collective-permute-done((f32[13,16,128]{2,1,0:T(8,128)S(1)}, f32[13,16,128]{2,1,0:T(8,128)S(1)}, u32[]{:S(2)}, u32[]{:S(2)}) %collective-permute-start.6) | collective-permute-done | bytes 106528 | tf_op jit(solution)/shard_map/ppermute | solution.py:740
  32.6 0.0 collective-permute-done.7.xr
  32.6 8.1 %collective-permute-start.9 = (f32[42,16,128]{2,1,0:T(8,128)S(1)}, f32[42,16,128]{2,1,0:T(8,128)S(1)}, u32[]{:S(2)}, u32[]{:S(2)}) collective-permute-start(f32[42,16,128]{2,1,0:T(8,128)S(1)} %constant_dynamic-update-slice_fusion.2), channel_id=1, source_target_pairs={{1,0},{2,1},{3,2},{4,3},{5,4},{6,5},{7,6},{8,7},{9,8},{10,9},{11,1... | collective-permute-start | bytes 1032200 | tf_op jit(solution)/shard_map/ppermute | solution.py:740
  40.8 0.0 collective-permute-start.8
  40.8 1.3 %collective-permute-done.9.yr = f32[42,16,128]{2,1,0:T(8,128)S(1)} collective-permute-done((f32[42,16,128]{2,1,0:T(8,128)S(1)}, f32[42,16,128]{2,1,0:T(8,128)S(1)}, u32[]{:S(2)}, u32[]{:S(2)}) %collective-permute-start.9) | collective-permute-done | bytes 344096 | tf_op jit(solution)/shard_map/ppermute | solution.py:740
  42.1 2.9 %collective-permute-done.8.yl = f32[42,16,128]{2,1,0:T(8,128)S(1)} collective-permute-done((f32[42,16,128]{2,1,0:T(8,128)S(1)}, f32[42,16,128]{2,1,0:T(8,128)S(1)}, u32[]{:S(2)}, u32[]{:S(2)}) %collective-permute-start.8) | collective-permute-done | bytes 344096 | tf_op jit(solution)/shard_map/ppermute | solution.py:740
  45.0 7.8 %down1.1 = (f32[16,16,128]{2,1,0:T(8,128)S(1)}, f32[14,2,7,32,128]{4,3,2,1,0:T(8,128)S(1)}, f32[2,24,64,128]{3,2,1,0:T(8,128)S(1)}) custom-call(f32[16,16,128]{2,1,0:T(8,128)S(1)} %get-tuple-element.14.own, f32[13,16,128]{2,1,0:T(8,128)S(1)} %collective-permute-done.6.xl, f32[13,16,128]{2,1,0:T(8,128)S(1)} %collective-permute-done.7.xr, ...), custom_call_target="tpu_custom_call" | custom-call | tf_op jit(solution)/shard_map/down1/pallas_call | solution.py:725
  52.7 1.6 %collective-permute-start.10 = (f32[8,16,128]{2,1,0:T(8,128)S(1)}, f32[8,16,128]{2,1,0:T(8,128)S(1)}, u32[]{:S(2)}, u32[]{:S(2)}) collective-permute-start(f32[8,16,128]{2,1,0:T(8,128)S(1)} %get-tuple-element.36), channel_id=1, source_target_pairs={{0,32},{32,64},{64,96},{96,128},{128,160},{160,192},{192,224},{224... | collective-permute-start | bytes 196616 | tf_op jit(solution)/shard_map/ppermute | solution.py:740
  54.4 1.4 %collective-permute-start.11 = (f32[8,16,128]{2,1,0:T(8,128)S(1)}, f32[8,16,128]{2,1,0:T(8,128)S(1)}, u32[]{:S(2)}, u32[]{:S(2)}) collective-permute-start(f32[8,16,128]{2,1,0:T(8,128)S(1)} %get-tuple-element.35), channel_id=1, source_target_pairs={{32,0},{64,32},{96,64},{128,96},{160,128},{192,160},{224,192},{0,2... | collective-permute-start | bytes 196616 | tf_op jit(solution)/shard_map/ppermute | solution.py:740
  55.8 1.6 %collective-permute-done.10.xl = f32[8,16,128]{2,1,0:T(8,128)S(1)} collective-permute-done((f32[8,16,128]{2,1,0:T(8,128)S(1)}, f32[8,16,128]{2,1,0:T(8,128)S(1)}, u32[]{:S(2)}, u32[]{:S(2)}) %collective-permute-start.10) | collective-permute-done | bytes 65568 | tf_op jit(solution)/shard_map/ppermute | solution.py:740
  57.4 0.4 collective-permute-done.11.xr
  57.8 7.3 %collective-permute-start.13 = (f32[32,8,128]{2,1,0:T(8,128)S(1)}, f32[32,8,128]{2,1,0:T(8,128)S(1)}, u32[]{:S(2)}, u32[]{:S(2)}) collective-permute-start(f32[32,8,128]{2,1,0:T(8,128)S(1)} %get-tuple-element.33), channel_id=1, source_target_pairs={{1,0},{2,1},{3,2},{4,3},{5,4},{6,5},{7,6},{8,7},{9,8},{10,9},{11,1... | collective-permute-start | bytes 393224 | tf_op jit(solution)/shard_map/ppermute | solution.py:740
  65.1 0.0 collective-permute-start.12
  65.1 1.0 collective-permute-done.13.yr
  66.1 1.0 collective-permute-done.12.yl
  67.1 4.4 %down2.1 = (f32[8,4,128]{2,1,0:T(4,128)S(1)}, f32[16,2,7,32,128]{4,3,2,1,0:T(8,128)S(1)}, f32[2,16,48,128]{3,2,1,0:T(8,128)S(1)}) custom-call(f32[16,16,128]{2,1,0:T(8,128)S(1)} %get-tuple-element.15.own, f32[8,16,128]{2,1,0:T(8,128)S(1)} %collective-permute-done.10.xl, f32[8,16,128]{2,1,0:T(8,128)S(1)} %collective-permute-done.11.xr, ...), custom_call_target="tpu_custom_call" | custom-call | tf_op jit(solution)/shard_map/down2/pallas_call | solution.py:725
  71.5 11.4 %all_to_all.5 = f32[8,4,128]{2,1,0:T(4,128)S(1)} all-to-all(f32[8,4,128]{2,1,0:T(4,128)S(1)} %get-tuple-element.16), channel_id=1, replica_groups=mesh['gx'=8,'gy'=32] {'gx'}, dimensions={0} | all-to-all | bytes 32768 | tf_op jit(solution)/shard_map/all_to_all | solution.py:777
  82.8 0.0 collective-permute-start.16
  82.8 0.7 collective-permute-start.15
  83.6 1.9 %collective-permute-start.14 = (f32[32,128]{1,0:T(8,128)S(1)}, f32[32,128]{1,0:T(8,128)S(1)}, u32[]{:S(2)}, u32[]{:S(2)}) collective-permute-start(f32[32,128]{1,0:T(8,128)S(1)} %bitcast.28), channel_id=1, source_target_pairs={{2,0},{3,1},{4,2},{5,3},{6,4},{7,5},{0,6},{1,7},{10,8},{11,9},{12,... | collective-permute-start | bytes 49160 | tf_op jit(solution)/shard_map/ppermute | solution.py:748
  85.5 1.1 collective-permute-done.16
  86.7 0.3 collective-permute-done.15
  86.9 0.8 collective-permute-done.14
  87.7 1.3 %collective-permute-start.18 = (f32[4,32,128]{2,1,0:T(8,128)S(1)}, f32[4,32,128]{2,1,0:T(8,128)S(1)}, u32[]{:S(2)}, u32[]{:S(2)}) collective-permute-start(f32[4,32,128]{2,1,0:T(8,128)S(1)} %get-tuple-element.40), channel_id=1, source_target_pairs={{16,0},{17,1},{18,2},{19,3},{20,4},{21,5},{22,6},{23,7},{24,8},{25... | collective-permute-start | bytes 196616 | tf_op jit(solution)/shard_map/ppermute | solution.py:748
  89.0 3.9 %collective-permute-start.17 = (f32[4,32,128]{2,1,0:T(8,128)S(1)}, f32[4,32,128]{2,1,0:T(8,128)S(1)}, u32[]{:S(2)}, u32[]{:S(2)}) collective-permute-start(f32[4,32,128]{2,1,0:T(8,128)S(1)} %get-tuple-element.40), channel_id=1, source_target_pairs={{8,0},{9,1},{10,2},{11,3},{12,4},{13,5},{14,6},{15,7},{16,8},{17,9... | collective-permute-start | bytes 196616 | tf_op jit(solution)/shard_map/ppermute | solution.py:748
  92.9 0.5 collective-permute-start.19
  93.4 2.9 %collective-permute-done.17 = f32[4,32,128]{2,1,0:T(8,128)S(1)} collective-permute-done((f32[4,32,128]{2,1,0:T(8,128)S(1)}, f32[4,32,128]{2,1,0:T(8,128)S(1)}, u32[]{:S(2)}, u32[]{:S(2)}) %collective-permute-start.17) | collective-permute-done | bytes 65568 | tf_op jit(solution)/shard_map/ppermute | solution.py:748
  96.3 1.0 collective-permute-done.19
  97.3 5.7 %collective-permute-start.20 = (f32[4,4,32,128]{3,2,1,0:T(8,128)S(1)}, f32[4,4,32,128]{3,2,1,0:T(8,128)S(1)}, u32[]{:S(2)}, u32[]{:S(2)}) collective-permute-start(f32[4,4,32,128]{3,2,1,0:T(8,128)S(1)} %pad_maximum_fusion.4.near), channel_id=1, source_target_pairs={{1,0},{0,1},{3,2},{2,3},{5,4},{4,5},{7,6},{6,7},{9,8},{8,9},{11,10... | collective-permute-start | bytes 786440 | tf_op jit(solution)/shard_map/ppermute | solution.py:748
  103.0 1.2 collective-permute-done.20.far
  104.2 16.1 %climb.1 = f32[32,32,128]{2,1,0:T(8,128)} custom-call(f32[4,4,32,128]{3,2,1,0:T(8,128)S(1)} %pad_maximum_fusion.4.near, f32[4,4,32,128]{3,2,1,0:T(8,128)S(1)} %collective-permute-done.20.far, f32[24,2,7,48,128]{4,3,2,1,0:T(8,128)S(1)} %get-tuple-element.17.s0, f32[2,24,64,128]{3,2,1,0:T(8,128)S(1)} %get-tuple-element.18.i0, ...), custom_call_target="tpu_custom_call" | custom-call | tf_op jit(solution)/shard_map/climb/pallas_call | solution.py:725
  (23 shorter events, 0.3 us)
Async XLA Ops:
  0.0 20.1 %copy-start.1 = (f32[32,32,128]{2,1,0:T(8,128)S(1)}, f32[32,32,128]{2,1,0:T(8,128)}, u32[]{:S(2)}) copy-start(f32[32,32,128]{2,1,0:T(8,128)} %e_in.1) | copy-start | bytes 1572868
  0.0 20.1 %copy-start = (f32[32,32,128]{2,1,0:T(8,128)S(1)}, f32[32,32,128]{2,1,0:T(8,128)}, u32[]{:S(2)}) copy-start(f32[32,32,128]{2,1,0:T(8,128)} %f_in.1) | copy-start | bytes 1572868
  1.3 12.5 %collective-permute-start = (f32[2,8,32,128]{3,2,1,0:T(8,128)S(1)}, f32[2,8,32,128]{3,2,1,0:T(8,128)S(1)}, u32[]{:S(2)}, u32[]{:S(2)}) collective-permute-start(f32[2,8,32,128]{3,2,1,0:T(8,128)S(1)} %pad_maximum_fusion), channel_id=1, source_target_pairs={{0,32},{32,64},{64,96},{96,128},{128,160},{160,192},{192,224},{224... | collective-permute-start | bytes 786440 | tf_op jit(solution)/shard_map/ppermute | solution.py:740
  3.8 10.0 %collective-permute-start.1 = (f32[2,8,32,128]{3,2,1,0:T(8,128)S(1)}, f32[2,8,32,128]{3,2,1,0:T(8,128)S(1)}, u32[]{:S(2)}, u32[]{:S(2)}) collective-permute-start(f32[2,8,32,128]{3,2,1,0:T(8,128)S(1)} %pad_maximum_fusion.1), channel_id=1, source_target_pairs={{32,0},{64,32},{96,64},{128,96},{160,128},{192,160},{224,192},{0,2... | collective-permute-start | bytes 786440 | tf_op jit(solution)/shard_map/ppermute | solution.py:740
  9.0 7.4 %collective-permute-start.2 = (f32[2,32,8,128]{3,2,1,0:T(8,128)S(1)}, f32[2,32,8,128]{3,2,1,0:T(8,128)S(1)}, u32[]{:S(2)}, u32[]{:S(2)}) collective-permute-start(f32[2,32,8,128]{3,2,1,0:T(8,128)S(1)} %pad_maximum_fusion.2), channel_id=1, source_target_pairs={{0,1},{1,2},{2,3},{3,4},{4,5},{5,6},{6,7},{7,8},{8,9},{9,10},{10,1... | collective-permute-start | bytes 786440 | tf_op jit(solution)/shard_map/ppermute | solution.py:740
  11.3 6.2 %collective-permute-start.3 = (f32[2,32,8,128]{3,2,1,0:T(8,128)S(1)}, f32[2,32,8,128]{3,2,1,0:T(8,128)S(1)}, u32[]{:S(2)}, u32[]{:S(2)}) collective-permute-start(f32[2,32,8,128]{3,2,1,0:T(8,128)S(1)} %pad_maximum_fusion.3), channel_id=1, source_target_pairs={{1,0},{2,1},{3,2},{4,3},{5,4},{6,5},{7,6},{8,7},{9,8},{10,9},{11,1... | collective-permute-start | bytes 786440 | tf_op jit(solution)/shard_map/ppermute | solution.py:740
  13.9 5.1 %collective-permute-start.5 = (f32[2,16,8,128]{3,2,1,0:T(8,128)S(1)}, f32[2,16,8,128]{3,2,1,0:T(8,128)S(1)}, u32[]{:S(2)}, u32[]{:S(2)}) collective-permute-start(f32[2,16,8,128]{3,2,1,0:T(8,128)S(1)} %get-tuple-element.23), channel_id=1, source_target_pairs={{1,0},{2,1},{3,2},{4,3},{5,4},{6,5},{7,6},{8,7},{9,8},{10,9},{11,1... | collective-permute-start | bytes 393224 | tf_op jit(solution)/shard_map/ppermute | solution.py:740
  15.4 4.7 %collective-permute-start.4 = (f32[2,16,8,128]{3,2,1,0:T(8,128)S(1)}, f32[2,16,8,128]{3,2,1,0:T(8,128)S(1)}, u32[]{:S(2)}, u32[]{:S(2)}) collective-permute-start(f32[2,16,8,128]{3,2,1,0:T(8,128)S(1)} %get-tuple-element.24), channel_id=1, source_target_pairs={{0,1},{1,2},{2,3},{3,4},{4,5},{5,6},{6,7},{7,8},{8,9},{9,10},{10,1... | collective-permute-start | bytes 393224 | tf_op jit(solution)/shard_map/ppermute | solution.py:740
  27.7 4.8 %collective-permute-start.6 = (f32[13,16,128]{2,1,0:T(8,128)S(1)}, f32[13,16,128]{2,1,0:T(8,128)S(1)}, u32[]{:S(2)}, u32[]{:S(2)}) collective-permute-start(f32[13,16,128]{2,1,0:T(8,128)S(1)} %get-tuple-element.38), channel_id=1, source_target_pairs={{0,32},{32,64},{64,96},{96,128},{128,160},{160,192},{192,224},{224... | collective-permute-start | bytes 319496 | tf_op jit(solution)/shard_map/ppermute | solution.py:740
  27.8 4.8 %collective-permute-start.7 = (f32[13,16,128]{2,1,0:T(8,128)S(1)}, f32[13,16,128]{2,1,0:T(8,128)S(1)}, u32[]{:S(2)}, u32[]{:S(2)}) collective-permute-start(f32[13,16,128]{2,1,0:T(8,128)S(1)} %get-tuple-element.37), channel_id=1, source_target_pairs={{32,0},{64,32},{96,64},{128,96},{160,128},{192,160},{224,192},{0,2... | collective-permute-start | bytes 319496 | tf_op jit(solution)/shard_map/ppermute | solution.py:740
  32.6 9.4 %collective-permute-start.9 = (f32[42,16,128]{2,1,0:T(8,128)S(1)}, f32[42,16,128]{2,1,0:T(8,128)S(1)}, u32[]{:S(2)}, u32[]{:S(2)}) collective-permute-start(f32[42,16,128]{2,1,0:T(8,128)S(1)} %constant_dynamic-update-slice_fusion.2), channel_id=1, source_target_pairs={{1,0},{2,1},{3,2},{4,3},{5,4},{6,5},{7,6},{8,7},{9,8},{10,9},{11,1... | collective-permute-start | bytes 1032200 | tf_op jit(solution)/shard_map/ppermute | solution.py:740
  40.8 4.2 %collective-permute-start.8 = (f32[42,16,128]{2,1,0:T(8,128)S(1)}, f32[42,16,128]{2,1,0:T(8,128)S(1)}, u32[]{:S(2)}, u32[]{:S(2)}) collective-permute-start(f32[42,16,128]{2,1,0:T(8,128)S(1)} %constant_dynamic-update-slice_fusion.2), channel_id=1, source_target_pairs={{0,1},{1,2},{2,3},{3,4},{4,5},{5,6},{6,7},{7,8},{8,9},{9,10},{10,1... | collective-permute-start | bytes 1032200 | tf_op jit(solution)/shard_map/ppermute | solution.py:740
  52.7 4.6 %collective-permute-start.10 = (f32[8,16,128]{2,1,0:T(8,128)S(1)}, f32[8,16,128]{2,1,0:T(8,128)S(1)}, u32[]{:S(2)}, u32[]{:S(2)}) collective-permute-start(f32[8,16,128]{2,1,0:T(8,128)S(1)} %get-tuple-element.36), channel_id=1, source_target_pairs={{0,32},{32,64},{64,96},{96,128},{128,160},{160,192},{192,224},{224... | collective-permute-start | bytes 196616 | tf_op jit(solution)/shard_map/ppermute | solution.py:740
  54.4 3.4 %collective-permute-start.11 = (f32[8,16,128]{2,1,0:T(8,128)S(1)}, f32[8,16,128]{2,1,0:T(8,128)S(1)}, u32[]{:S(2)}, u32[]{:S(2)}) collective-permute-start(f32[8,16,128]{2,1,0:T(8,128)S(1)} %get-tuple-element.35), channel_id=1, source_target_pairs={{32,0},{64,32},{96,64},{128,96},{160,128},{192,160},{224,192},{0,2... | collective-permute-start | bytes 196616 | tf_op jit(solution)/shard_map/ppermute | solution.py:740
  57.8 8.3 %collective-permute-start.13 = (f32[32,8,128]{2,1,0:T(8,128)S(1)}, f32[32,8,128]{2,1,0:T(8,128)S(1)}, u32[]{:S(2)}, u32[]{:S(2)}) collective-permute-start(f32[32,8,128]{2,1,0:T(8,128)S(1)} %get-tuple-element.33), channel_id=1, source_target_pairs={{1,0},{2,1},{3,2},{4,3},{5,4},{6,5},{7,6},{8,7},{9,8},{10,9},{11,1... | collective-permute-start | bytes 393224 | tf_op jit(solution)/shard_map/ppermute | solution.py:740
  65.1 2.0 %collective-permute-start.12 = (f32[32,8,128]{2,1,0:T(8,128)S(1)}, f32[32,8,128]{2,1,0:T(8,128)S(1)}, u32[]{:S(2)}, u32[]{:S(2)}) collective-permute-start(f32[32,8,128]{2,1,0:T(8,128)S(1)} %get-tuple-element.34), channel_id=1, source_target_pairs={{0,1},{1,2},{2,3},{3,4},{4,5},{5,6},{6,7},{7,8},{8,9},{9,10},{10,1... | collective-permute-start | bytes 393224 | tf_op jit(solution)/shard_map/ppermute | solution.py:740
  82.8 3.8 %collective-permute-start.16 = (f32[32,128]{1,0:T(8,128)S(1)}, f32[32,128]{1,0:T(8,128)S(1)}, u32[]{:S(2)}, u32[]{:S(2)}) collective-permute-start(f32[32,128]{1,0:T(8,128)S(1)} %bitcast.26), channel_id=1, source_target_pairs={{6,0},{7,1},{0,2},{1,3},{2,4},{3,5},{4,6},{5,7},{14,8},{15,9},{8,1... | collective-permute-start | bytes 49160 | tf_op jit(solution)/shard_map/ppermute | solution.py:748
  82.8 4.1 %collective-permute-start.15 = (f32[32,128]{1,0:T(8,128)S(1)}, f32[32,128]{1,0:T(8,128)S(1)}, u32[]{:S(2)}, u32[]{:S(2)}) collective-permute-start(f32[32,128]{1,0:T(8,128)S(1)} %bitcast.27), channel_id=1, source_target_pairs={{4,0},{5,1},{6,2},{7,3},{0,4},{1,5},{2,6},{3,7},{12,8},{13,9},{14,... | collective-permute-start | bytes 49160 | tf_op jit(solution)/shard_map/ppermute | solution.py:748
  83.6 4.1 %collective-permute-start.14 = (f32[32,128]{1,0:T(8,128)S(1)}, f32[32,128]{1,0:T(8,128)S(1)}, u32[]{:S(2)}, u32[]{:S(2)}) collective-permute-start(f32[32,128]{1,0:T(8,128)S(1)} %bitcast.28), channel_id=1, source_target_pairs={{2,0},{3,1},{4,2},{5,3},{6,4},{7,5},{0,6},{1,7},{10,8},{11,9},{12,... | collective-permute-start | bytes 49160 | tf_op jit(solution)/shard_map/ppermute | solution.py:748
  87.7 5.7 %collective-permute-start.18 = (f32[4,32,128]{2,1,0:T(8,128)S(1)}, f32[4,32,128]{2,1,0:T(8,128)S(1)}, u32[]{:S(2)}, u32[]{:S(2)}) collective-permute-start(f32[4,32,128]{2,1,0:T(8,128)S(1)} %get-tuple-element.40), channel_id=1, source_target_pairs={{16,0},{17,1},{18,2},{19,3},{20,4},{21,5},{22,6},{23,7},{24,8},{25... | collective-permute-start | bytes 196616 | tf_op jit(solution)/shard_map/ppermute | solution.py:748
  89.0 7.3 %collective-permute-start.17 = (f32[4,32,128]{2,1,0:T(8,128)S(1)}, f32[4,32,128]{2,1,0:T(8,128)S(1)}, u32[]{:S(2)}, u32[]{:S(2)}) collective-permute-start(f32[4,32,128]{2,1,0:T(8,128)S(1)} %get-tuple-element.40), channel_id=1, source_target_pairs={{8,0},{9,1},{10,2},{11,3},{12,4},{13,5},{14,6},{15,7},{16,8},{17,9... | collective-permute-start | bytes 196616 | tf_op jit(solution)/shard_map/ppermute | solution.py:748
  92.9 4.3 %collective-permute-start.19 = (f32[4,32,128]{2,1,0:T(8,128)S(1)}, f32[4,32,128]{2,1,0:T(8,128)S(1)}, u32[]{:S(2)}, u32[]{:S(2)}) collective-permute-start(f32[4,32,128]{2,1,0:T(8,128)S(1)} %get-tuple-element.40), channel_id=1, source_target_pairs={{24,0},{25,1},{26,2},{27,3},{28,4},{29,5},{30,6},{31,7},{0,8},{1,9... | collective-permute-start | bytes 196616 | tf_op jit(solution)/shard_map/ppermute | solution.py:748
  97.3 6.9 %collective-permute-start.20 = (f32[4,4,32,128]{3,2,1,0:T(8,128)S(1)}, f32[4,4,32,128]{3,2,1,0:T(8,128)S(1)}, u32[]{:S(2)}, u32[]{:S(2)}) collective-permute-start(f32[4,4,32,128]{3,2,1,0:T(8,128)S(1)} %pad_maximum_fusion.4.near), channel_id=1, source_target_pairs={{1,0},{0,1},{3,2},{2,3},{5,4},{4,5},{7,6},{6,7},{9,8},{8,9},{11,10... | collective-permute-start | bytes 786440 | tf_op jit(solution)/shard_map/ppermute | solution.py:748

commit v6 on v5

--- a/solution.py
+++ b/solution.py
@@ -14,12 +14,12 @@
 GX = 8
 GY = 32
 CHUNK = 8
-C3 = 8
+C3 = 16
 KEPT = (5, 19, 8, 40)
 GROUPS = 4
 
 
-UNROLL = {"sweep": 6, "restrict": 4, "put": 16, "add": 4}
+UNROLL = {"sweep": 8, "restrict": 4, "put": 16, "add": 4}
 STOP = 99
 KEPT_SPEC = "vvv"
 

time: 120 us -> 118 us (0.983)
  Pallas kernels: 35.8 us -> 33.8 us
    pallas_call x4, Pallas kernels: 35.8 us -> 33.8 us  [kernel_call(): pl.pallas_call(body, in_specs=specs(in_spaces), out_specs=tuple(specs(out...]
where the time goes in v6:
time: 118 us
  starting transfers between devices  46.8 us (40%)
  Pallas kernels  33.8 us (29%)
  waiting for transfers between devices  23.2 us (20%)
  blocking collectives  11.5 us (10%)
  local copies, waits for them, and re-layouts  2.51 us (2%)
    pallas_call x4, Pallas kernels, kernel_call(): pl.pallas_call(body, in_specs=specs(in_spaces), out_specs=tuple(specs(out...  33.8 us
    ppermute x7, starting transfers between devices, exchange(): lax.ppermute(to_previous, axis, backward)  25.2 us
    ppermute x7, starting transfers between devices, from_offset(): return lax.ppermute(values, 'gy', moves)  14.1 us
    all_to_all x1, blocking collectives, per_device(): column = lax.all_to_all(p3, 'gx', 0, 0, tiled=True).reshape(4 * GX, LANES)  11.5 us
    ppermute x7, waiting for transfers between devices, exchange(): lax.ppermute(to_next, axis, onward)  10.9 us
    ppermute x7, starting transfers between devices, exchange(): lax.ppermute(to_next, axis, onward)  7.52 us
    ppermute x7, waiting for transfers between devices, from_offset(): return lax.ppermute(values, 'gy', moves)  7.16 us
    ppermute x7, waiting for transfers between devices, exchange(): lax.ppermute(to_previous, axis, backward)  5.19 us
  transfers between devices with their start and end apart: 21, of which 17 were waited for; matrix products, arithmetic and copies ran while one was open for 1% of the time, Pallas kernels for 0%

profile of v6, /device:TPU:1, one launch (start us, length us, event | category | flops | bytes accessed | tf_op | source)
XLA Modules:
  0.0 118.3 jit_solution(8207974361970237124)
XLA Ops:
  0.0 1.2 %slice_bitcast_fusion.4 = (f32[1,8,32,128]{3,2,1,0:T(8,128)S(1)}, f32[1,8,32,128]{3,2,1,0:T(8,128)S(1)}, f32[1,8,32,128]{3,2,1,0:T(8,128)S(1)}, f32[1,8,32,128]{3,2,1,0:T(8,128)S(1)}) fusion(f32[32,32,128]{2,1,0:T(8,128)} %e_in.1, f32[32,32,128]{2,1,0:T(8,128)} %f_in.1), kind=kLoop, calls=%fused_computation.9 | loop fusion | bytes 1048576 | tf_op jit(solution)/shard_map/stack | solution.py:753
  1.3 2.5 %collective-permute-start = (f32[2,8,32,128]{3,2,1,0:T(8,128)S(1)}, f32[2,8,32,128]{3,2,1,0:T(8,128)S(1)}, u32[]{:S(2)}, u32[]{:S(2)}) collective-permute-start(f32[2,8,32,128]{3,2,1,0:T(8,128)S(1)} %pad_maximum_fusion), channel_id=1, source_target_pairs={{0,32},{32,64},{64,96},{96,128},{128,160},{160,192},{192,224},{224... | collective-permute-start | bytes 786440 | tf_op jit(solution)/shard_map/ppermute | solution.py:740
  3.8 4.0 %collective-permute-start.1 = (f32[2,8,32,128]{3,2,1,0:T(8,128)S(1)}, f32[2,8,32,128]{3,2,1,0:T(8,128)S(1)}, u32[]{:S(2)}, u32[]{:S(2)}) collective-permute-start(f32[2,8,32,128]{3,2,1,0:T(8,128)S(1)} %pad_maximum_fusion.1), channel_id=1, source_target_pairs={{32,0},{64,32},{96,64},{128,96},{160,128},{192,160},{224,192},{0,2... | collective-permute-start | bytes 786440 | tf_op jit(solution)/shard_map/ppermute | solution.py:740
  7.9 1.1 slice_bitcast_fusion
  9.0 2.2 %collective-permute-start.2 = (f32[2,32,8,128]{3,2,1,0:T(8,128)S(1)}, f32[2,32,8,128]{3,2,1,0:T(8,128)S(1)}, u32[]{:S(2)}, u32[]{:S(2)}) collective-permute-start(f32[2,32,8,128]{3,2,1,0:T(8,128)S(1)} %pad_maximum_fusion.2), channel_id=1, source_target_pairs={{0,1},{1,2},{2,3},{3,4},{4,5},{5,6},{6,7},{7,8},{8,9},{9,10},{10,1... | collective-permute-start | bytes 786440 | tf_op jit(solution)/shard_map/ppermute | solution.py:740
  11.3 0.1 collective-permute-start.3
  11.3 2.4 %collective-permute-done.xl = f32[2,8,32,128]{3,2,1,0:T(8,128)S(1)} collective-permute-done((f32[2,8,32,128]{3,2,1,0:T(8,128)S(1)}, f32[2,8,32,128]{3,2,1,0:T(8,128)S(1)}, u32[]{:S(2)}, u32[]{:S(2)}) %collective-permute-start) | collective-permute-done | bytes 262176 | tf_op jit(solution)/shard_map/ppermute | solution.py:740
  13.8 0.0 collective-permute-done.1.xr
  13.9 1.5 %collective-permute-start.5 = (f32[2,16,8,128]{3,2,1,0:T(8,128)S(1)}, f32[2,16,8,128]{3,2,1,0:T(8,128)S(1)}, u32[]{:S(2)}, u32[]{:S(2)}) collective-permute-start(f32[2,16,8,128]{3,2,1,0:T(8,128)S(1)} %get-tuple-element.23), channel_id=1, source_target_pairs={{1,0},{2,1},{3,2},{4,3},{5,4},{6,5},{7,6},{8,7},{9,8},{10,9},{11,1... | collective-permute-start | bytes 393224 | tf_op jit(solution)/shard_map/ppermute | solution.py:740
  15.4 1.0 collective-permute-start.4
  16.4 0.0 collective-permute-done.2.yl
  16.4 1.0 collective-permute-done.3.yr
  17.4 1.6 %collective-permute-done.5.cr = f32[2,16,8,128]{3,2,1,0:T(8,128)S(1)} collective-permute-done((f32[2,16,8,128]{3,2,1,0:T(8,128)S(1)}, f32[2,16,8,128]{3,2,1,0:T(8,128)S(1)}, u32[]{:S(2)}, u32[]{:S(2)}) %collective-permute-start.5) | collective-permute-done | bytes 131104 | tf_op jit(solution)/shard_map/ppermute | solution.py:740
  19.0 1.1 collective-permute-done.4.cl
  20.1 7.4 %down0.1 = (f32[16,16,128]{2,1,0:T(8,128)S(1)}, f32[24,2,7,48,128]{4,3,2,1,0:T(8,128)S(1)}, f32[2,24,64,128]{3,2,1,0:T(8,128)S(1)}) custom-call(f32[32,32,128]{2,1,0:T(8,128)S(1)} %copy-done, f32[32,32,128]{2,1,0:T(8,128)S(1)} %copy-done.1, f32[2,8,32,128]{3,2,1,0:T(8,128)S(1)} %collective-permute-done.xl, f32[2,8,32,128]{3,2,1,0:T(8,128)S(1)} %collective-permute-done.1.xr, ...), custom_call_target="tpu_custom_call" | custom-call | tf_op jit(solution)/shard_map/down0/pallas_call | solution.py:725
  27.5 0.1 collective-permute-start.6
  27.6 2.7 %collective-permute-start.7 = (f32[13,16,128]{2,1,0:T(8,128)S(1)}, f32[13,16,128]{2,1,0:T(8,128)S(1)}, u32[]{:S(2)}, u32[]{:S(2)}) collective-permute-start(f32[13,16,128]{2,1,0:T(8,128)S(1)} %get-tuple-element.37), channel_id=1, source_target_pairs={{32,0},{64,32},{96,64},{128,96},{160,128},{192,160},{224,192},{0,2... | collective-permute-start | bytes 319496 | tf_op jit(solution)/shard_map/ppermute | solution.py:740
  30.3 2.1 %collective-permute-done.6.xl = f32[13,16,128]{2,1,0:T(8,128)S(1)} collective-permute-done((f32[13,16,128]{2,1,0:T(8,128)S(1)}, f32[13,16,128]{2,1,0:T(8,128)S(1)}, u32[]{:S(2)}, u32[]{:S(2)}) %collective-permute-start.6) | collective-permute-done | bytes 106528 | tf_op jit(solution)/shard_map/ppermute | solution.py:740
  32.4 0.0 collective-permute-done.7.xr
  32.4 8.1 %collective-permute-start.9 = (f32[42,16,128]{2,1,0:T(8,128)S(1)}, f32[42,16,128]{2,1,0:T(8,128)S(1)}, u32[]{:S(2)}, u32[]{:S(2)}) collective-permute-start(f32[42,16,128]{2,1,0:T(8,128)S(1)} %constant_dynamic-update-slice_fusion.2), channel_id=1, source_target_pairs={{1,0},{2,1},{3,2},{4,3},{5,4},{6,5},{7,6},{8,7},{9,8},{10,9},{11,1... | collective-permute-start | bytes 1032200 | tf_op jit(solution)/shard_map/ppermute | solution.py:740
  40.6 0.0 collective-permute-start.8
  40.6 1.3 %collective-permute-done.9.yr = f32[42,16,128]{2,1,0:T(8,128)S(1)} collective-permute-done((f32[42,16,128]{2,1,0:T(8,128)S(1)}, f32[42,16,128]{2,1,0:T(8,128)S(1)}, u32[]{:S(2)}, u32[]{:S(2)}) %collective-permute-start.9) | collective-permute-done | bytes 344096 | tf_op jit(solution)/shard_map/ppermute | solution.py:740
  41.8 2.9 %collective-permute-done.8.yl = f32[42,16,128]{2,1,0:T(8,128)S(1)} collective-permute-done((f32[42,16,128]{2,1,0:T(8,128)S(1)}, f32[42,16,128]{2,1,0:T(8,128)S(1)}, u32[]{:S(2)}, u32[]{:S(2)}) %collective-permute-start.8) | collective-permute-done | bytes 344096 | tf_op jit(solution)/shard_map/ppermute | solution.py:740
  44.8 7.7 %down1.1 = (f32[16,16,128]{2,1,0:T(8,128)S(1)}, f32[14,2,7,32,128]{4,3,2,1,0:T(8,128)S(1)}, f32[2,24,64,128]{3,2,1,0:T(8,128)S(1)}) custom-call(f32[16,16,128]{2,1,0:T(8,128)S(1)} %get-tuple-element.14.own, f32[13,16,128]{2,1,0:T(8,128)S(1)} %collective-permute-done.6.xl, f32[13,16,128]{2,1,0:T(8,128)S(1)} %collective-permute-done.7.xr, ...), custom_call_target="tpu_custom_call" | custom-call | tf_op jit(solution)/shard_map/down1/pallas_call | solution.py:725
  52.5 1.6 %collective-permute-start.10 = (f32[8,16,128]{2,1,0:T(8,128)S(1)}, f32[8,16,128]{2,1,0:T(8,128)S(1)}, u32[]{:S(2)}, u32[]{:S(2)}) collective-permute-start(f32[8,16,128]{2,1,0:T(8,128)S(1)} %get-tuple-element.36), channel_id=1, source_target_pairs={{0,32},{32,64},{64,96},{96,128},{128,160},{160,192},{192,224},{224... | collective-permute-start | bytes 196616 | tf_op jit(solution)/shard_map/ppermute | solution.py:740
  54.1 1.6 %collective-permute-start.11 = (f32[8,16,128]{2,1,0:T(8,128)S(1)}, f32[8,16,128]{2,1,0:T(8,128)S(1)}, u32[]{:S(2)}, u32[]{:S(2)}) collective-permute-start(f32[8,16,128]{2,1,0:T(8,128)S(1)} %get-tuple-element.35), channel_id=1, source_target_pairs={{32,0},{64,32},{96,64},{128,96},{160,128},{192,160},{224,192},{0,2... | collective-permute-start | bytes 196616 | tf_op jit(solution)/shard_map/ppermute | solution.py:740
  55.7 1.4 %collective-permute-done.10.xl = f32[8,16,128]{2,1,0:T(8,128)S(1)} collective-permute-done((f32[8,16,128]{2,1,0:T(8,128)S(1)}, f32[8,16,128]{2,1,0:T(8,128)S(1)}, u32[]{:S(2)}, u32[]{:S(2)}) %collective-permute-start.10) | collective-permute-done | bytes 65568 | tf_op jit(solution)/shard_map/ppermute | solution.py:740
  57.1 0.4 collective-permute-done.11.xr
  57.5 7.1 %collective-permute-start.13 = (f32[32,8,128]{2,1,0:T(8,128)S(1)}, f32[32,8,128]{2,1,0:T(8,128)S(1)}, u32[]{:S(2)}, u32[]{:S(2)}) collective-permute-start(f32[32,8,128]{2,1,0:T(8,128)S(1)} %get-tuple-element.33), channel_id=1, source_target_pairs={{1,0},{2,1},{3,2},{4,3},{5,4},{6,5},{7,6},{8,7},{9,8},{10,9},{11,1... | collective-permute-start | bytes 393224 | tf_op jit(solution)/shard_map/ppermute | solution.py:740
  64.6 0.0 collective-permute-start.12
  64.6 1.0 collective-permute-done.13.yr
  65.6 1.0 collective-permute-done.12.yl
  66.6 3.9 %down2.1 = (f32[8,4,128]{2,1,0:T(4,128)S(1)}, f32[16,2,7,32,128]{4,3,2,1,0:T(8,128)S(1)}, f32[2,16,48,128]{3,2,1,0:T(8,128)S(1)}) custom-call(f32[16,16,128]{2,1,0:T(8,128)S(1)} %get-tuple-element.15.own, f32[8,16,128]{2,1,0:T(8,128)S(1)} %collective-permute-done.10.xl, f32[8,16,128]{2,1,0:T(8,128)S(1)} %collective-permute-done.11.xr, ...), custom_call_target="tpu_custom_call" | custom-call | tf_op jit(solution)/shard_map/down2/pallas_call | solution.py:725
  70.5 11.5 %all_to_all.5 = f32[8,4,128]{2,1,0:T(4,128)S(1)} all-to-all(f32[8,4,128]{2,1,0:T(4,128)S(1)} %get-tuple-element.16), channel_id=1, replica_groups=mesh['gx'=8,'gy'=32] {'gx'}, dimensions={0} | all-to-all | bytes 32768 | tf_op jit(solution)/shard_map/all_to_all | solution.py:777
  82.0 0.0 collective-permute-start.16
  82.1 0.7 collective-permute-start.15
  82.8 1.9 %collective-permute-start.14 = (f32[32,128]{1,0:T(8,128)S(1)}, f32[32,128]{1,0:T(8,128)S(1)}, u32[]{:S(2)}, u32[]{:S(2)}) collective-permute-start(f32[32,128]{1,0:T(8,128)S(1)} %bitcast.28), channel_id=1, source_target_pairs={{2,0},{3,1},{4,2},{5,3},{6,4},{7,5},{0,6},{1,7},{10,8},{11,9},{12,... | collective-permute-start | bytes 49160 | tf_op jit(solution)/shard_map/ppermute | solution.py:748
  84.7 1.1 collective-permute-done.16
  85.9 0.3 collective-permute-done.15
  86.1 0.8 collective-permute-done.14
  86.9 1.3 %collective-permute-start.18 = (f32[4,32,128]{2,1,0:T(8,128)S(1)}, f32[4,32,128]{2,1,0:T(8,128)S(1)}, u32[]{:S(2)}, u32[]{:S(2)}) collective-permute-start(f32[4,32,128]{2,1,0:T(8,128)S(1)} %get-tuple-element.40), channel_id=1, source_target_pairs={{16,0},{17,1},{18,2},{19,3},{20,4},{21,5},{22,6},{23,7},{24,8},{25... | collective-permute-start | bytes 196616 | tf_op jit(solution)/shard_map/ppermute | solution.py:748
  88.2 4.0 %collective-permute-start.17 = (f32[4,32,128]{2,1,0:T(8,128)S(1)}, f32[4,32,128]{2,1,0:T(8,128)S(1)}, u32[]{:S(2)}, u32[]{:S(2)}) collective-permute-start(f32[4,32,128]{2,1,0:T(8,128)S(1)} %get-tuple-element.40), channel_id=1, source_target_pairs={{8,0},{9,1},{10,2},{11,3},{12,4},{13,5},{14,6},{15,7},{16,8},{17,9... | collective-permute-start | bytes 196616 | tf_op jit(solution)/shard_map/ppermute | solution.py:748
  92.1 0.5 collective-permute-start.19
  92.6 2.9 %collective-permute-done.17 = f32[4,32,128]{2,1,0:T(8,128)S(1)} collective-permute-done((f32[4,32,128]{2,1,0:T(8,128)S(1)}, f32[4,32,128]{2,1,0:T(8,128)S(1)}, u32[]{:S(2)}, u32[]{:S(2)}) %collective-permute-start.17) | collective-permute-done | bytes 65568 | tf_op jit(solution)/shard_map/ppermute | solution.py:748
  95.5 0.9 collective-permute-done.19
  96.5 5.7 %collective-permute-start.20 = (f32[4,4,32,128]{3,2,1,0:T(8,128)S(1)}, f32[4,4,32,128]{3,2,1,0:T(8,128)S(1)}, u32[]{:S(2)}, u32[]{:S(2)}) collective-permute-start(f32[4,4,32,128]{3,2,1,0:T(8,128)S(1)} %pad_maximum_fusion.4.near), channel_id=1, source_target_pairs={{1,0},{0,1},{3,2},{2,3},{5,4},{4,5},{7,6},{6,7},{9,8},{8,9},{11,10... | collective-permute-start | bytes 786440 | tf_op jit(solution)/shard_map/ppermute | solution.py:748
  102.2 1.2 collective-permute-done.20.far
  103.4 14.9 %climb.1 = f32[32,32,128]{2,1,0:T(8,128)} custom-call(f32[4,4,32,128]{3,2,1,0:T(8,128)S(1)} %pad_maximum_fusion.4.near, f32[4,4,32,128]{3,2,1,0:T(8,128)S(1)} %collective-permute-done.20.far, f32[24,2,7,48,128]{4,3,2,1,0:T(8,128)S(1)} %get-tuple-element.17.s0, f32[2,24,64,128]{3,2,1,0:T(8,128)S(1)} %get-tuple-element.18.i0, ...), custom_call_target="tpu_custom_call" | custom-call | tf_op jit(solution)/shard_map/climb/pallas_call | solution.py:725
  (23 shorter events, 0.3 us)
Async XLA Ops:
  0.0 20.1 %copy-start.1 = (f32[32,32,128]{2,1,0:T(8,128)S(1)}, f32[32,32,128]{2,1,0:T(8,128)}, u32[]{:S(2)}) copy-start(f32[32,32,128]{2,1,0:T(8,128)} %e_in.1) | copy-start | bytes 1572868
  0.0 20.1 %copy-start = (f32[32,32,128]{2,1,0:T(8,128)S(1)}, f32[32,32,128]{2,1,0:T(8,128)}, u32[]{:S(2)}) copy-start(f32[32,32,128]{2,1,0:T(8,128)} %f_in.1) | copy-start | bytes 1572868
  1.3 12.5 %collective-permute-start = (f32[2,8,32,128]{3,2,1,0:T(8,128)S(1)}, f32[2,8,32,128]{3,2,1,0:T(8,128)S(1)}, u32[]{:S(2)}, u32[]{:S(2)}) collective-permute-start(f32[2,8,32,128]{3,2,1,0:T(8,128)S(1)} %pad_maximum_fusion), channel_id=1, source_target_pairs={{0,32},{32,64},{64,96},{96,128},{128,160},{160,192},{192,224},{224... | collective-permute-start | bytes 786440 | tf_op jit(solution)/shard_map/ppermute | solution.py:740
  3.8 10.0 %collective-permute-start.1 = (f32[2,8,32,128]{3,2,1,0:T(8,128)S(1)}, f32[2,8,32,128]{3,2,1,0:T(8,128)S(1)}, u32[]{:S(2)}, u32[]{:S(2)}) collective-permute-start(f32[2,8,32,128]{3,2,1,0:T(8,128)S(1)} %pad_maximum_fusion.1), channel_id=1, source_target_pairs={{32,0},{64,32},{96,64},{128,96},{160,128},{192,160},{224,192},{0,2... | collective-permute-start | bytes 786440 | tf_op jit(solution)/shard_map/ppermute | solution.py:740
  9.0 7.4 %collective-permute-start.2 = (f32[2,32,8,128]{3,2,1,0:T(8,128)S(1)}, f32[2,32,8,128]{3,2,1,0:T(8,128)S(1)}, u32[]{:S(2)}, u32[]{:S(2)}) collective-permute-start(f32[2,32,8,128]{3,2,1,0:T(8,128)S(1)} %pad_maximum_fusion.2), channel_id=1, source_target_pairs={{0,1},{1,2},{2,3},{3,4},{4,5},{5,6},{6,7},{7,8},{8,9},{9,10},{10,1... | collective-permute-start | bytes 786440 | tf_op jit(solution)/shard_map/ppermute | solution.py:740
  11.3 6.2 %collective-permute-start.3 = (f32[2,32,8,128]{3,2,1,0:T(8,128)S(1)}, f32[2,32,8,128]{3,2,1,0:T(8,128)S(1)}, u32[]{:S(2)}, u32[]{:S(2)}) collective-permute-start(f32[2,32,8,128]{3,2,1,0:T(8,128)S(1)} %pad_maximum_fusion.3), channel_id=1, source_target_pairs={{1,0},{2,1},{3,2},{4,3},{5,4},{6,5},{7,6},{8,7},{9,8},{10,9},{11,1... | collective-permute-start | bytes 786440 | tf_op jit(solution)/shard_map/ppermute | solution.py:740
  13.9 5.1 %collective-permute-start.5 = (f32[2,16,8,128]{3,2,1,0:T(8,128)S(1)}, f32[2,16,8,128]{3,2,1,0:T(8,128)S(1)}, u32[]{:S(2)}, u32[]{:S(2)}) collective-permute-start(f32[2,16,8,128]{3,2,1,0:T(8,128)S(1)} %get-tuple-element.23), channel_id=1, source_target_pairs={{1,0},{2,1},{3,2},{4,3},{5,4},{6,5},{7,6},{8,7},{9,8},{10,9},{11,1... | collective-permute-start | bytes 393224 | tf_op jit(solution)/shard_map/ppermute | solution.py:740
  15.4 4.7 %collective-permute-start.4 = (f32[2,16,8,128]{3,2,1,0:T(8,128)S(1)}, f32[2,16,8,128]{3,2,1,0:T(8,128)S(1)}, u32[]{:S(2)}, u32[]{:S(2)}) collective-permute-start(f32[2,16,8,128]{3,2,1,0:T(8,128)S(1)} %get-tuple-element.24), channel_id=1, source_target_pairs={{0,1},{1,2},{2,3},{3,4},{4,5},{5,6},{6,7},{7,8},{8,9},{9,10},{10,1... | collective-permute-start | bytes 393224 | tf_op jit(solution)/shard_map/ppermute | solution.py:740
  27.5 4.8 %collective-permute-start.6 = (f32[13,16,128]{2,1,0:T(8,128)S(1)}, f32[13,16,128]{2,1,0:T(8,128)S(1)}, u32[]{:S(2)}, u32[]{:S(2)}) collective-permute-start(f32[13,16,128]{2,1,0:T(8,128)S(1)} %get-tuple-element.38), channel_id=1, source_target_pairs={{0,32},{32,64},{64,96},{96,128},{128,160},{160,192},{192,224},{224... | collective-permute-start | bytes 319496 | tf_op jit(solution)/shard_map/ppermute | solution.py:740
  27.6 4.8 %collective-permute-start.7 = (f32[13,16,128]{2,1,0:T(8,128)S(1)}, f32[13,16,128]{2,1,0:T(8,128)S(1)}, u32[]{:S(2)}, u32[]{:S(2)}) collective-permute-start(f32[13,16,128]{2,1,0:T(8,128)S(1)} %get-tuple-element.37), channel_id=1, source_target_pairs={{32,0},{64,32},{96,64},{128,96},{160,128},{192,160},{224,192},{0,2... | collective-permute-start | bytes 319496 | tf_op jit(solution)/shard_map/ppermute | solution.py:740
  32.4 9.4 %collective-permute-start.9 = (f32[42,16,128]{2,1,0:T(8,128)S(1)}, f32[42,16,128]{2,1,0:T(8,128)S(1)}, u32[]{:S(2)}, u32[]{:S(2)}) collective-permute-start(f32[42,16,128]{2,1,0:T(8,128)S(1)} %constant_dynamic-update-slice_fusion.2), channel_id=1, source_target_pairs={{1,0},{2,1},{3,2},{4,3},{5,4},{6,5},{7,6},{8,7},{9,8},{10,9},{11,1... | collective-permute-start | bytes 1032200 | tf_op jit(solution)/shard_map/ppermute | solution.py:740
  40.6 4.2 %collective-permute-start.8 = (f32[42,16,128]{2,1,0:T(8,128)S(1)}, f32[42,16,128]{2,1,0:T(8,128)S(1)}, u32[]{:S(2)}, u32[]{:S(2)}) collective-permute-start(f32[42,16,128]{2,1,0:T(8,128)S(1)} %constant_dynamic-update-slice_fusion.2), channel_id=1, source_target_pairs={{0,1},{1,2},{2,3},{3,4},{4,5},{5,6},{6,7},{7,8},{8,9},{9,10},{10,1... | collective-permute-start | bytes 1032200 | tf_op jit(solution)/shard_map/ppermute | solution.py:740
  52.5 4.6 %collective-permute-start.10 = (f32[8,16,128]{2,1,0:T(8,128)S(1)}, f32[8,16,128]{2,1,0:T(8,128)S(1)}, u32[]{:S(2)}, u32[]{:S(2)}) collective-permute-start(f32[8,16,128]{2,1,0:T(8,128)S(1)} %get-tuple-element.36), channel_id=1, source_target_pairs={{0,32},{32,64},{64,96},{96,128},{128,160},{160,192},{192,224},{224... | collective-permute-start | bytes 196616 | tf_op jit(solution)/shard_map/ppermute | solution.py:740
  54.1 3.4 %collective-permute-start.11 = (f32[8,16,128]{2,1,0:T(8,128)S(1)}, f32[8,16,128]{2,1,0:T(8,128)S(1)}, u32[]{:S(2)}, u32[]{:S(2)}) collective-permute-start(f32[8,16,128]{2,1,0:T(8,128)S(1)} %get-tuple-element.35), channel_id=1, source_target_pairs={{32,0},{64,32},{96,64},{128,96},{160,128},{192,160},{224,192},{0,2... | collective-permute-start | bytes 196616 | tf_op jit(solution)/shard_map/ppermute | solution.py:740
  57.5 8.1 %collective-permute-start.13 = (f32[32,8,128]{2,1,0:T(8,128)S(1)}, f32[32,8,128]{2,1,0:T(8,128)S(1)}, u32[]{:S(2)}, u32[]{:S(2)}) collective-permute-start(f32[32,8,128]{2,1,0:T(8,128)S(1)} %get-tuple-element.33), channel_id=1, source_target_pairs={{1,0},{2,1},{3,2},{4,3},{5,4},{6,5},{7,6},{8,7},{9,8},{10,9},{11,1... | collective-permute-start | bytes 393224 | tf_op jit(solution)/shard_map/ppermute | solution.py:740
  64.6 2.0 %collective-permute-start.12 = (f32[32,8,128]{2,1,0:T(8,128)S(1)}, f32[32,8,128]{2,1,0:T(8,128)S(1)}, u32[]{:S(2)}, u32[]{:S(2)}) collective-permute-start(f32[32,8,128]{2,1,0:T(8,128)S(1)} %get-tuple-element.34), channel_id=1, source_target_pairs={{0,1},{1,2},{2,3},{3,4},{4,5},{5,6},{6,7},{7,8},{8,9},{9,10},{10,1... | collective-permute-start | bytes 393224 | tf_op jit(solution)/shard_map/ppermute | solution.py:740
  82.0 3.8 %collective-permute-start.16 = (f32[32,128]{1,0:T(8,128)S(1)}, f32[32,128]{1,0:T(8,128)S(1)}, u32[]{:S(2)}, u32[]{:S(2)}) collective-permute-start(f32[32,128]{1,0:T(8,128)S(1)} %bitcast.26), channel_id=1, source_target_pairs={{6,0},{7,1},{0,2},{1,3},{2,4},{3,5},{4,6},{5,7},{14,8},{15,9},{8,1... | collective-permute-start | bytes 49160 | tf_op jit(solution)/shard_map/ppermute | solution.py:748
  82.1 4.1 %collective-permute-start.15 = (f32[32,128]{1,0:T(8,128)S(1)}, f32[32,128]{1,0:T(8,128)S(1)}, u32[]{:S(2)}, u32[]{:S(2)}) collective-permute-start(f32[32,128]{1,0:T(8,128)S(1)} %bitcast.27), channel_id=1, source_target_pairs={{4,0},{5,1},{6,2},{7,3},{0,4},{1,5},{2,6},{3,7},{12,8},{13,9},{14,... | collective-permute-start | bytes 49160 | tf_op jit(solution)/shard_map/ppermute | solution.py:748
  82.8 4.1 %collective-permute-start.14 = (f32[32,128]{1,0:T(8,128)S(1)}, f32[32,128]{1,0:T(8,128)S(1)}, u32[]{:S(2)}, u32[]{:S(2)}) collective-permute-start(f32[32,128]{1,0:T(8,128)S(1)} %bitcast.28), channel_id=1, source_target_pairs={{2,0},{3,1},{4,2},{5,3},{6,4},{7,5},{0,6},{1,7},{10,8},{11,9},{12,... | collective-permute-start | bytes 49160 | tf_op jit(solution)/shard_map/ppermute | solution.py:748
  86.9 5.7 %collective-permute-start.18 = (f32[4,32,128]{2,1,0:T(8,128)S(1)}, f32[4,32,128]{2,1,0:T(8,128)S(1)}, u32[]{:S(2)}, u32[]{:S(2)}) collective-permute-start(f32[4,32,128]{2,1,0:T(8,128)S(1)} %get-tuple-element.40), channel_id=1, source_target_pairs={{16,0},{17,1},{18,2},{19,3},{20,4},{21,5},{22,6},{23,7},{24,8},{25... | collective-permute-start | bytes 196616 | tf_op jit(solution)/shard_map/ppermute | solution.py:748
  88.2 7.4 %collective-permute-start.17 = (f32[4,32,128]{2,1,0:T(8,128)S(1)}, f32[4,32,128]{2,1,0:T(8,128)S(1)}, u32[]{:S(2)}, u32[]{:S(2)}) collective-permute-start(f32[4,32,128]{2,1,0:T(8,128)S(1)} %get-tuple-element.40), channel_id=1, source_target_pairs={{8,0},{9,1},{10,2},{11,3},{12,4},{13,5},{14,6},{15,7},{16,8},{17,9... | collective-permute-start | bytes 196616 | tf_op jit(solution)/shard_map/ppermute | solution.py:748
  92.1 4.3 %collective-permute-start.19 = (f32[4,32,128]{2,1,0:T(8,128)S(1)}, f32[4,32,128]{2,1,0:T(8,128)S(1)}, u32[]{:S(2)}, u32[]{:S(2)}) collective-permute-start(f32[4,32,128]{2,1,0:T(8,128)S(1)} %get-tuple-element.40), channel_id=1, source_target_pairs={{24,0},{25,1},{26,2},{27,3},{28,4},{29,5},{30,6},{31,7},{0,8},{1,9... | collective-permute-start | bytes 196616 | tf_op jit(solution)/shard_map/ppermute | solution.py:748
  96.5 6.9 %collective-permute-start.20 = (f32[4,4,32,128]{3,2,1,0:T(8,128)S(1)}, f32[4,4,32,128]{3,2,1,0:T(8,128)S(1)}, u32[]{:S(2)}, u32[]{:S(2)}) collective-permute-start(f32[4,4,32,128]{3,2,1,0:T(8,128)S(1)} %pad_maximum_fusion.4.near), channel_id=1, source_target_pairs={{1,0},{0,1},{3,2},{2,3},{5,4},{4,5},{7,6},{6,7},{9,8},{8,9},{11,10... | collective-permute-start | bytes 786440 | tf_op jit(solution)/shard_map/ppermute | solution.py:748
